TPU v7x, 32 devices: a whole 2x2x4 slice. The times are simulated.
32 devices in a mesh: dp: 4 (over y, x), tm: 8 (over z, core).
Axes of the slice: x: 2, y: 2, z: 4, core: 2. Of those that a mesh axis runs over, the one named last changes fastest.
Arguments:
- frames: bfloat16 [4, 8, 4, 128, 1536], P('dp', 'tm'), may hold values from -6 to 6
- route: int32 [4, 8, 4], P('dp', 'tm'), may hold values from 0 to 31, as said below
- utterance: int32 [4, 8, 4], P('dp', 'tm'), may hold values from 0 to 2, as said below
- gain: float32 [1536], replicated, may hold values from 0.5 to 1.5
- w_in: bfloat16 [1536, 3072], P('dp'), may hold values from -0.15625 to 0.15625
- kernel: float32 [31, 1536], replicated, may hold values from -3 to 3
- cotangent: bfloat16 [4, 8, 4, 128, 1536], P('dp', 'tm'), may hold values from -4 to 4
Outputs:
- grad_frames: bfloat16 [4, 8, 4, 128, 1536], P('dp', 'tm')
- grad_w_in: float32 [1536, 3072], P('dp', 'tm')
- grad_kernel: float32 [31, 1536], replicated
- grad_gain: float32 [1536], replicated
Inputs may be any that keep to these rules, and one draw needn't show every extreme that they name: route[g, s, j] is owner * 4 + slot for panel j of loader s of data group g; over one data group every stream position appears exactly once, and the 4 panels of one loader go to 4 different owners. Utterance ids never fall along a data group's stream (owner after owner, slot after slot), start at 0 in each group, each utterance is a run of whole panels, and every group holds exactly 3 utterances.
All inputs are finite; a program needn't handle non-finite values.
Results may differ from a plain program's by a relative error of at most 0.015.
Values may be sent and summed in bfloat16 or wider, within the bound.
No kernel may reach another device: no remote copies, remote signals or barrier semaphores. Data moves between devices by JAX's collectives and lax.ppermute only.
A program may use at most 128 MiB of HBM per device.

v0:
```python
import jax
import jax.numpy as jnp
from jax import lax
from jax.sharding import PartitionSpec as P


def with_halo(block, sides, width):
    for axis, dim in sides:
        count = lax.axis_size(axis)
        forward = [(i, i + 1) for i in range(count - 1)]
        backward = [(target, source) for source, target in forward]
        low = lax.ppermute(
            lax.slice_in_dim(block, block.shape[dim] - width, None, axis=dim), axis, forward
        )
        high = lax.ppermute(lax.slice_in_dim(block, 0, width, axis=dim), axis, backward)
        block = jnp.concatenate([low, block, high], axis=dim)
    return block


def outer_sum(left, right):
    return lax.dot_general(
        left, right, (((0,), (0,)), ((), ())), preferred_element_type=jnp.float32
    )


def times_transposed(left, right):
    return lax.dot_general(
        left, right, (((1,), (1,)), ((), ())), preferred_element_type=jnp.float32
    )


def masked_taps(padded, masks, kernel, rows, flip):
    taps = kernel.shape[0]
    total = jnp.zeros((rows, kernel.shape[1]), jnp.float32)
    for tap in range(taps):
        source = taps - 1 - tap if flip else tap
        piece = jnp.where(masks[source], padded[source : source + rows].astype(jnp.float32), 0.0)
        total = total + kernel[tap] * piece
    return total


def local(frames, route, utterance, gain, w_in, kernel, cotangent):
    panels = frames.shape[2]
    panel_len = frames.shape[3]
    width = frames.shape[4]
    owners = lax.axis_size("tm")
    rows = panels * panel_len
    taps = kernel.shape[0]
    reach = taps // 2
    loaded = frames[0, 0]
    target = route[0, 0]
    labels = utterance[0, 0]
    owner_of = target // panels
    slot_of = target % panels
    pick = owner_of[None, :] == jnp.arange(owners, dtype=jnp.int32)[:, None]
    pick_cast = pick.astype(jnp.bfloat16)
    outgoing = jnp.einsum(
        "oj,jfd->ofd", pick_cast, loaded, preferred_element_type=jnp.float32
    ).astype(jnp.bfloat16)
    slot_tags = jnp.sum(jnp.where(pick, slot_of[None, :] + 1, 0), axis=1)
    label_tags = jnp.sum(jnp.where(pick, labels[None, :] + 1, 0), axis=1)
    tags = jnp.stack([slot_tags, label_tags], axis=1)
    arrived, arrived_tags = (
        lax.all_to_all(outgoing, "tm", split_axis=0, concat_axis=0, tiled=True),
        lax.all_to_all(tags, "tm", split_axis=0, concat_axis=0, tiled=True),
    )
    place = arrived_tags[:, 0][None, :] == jnp.arange(panels, dtype=jnp.int32)[:, None] + 1
    place_cast = place.astype(jnp.bfloat16)
    stream = jnp.einsum(
        "js,sfd->jfd", place_cast, arrived, preferred_element_type=jnp.float32
    ).astype(jnp.bfloat16)
    stream = stream.reshape(rows, width)
    panel_ids = jnp.sum(jnp.where(place, arrived_tags[:, 1][None, :], 0), axis=1).astype(jnp.int32)
    row_ids = jnp.repeat(panel_ids, panel_len)
    padded_ids = with_halo(row_ids, (("tm", 0),), reach)
    masks = [(padded_ids[tap : tap + rows] == row_ids)[:, None] for tap in range(taps)]
    full_in = lax.all_gather(w_in, "dp", axis=0, tiled=True)
    values = stream.astype(jnp.float32)
    center = jnp.mean(values, axis=1, keepdims=True)
    variance = jnp.mean((values - center) ** 2, axis=1, keepdims=True)
    inv_scale = lax.rsqrt(variance + 1e-05)
    unit = (values - center) * inv_scale
    normed = (unit * gain).astype(jnp.bfloat16)
    pre = jnp.dot(normed, full_in, preferred_element_type=jnp.float32)
    linear = pre[:, :width]
    gate_sig = jax.nn.sigmoid(pre[:, width:])
    glu = (linear * gate_sig).astype(jnp.bfloat16)
    glu_padded = with_halo(glu, (("tm", 0),), reach)
    depth = masked_taps(glu_padded, masks, kernel, rows, False)
    depth_sig = jax.nn.sigmoid(depth)
    upstream = cotangent[0, 0].reshape(rows, width)
    grad_depth = (
        upstream.astype(jnp.float32) * depth_sig * (1.0 + depth * (1.0 - depth_sig))
    ).astype(jnp.bfloat16)
    grad_padded = with_halo(grad_depth, (("tm", 0),), reach)
    grad_depth_f = grad_depth.astype(jnp.float32)
    kernel_term = jnp.stack(
        [
            jnp.sum(
                grad_depth_f
                * jnp.where(masks[tap], glu_padded[tap : tap + rows].astype(jnp.float32), 0.0),
                axis=0,
            )
            for tap in range(taps)
        ]
    )
    grad_glu = masked_taps(grad_padded, masks, kernel, rows, True)
    grad_pre = jnp.concatenate(
        [grad_glu * gate_sig, grad_glu * linear * gate_sig * (1.0 - gate_sig)], axis=1
    ).astype(jnp.bfloat16)
    in_term = outer_sum(normed, grad_pre)
    grad_normed = times_transposed(grad_pre, full_in)
    gain_term = jnp.sum(grad_normed * unit, axis=0)
    scaled = grad_normed * gain
    grad_x = upstream.astype(jnp.float32) + inv_scale * (
        scaled
        - jnp.mean(scaled, axis=1, keepdims=True)
        - unit * jnp.mean(scaled * unit, axis=1, keepdims=True)
    )
    grad_x = grad_x.astype(jnp.bfloat16).reshape(panels, panel_len, width)
    backward = jnp.einsum(
        "js,jfd->sfd", place_cast, grad_x, preferred_element_type=jnp.float32
    ).astype(jnp.bfloat16)
    returned = lax.all_to_all(backward, "tm", split_axis=0, concat_axis=0, tiled=True)
    grad_loaded = jnp.einsum(
        "oj,ofd->jfd", pick_cast, returned, preferred_element_type=jnp.float32
    ).astype(jnp.bfloat16)
    kernel_sum, gain_sum = lax.psum((kernel_term, gain_term), ("dp", "tm"))
    time_in = lax.psum_scatter(in_term.astype(jnp.bfloat16), "tm", scatter_dimension=1, tiled=True)
    shard_in = lax.psum_scatter(time_in, "dp", scatter_dimension=0, tiled=True).astype(jnp.float32)
    return (grad_loaded[None, None], shard_in, kernel_sum, gain_sum)


def solution(mesh):
    in_specs = (
        P("dp", "tm", None, None, None),
        P("dp", "tm", None),
        P("dp", "tm", None),
        P(),
        P("dp", None),
        P(),
        P("dp", "tm", None, None, None),
    )
    out_specs = (P("dp", "tm", None, None, None), P("dp", "tm"), P(), P())
    return jax.shard_map(local, mesh=mesh, in_specs=in_specs, out_specs=out_specs, check_vma=False)
```

profile of v0, /device:TPU:8, one launch (start us, length us, event | category | flops | bytes accessed | tf_op | source)
XLA Modules:
  0.0 584.4 jit_solution(2706242645408856636)
XLA Ops:
  10.0 5.3 all-to-all-start
  19.8 5.5 all-to-all-start.1
  31.8 45.4 %collective-permute-done.1 = s32[15]{0:T(128)S(1)} collective-permute-done((s32[15]{0:T(128)S(1)}, s32[15]{0:T(128)S(1)}, u32[]{:S(2)}, u32[]{:S(2)}) %collective-permute-start.1) | collective-permute-done | bytes 92 | tf_op jit(solution)/shard_map/ppermute | solution.py:12
  78.0 15.3 %all-to-all-done.1 = bf16[8,128,1536]{2,1,0:T(8,128)(2,1)} async-done(((bf16[8,128,1536]{2,1,0:T(8,128)(2,1)}), bf16[8,128,1536]{2,1,0:T(8,128)(2,1)}, u32[]{:S(2)}, u32[]{:S(2)}) %all-to-all-start.1) | async-done | bytes 3145760 | tf_op jit(solution)/shard_map/all_to_all | solution.py:64
  93.3 5.8 fusion.159
  99.2 4.8 copy.35
  108.6 7.6 %fusion.160 = f32[512,3072]{1,0:T(8,128)S(1)} fusion(bf16[512,1536]{1,0:T(8,128)(2,1)S(1)} %multiply_convert_fusion.3, bf16[1536,3072]{1,0:T(8,128)(2,1)} %all-gather.2.cloned.1.call-done), kind=kOutput, calls=%fused_computation.387 | convolution fusion | flops 4831838208 | bytes 17301504 | tf_op jit(solution)/shard_map/dot_general | solution.py:84
  118.9 5.0 collective-permute-start.2
  127.7 41.3 %fusion.64 = (f32[1536]{0:T(1024)}, f32[1536]{0:T(1024)}, f32[1536]{0:T(1024)}, f32[1536]{0:T(1024)}, f32[1536]{0:T(1024)}, /*index=5*/f32[1536]{0:T(1024)}, bf16[512,1536]{1,0:T(8,128)(2,1)S(1)}) fusion(pred[512]{0:T(512)(128)(4,1)S(1)} %get-tuple-element.110, bf16[15,1536]{1,0:T(8,128)(2,1)S(1)} %collective-permute-done.3, ...), kind=kLoop, calls=%fused_computation.158 | loop fusion | flops 208395264 | bytes 5053440 | tf_op jit(solution)/shard_map/reduce_sum | solution.py:99
  169.0 3.7 collective-permute-start.4
  178.2 40.9 %multiply_convert_fusion.1 = (bf16[512,1536]{1,0:T(8,128)(2,1)}, f32[512,1536]{1,0:T(8,128)}) fusion(f32[512,3072]{1,0:T(8,128)} %copy-done.2, bf16[512,1536]{1,0:T(8,128)(2,1)S(1)} %get-tuple-element.87, bf16[15,1536]{1,0:T(8,128)(2,1)} %collective-permute-done.5, pred[512]{0:T(512)(128)(4,1)} %copy-done.37, f32[1536]{0:T(1024)S(1)} %get-tuple-element.83, ...), kind=kLoop, calls=%fused_computation.174 | loop fusion | flops 170655744 | bytes 9735168 | tf_op jit(solution)/shard_map/convert.2
  219.2 5.1 multiply_convert_fusion
  225.4 7.9 %convolution_convert_fusion = bf16[1536,3072]{1,0:T(8,128)(2,1)} fusion(bf16[512,1536]{1,0:T(8,128)(2,1)S(1)} %copy-done.8, bf16[512,1536]{1,0:T(8,128)(2,1)S(1)} %multiply_convert_fusion, bf16[512,1536]{1,0:T(8,128)(2,1)S(1)} %copy-done.9), kind=kOutput, calls=%fused_computation.32 | convolution fusion | flops 4842848256 | bytes 14155776 | tf_op jit(solution)/shard_map/dot_general | solution.py:21
  233.3 12.7 %copy.40 = bf16[1536,3072]{0,1:T(8,128)(2,1)} copy(bf16[1536,3072]{1,0:T(8,128)(2,1)} %convolution_convert_fusion) | data formatting | bytes 18874368
  246.7 11.1 %multiply_reduce_fusion = (f32[1536]{0:T(1024)S(1)}, f32[512]{0:T(512)S(1)}, f32[512]{0:T(512)S(1)}, f32[512,1536]{1,0:T(8,128)S(1)}) fusion(f32[4,128,1536]{2,1,0:T(8,128)} %copy.35, f32[512]{0:T(512)S(1)} %bitcast.102, f32[512]{0:T(512)S(1)} %bitcast.105, f32[1536]{0:T(1024)S(1)} %copy-done.12, bf16[1536,3072]{1,0:T(8,128)(2,1)} %all-gather.2.cloned.1.call-done, ...), kind=kOutput, calls=%fused_computation.171 | convolution fusion | flops 4844418560 | bytes 18894848 | tf_op jit(solution)/shard_map/dot_general | solution.py:27
  263.4 4.9 all-to-all-start.2
  268.4 5.4 fusion.63
  274.0 10.4 %fusion.65 = (f32[1536]{0:T(1024)S(1)}, f32[1536]{0:T(1024)S(1)}, f32[1536]{0:T(1024)S(1)}, f32[1536]{0:T(1024)S(1)}, f32[1536]{0:T(1024)S(1)}, /*index=5*/f32[1536]{0:T(1024)S(1)}) fusion(bf16[512,1536]{1,0:T(8,128)(2,1)S(1)} %get-tuple-element.87, bf16[15,1536]{1,0:T(8,128)(2,1)S(1)} %collective-permute-done.3, ...), kind=kLoop, calls=%fused_computation.159 | loop fusion | flops 33807360 | bytes 3231744 | tf_op jit(solution)/shard_map/reduce_sum | solution.py:99
  284.4 123.1 %reduce-scatter.7.cloned.1.call-done = bf16[384,1536]{1,0:T(8,128)(2,1)} async-done(((bf16[3072,1536]{1,0:T(8,128)(2,1)}), bf16[384,1536]{1,0:T(8,128)(2,1)}) %reduce-scatter.7.cloned.1.call-update) | async-done | bytes 1179664
  413.4 5.4 fusion.49
  418.9 6.2 %fusion.48 = (f32[1536]{0:T(1024)S(1)}, f32[1536]{0:T(1024)S(1)}, f32[1536]{0:T(1024)S(1)}, f32[1536]{0:T(1024)S(1)}, f32[1536]{0:T(1024)S(1)}, /*index=5*/f32[1536]{0:T(1024)S(1)}) fusion(bf16[512,1536]{1,0:T(8,128)(2,1)S(1)} %get-tuple-element.87, pred[512]{0:T(512)(128)(4,1)S(1)} %copy-done.40, bf16[512,1536]{1,0:T(8,128)(2,1)S(1)} %multiply_convert_fusion.2, ...), kind=kLoop, calls=%fused_computation.142 | loop fusion | flops 33807360 | bytes 3231744 | tf_op jit(solution)/shard_map/reduce_sum | solution.py:99
  428.1 42.7 %psum.15 = f32[1536]{0:T(1024)} all-reduce(f32[1536]{0:T(1024)S(1)} %get-tuple-element.20), channel_id=1, replica_groups=mesh['dp'=4,'tm'=8] {'dp','tm'}, use_global_device_ids=true, to_apply=%region_42.43 | all-reduce | flops 1536 | bytes 12288 | tf_op jit(solution)/shard_map/psum | solution.py:128
  470.8 4.1 fusion.83
  478.2 97.7 %all-reduce.2.cloned.1.call-done = f32[31,1536]{1,0:T(8,128)} async-done(((f32[31,1536]{1,0:T(8,128)}), f32[31,1536]{1,0:T(8,128)}) %all-reduce.2.cloned.1.call-update) | async-done | bytes 190480 | tf_op jit(solution)/shard_map/psum | solution.py:128
  (255 shorter events, 51.4 us)
Async XLA Ops:
  7.2 100.3 %all-gather.2.cloned.1.call-start = ((), (), s32[]{:S(2)}) async-start(), calls=%async_computation.5 | async-start | bytes 11796480 | tf_op jit(solution)/shard_map/all_gather | solution.py:77
  10.0 9.7 %all-to-all-start = ((s32[8,1,2]{2,1,0:T(1,128)}), s32[8,1,2]{2,1,0:T(1,128)S(1)}, u32[]{:S(2)}, u32[]{:S(2)}) async-start(s32[8,1,2]{2,1,0:T(1,128)} %copy.27), calls=%async_computation | async-start | bytes 8192 | tf_op jit(solution)/shard_map/all_to_all | solution.py:65
  19.8 73.6 %all-to-all-start.1 = ((bf16[8,128,1536]{2,1,0:T(8,128)(2,1)}), bf16[8,128,1536]{2,1,0:T(8,128)(2,1)}, u32[]{:S(2)}, u32[]{:S(2)}) async-start(bf16[8,128,1536]{2,1,0:T(8,128)(2,1)} %copy.30), calls=%async_computation.1 | async-start | bytes 6291456 | tf_op jit(solution)/shard_map/all_to_all | solution.py:64
  25.3 382.2 %reduce-scatter.7.cloned.1.call-start = ((), (), s32[]{:S(2)}) async-start(), calls=%async_computation.8 | async-start | bytes 10616832
  25.3 73.8 %copy-start.75 = (s32[4]{0:T(128)}, s32[4]{0:T(128)S(1)}, u32[]{:S(2)}) copy-start(s32[4]{0:T(128)S(1)} %iota_add_fusion) | copy-start | bytes 52
  25.9 73.2 %copy-start.23 = (s32[8]{0:T(128)}, s32[8]{0:T(128)S(1)}, u32[]{:S(2)}) copy-start(s32[8]{0:T(128)S(1)} %get-tuple-element.129) | copy-start | bytes 100
  26.2 51.0 %collective-permute-start.1 = (s32[15]{0:T(128)S(1)}, s32[15]{0:T(128)S(1)}, u32[]{:S(2)}, u32[]{:S(2)}) collective-permute-start(s32[15]{0:T(128)S(1)} %get-tuple-element.126), channel_id=1, source_target_pairs={{0,1},{1,2},{2,3},{3,4},{4,5},{5,6},{6,7},{8,9},{9,10},{10,11},{11... | collective-permute-start | bytes 188 | tf_op jit(solution)/shard_map/ppermute | solution.py:12
  28.3 49.0 %collective-permute-start = (s32[15]{0:T(128)S(1)}, s32[15]{0:T(128)S(1)}, u32[]{:S(2)}, u32[]{:S(2)}) collective-permute-start(s32[15]{0:T(128)S(1)} %get-tuple-element.127), channel_id=1, source_target_pairs={{1,0},{2,1},{3,2},{4,3},{5,4},{6,5},{7,6},{9,8},{10,9},{11,10},{12... | collective-permute-start | bytes 188 | tf_op jit(solution)/shard_map/ppermute | solution.py:15
  78.0 49.5 %copy-start.25 = (pred[512]{0:T(512)(128)(4,1)}, pred[512]{0:T(512)(128)(4,1)S(1)}, u32[]{:S(2)}) copy-start(pred[512]{0:T(512)(128)(4,1)S(1)} %get-tuple-element.106) | copy-start | bytes 1540
  78.0 49.5 %copy-start.27 = (pred[512]{0:T(512)(128)(4,1)}, pred[512]{0:T(512)(128)(4,1)S(1)}, u32[]{:S(2)}) copy-start(pred[512]{0:T(512)(128)(4,1)S(1)} %get-tuple-element.107) | copy-start | bytes 1540
  78.0 49.5 %copy-start.29 = (pred[512]{0:T(512)(128)(4,1)}, pred[512]{0:T(512)(128)(4,1)S(1)}, u32[]{:S(2)}) copy-start(pred[512]{0:T(512)(128)(4,1)S(1)} %get-tuple-element.108) | copy-start | bytes 1540
  78.0 49.5 %copy-start.37 = (pred[512]{0:T(512)(128)(4,1)}, pred[512]{0:T(512)(128)(4,1)S(1)}, u32[]{:S(2)}) copy-start(pred[512]{0:T(512)(128)(4,1)S(1)} %get-tuple-element.94) | copy-start | bytes 1540
  118.9 7.3 %collective-permute-start.2 = (bf16[15,1536]{1,0:T(8,128)(2,1)S(1)}, bf16[15,1536]{1,0:T(8,128)(2,1)S(1)}, u32[]{:S(2)}, u32[]{:S(2)}) collective-permute-start(bf16[15,1536]{1,0:T(8,128)(2,1)S(1)} %get-tuple-element.92), channel_id=1, source_target_pairs={{0,1},{1,2},{2,3},{3,4},{4,5},{5,6},{6,7},{8,9},{9,10},{10,11},{11... | collective-permute-start | bytes 138248 | tf_op jit(solution)/shard_map/ppermute | solution.py:12
  123.9 3.7 collective-permute-start.3
  169.0 5.8 collective-permute-start.4
  172.7 5.5 collective-permute-start.5
  263.4 207.4 %all-to-all-start.2 = ((bf16[8,128,1536]{2,1,0:T(8,128)(2,1)}), bf16[8,128,1536]{2,1,0:T(8,128)(2,1)}, u32[]{:S(2)}, u32[]{:S(2)}) async-start(bf16[8,128,1536]{2,1,0:T(8,128)(2,1)} %copy.37), calls=%async_computation.2 | async-start | bytes 6291456 | tf_op jit(solution)/shard_map/all_to_all | solution.py:124
  268.4 208.0 %reduce-scatter.5.cloned.1.call-start = ((), (), s32[]{:S(2)}) async-start(), calls=%async_computation.6 | async-start | bytes 1474560 | tf_op jit(solution)/shard_map/reduce_scatter | solution.py:130
  273.9 136.2 %copy-start.26 = (pred[512]{0:T(512)(128)(4,1)S(1)}, pred[512]{0:T(512)(128)(4,1)}, u32[]{:S(2)}) copy-start(pred[512]{0:T(512)(128)(4,1)} %copy-done.25) | copy-start | bytes 1540
  273.9 136.2 %copy-start.28 = (pred[512]{0:T(512)(128)(4,1)S(1)}, pred[512]{0:T(512)(128)(4,1)}, u32[]{:S(2)}) copy-start(pred[512]{0:T(512)(128)(4,1)} %copy-done.27) | copy-start | bytes 1540
  273.9 136.2 %copy-start.30 = (pred[512]{0:T(512)(128)(4,1)S(1)}, pred[512]{0:T(512)(128)(4,1)}, u32[]{:S(2)}) copy-start(pred[512]{0:T(512)(128)(4,1)} %copy-done.29) | copy-start | bytes 1540
  410.1 165.8 %all-reduce.2.cloned.1.call-start = ((), (), s32[]{:S(2)}) async-start(), calls=%async_computation.7 | async-start | bytes 393216 | tf_op jit(solution)/shard_map/psum | solution.py:128
  413.4 57.4 %copy-start.74 = (s32[4]{0:T(128)S(1)}, s32[4]{0:T(128)}, u32[]{:S(2)}) copy-start(s32[4]{0:T(128)} %copy-done.73) | copy-start | bytes 52
  470.8 106.7 %copy-start.1 = (bf16[1,1,4,128,1536]{4,3,2,1,0:T(8,128)(2,1)S(1)}, bf16[1,1,4,128,1536]{4,3,2,1,0:T(8,128)(2,1)}, u32[]{:S(2)}) copy-start(bf16[1,1,4,128,1536]{4,3,2,1,0:T(8,128)(2,1)} %param.7) | copy-start | bytes 4718596
  (72 other events, 1262.6 us)
Sparse Core Ops, SparseCore 0:
  9.8 97.3 all-gather.1
  246.2 161.2 reduce-scatter.6
  410.4 32.6 reduce-scatter.4
  449.1 126.6 all-reduce.1
where the time goes:
time: 593 us; the launch traced here: 584 us
  waiting for transfers between devices  287 us (48%)
  other arithmetic  127 us (21%)
  blocking collectives  42.7 us (7%)
  matrix products  39.9 us (7%)
  local copies, waits for them, and re-layouts  37.9 us (6%)
  starting transfers between devices  34.3 us (6%)
  between operations  15.7 us (3%)
    unnamed x5, waiting for transfers between devices  124 us
    psum x1, waiting for transfers between devices, local(): kernel_sum, gain_sum = lax.psum((kernel_term, gain_term), ('dp', 'tm'))  97.7 us
    reduce_sum x6, other arithmetic, local(): jnp.sum(grad_depth_f * jnp.where(masks[tap], glu_padded[tap:tap + rows].a...  71.6 us
    ppermute x3, waiting for transfers between devices, with_halo(): lax.ppermute(lax.slice_in_dim(block, block.shape[dim] - width, None, axis...  48.7 us
    another operation x2, other arithmetic  46 us
    psum x1, blocking collectives, local(): kernel_sum, gain_sum = lax.psum((kernel_term, gain_term), ('dp', 'tm'))  42.7 us
    unnamed x172, local copies, waits for them, and re-layouts  23.3 us
    all_to_all x1, waiting for transfers between devices, local(): lax.all_to_all(outgoing, 'tm', split_axis=0, concat_axis=0, tiled=True)  15.3 us
  transfers between devices with their start and end apart: 13, of which 6 were waited for; matrix products, arithmetic and copies ran while one was open for 14% of the time, Pallas kernels for 0%

commit v1 on v0

v1 whole, which is shorter than its diff:
```python
import functools

import jax
import jax.numpy as jnp
from jax import lax
from jax.experimental import pallas as pl
from jax.experimental.pallas import tpu as pltpu
from jax.sharding import PartitionSpec as P

BF = jnp.bfloat16
F32 = jnp.float32
RIM = 16
LANES = 128
TILE = 32


def params(count, mib=48):
    return pltpu.CompilerParams(
        dimension_semantics=("arbitrary",) * count, vmem_limit_bytes=mib << 20
    )


def flip(axis, mask):
    return [(i, i ^ mask) for i in range(lax.axis_size(axis))]


def flip_bit(axis, bit):
    return flip(axis, 1 << bit)


def bits_of(count):
    bits = count.bit_length() - 1
    assert 1 << bits == count
    return list(range(bits))


def copy_body(_, source, target):
    target[...] = source[...]


def pick_panels(source, index, count):
    _, rows, width = source.shape
    return pl.pallas_call(
        copy_body,
        grid_spec=pltpu.PrefetchScalarGridSpec(
            num_scalar_prefetch=1,
            grid=(count,),
            in_specs=[pl.BlockSpec((1, rows, width), lambda i, idx: (idx[i], 0, 0))],
            out_specs=pl.BlockSpec((1, rows, width), lambda i, idx: (i, 0, 0)),
        ),
        out_shape=jax.ShapeDtypeStruct((count, rows, width), source.dtype),
        compiler_params=params(1),
        name="pick_panels",
    )(index, source)


def gather_order(block, order):
    have = block[None]
    relative = [0]
    for bit in order:
        got = lax.ppermute(have, "dp", flip_bit("dp", bit))
        have = jnp.concatenate([have, got], axis=0)
        relative = relative + [r ^ (1 << bit) for r in relative]
    return have, relative


def gather_weights(w_in, core):
    shard, width = w_in.shape
    quarter = shard // 4
    count = lax.axis_size("dp")
    place = lax.axis_index("dp")
    bits = bits_of(count)
    half = lax.dynamic_slice_in_dim(w_in, core * (2 * quarter), 2 * quarter, axis=0)
    first, first_rel = gather_order(half[:quarter], bits)
    second, second_rel = gather_order(half[quarter:], bits[::-1])
    other_first = lax.ppermute(first, "tm", flip_bit("tm", 0))
    other_second = lax.ppermute(second, "tm", flip_bit("tm", 0))
    rels = [first_rel, second_rel]

    def out_index(side):
        index = []
        for source in range(2):
            for position in range(count):
                index.append(((place ^ rels[source][position]) * 2 + side) * 2 + source)
        return jnp.stack(index).astype(jnp.int32)

    def body(_, a, b, *rest):
        target = rest[-1]
        for number, ref in enumerate((a, b)):

            @pl.when(pl.program_id(0) == number)
            def _():
                target[...] = ref[...]

    def spec(number):
        def index(source, position, _):
            last = count - 1 if number == 0 else 0
            return (jnp.where(source == number, position, last), 0, 0)

        return pl.BlockSpec((1, quarter, width), index)

    def put(side, pair, *base):
        return pl.pallas_call(
            body,
            grid_spec=pltpu.PrefetchScalarGridSpec(
                num_scalar_prefetch=1,
                grid=(2, count),
                in_specs=[spec(0), spec(1)] + [pl.BlockSpec(memory_space=pl.ANY) for _ in base],
                out_specs=pl.BlockSpec(
                    (1, quarter, width),
                    lambda source, position, idx: (idx[source * count + position], 0, 0),
                ),
            ),
            out_shape=jax.ShapeDtypeStruct((4 * count, quarter, width), w_in.dtype),
            input_output_aliases={3: 0} if base else {},
            compiler_params=params(2),
            name="put_weights",
        )(out_index(side), *pair, *base)

    full = put(core, (first, second))
    full = put(1 - core, (other_first, other_second), full)
    return full.reshape(4 * quarter * count, width)


def forward_body(source, x_hbm, gain_ref, lin_w, gate_w, normed, pair, lin_out, gate_out, glu_out, xs, sems, *, panels):
    rows = xs.shape[1]

    def fetch(s):
        return pltpu.make_async_copy(x_hbm.at[source[s]], xs.at[s], sems.at[s])

    @pl.when(pl.program_id(0) == 0)
    def _():
        for s in range(panels):
            fetch(s).start()
        for s in range(panels):
            fetch(s).wait()

            x = xs[s].astype(F32)
            x = x - jnp.mean(x, axis=1, keepdims=True)
            scale = lax.rsqrt(jnp.mean(x * x, axis=1, keepdims=True) + 1e-05)
            normed[s * rows : (s + 1) * rows, :] = (x * scale * gain_ref[...]).astype(BF)

        pair[...] = normed[...]

    lin = jnp.dot(normed[...], lin_w[...], preferred_element_type=F32)
    lin_out[...] = lin
    gate = jnp.dot(normed[...], gate_w[...], preferred_element_type=F32)
    gate_out[...] = gate
    glu_out[...] = (lin * jax.nn.sigmoid(gate)).astype(BF)


def forward(arrived, source, gain, full_in, panels, block):
    _, rows, width = arrived.shape
    blocks = width // block
    column = pl.BlockSpec((panels * rows, block), lambda j, idx: (0, j))
    whole = pl.BlockSpec((panels * rows, width), lambda j, idx: (0, 0))
    wide = lambda dtype, times=1: jax.ShapeDtypeStruct((times * panels * rows, width), dtype)
    return pl.pallas_call(
        functools.partial(forward_body, panels=panels),
        grid_spec=pltpu.PrefetchScalarGridSpec(
            num_scalar_prefetch=1,
            grid=(blocks,),
            in_specs=[
                pl.BlockSpec(memory_space=pl.ANY),
                pl.BlockSpec((1, width), lambda j, idx: (0, 0)),
                pl.BlockSpec((width, block), lambda j, idx: (0, j)),
                pl.BlockSpec((width, block), lambda j, idx: (0, blocks + j)),
            ],
            out_specs=[
                whole,
                whole,
                column,
                column,
                column,
            ],
            scratch_shapes=[
                pltpu.VMEM((panels, rows, width), BF),
                pltpu.SemaphoreType.DMA((panels,)),
            ],
        ),
        out_shape=[wide(BF), wide(BF, 2), wide(F32), wide(F32), wide(BF)],
        compiler_params=params(1),
        name="forward",
    )(source, arrived, gain.reshape(1, width), full_in, full_in)


def fill_padded(flags, padded, main, low, high, panels, length):
    for s in range(panels):
        at = s * length
        middle = main[at : at + length, :].astype(F32)
        before = low[...] if s == 0 else main[at - RIM : at, :]
        after = high[...] if s == panels - 1 else main[at + length : at + length + RIM, :]
        before = jnp.where(flags[s] > 0, before.astype(F32), 0.0)
        after = jnp.where(flags[panels + s] > 0, after.astype(F32), 0.0)
        for chunk in range(main.shape[1] // LANES):
            lanes = slice(chunk * LANES, (chunk + 1) * LANES)
            padded[chunk, s, RIM : RIM + length, :] = middle[:, lanes]
            padded[chunk, s, 0:RIM, :] = before[:, lanes]
            padded[chunk, s, RIM + length :, :] = after[:, lanes]


def shifted_sum(padded, weights, chunk, s, start, taps, flip):
    lanes = pl.ds(chunk * LANES, LANES)
    total = jnp.zeros((TILE, LANES), F32)
    for tap in range(taps):
        offset = taps - tap if flip else tap + 1
        view = padded[chunk, s, pl.ds(start + offset, TILE), :]
        total = total + weights[pl.ds(tap, 1), lanes] * view
    return total


def tiles(width, panels, length, work):
    for chunk in range(width // LANES):

        def step(s, carry):
            for start in range(0, length, TILE):
                rows = pl.ds(pl.multiple_of(s * length + start, TILE), TILE)
                work(chunk, s, start, rows, pl.ds(chunk * LANES, LANES))
            return carry

        lax.fori_loop(0, panels, step, 0)


def depth_body(flags, glu, low, high, upstream, weights, out, padded, *, panels, length, taps):
    fill_padded(flags, padded, glu, low, high, panels, length)

    def work(chunk, s, start, rows, lanes):
        depth = shifted_sum(padded, weights, chunk, s, start, taps, False)
        sig = jax.nn.sigmoid(depth)
        up = upstream[rows, lanes].astype(F32)
        out[rows, lanes] = (up * sig * (1.0 + depth * (1.0 - sig))).astype(BF)

    tiles(glu.shape[1], panels, length, work)


def taps_body(flags, glu, low, high, grad, out, padded, partial, *, panels, length, taps):
    fill_padded(flags, padded, glu, low, high, panels, length)
    for chunk in range(glu.shape[1] // LANES):
        lanes = pl.ds(chunk * LANES, LANES)
        partial[...] = jnp.zeros_like(partial)

        def step(s, carry):
            rows = pl.ds(pl.multiple_of(s * length, length), length)
            g = grad[rows, lanes].astype(F32)
            for tap in range(taps):
                product = g * padded[chunk, s, pl.ds(tap + 1, length), :]
                partial[tap] += jnp.sum(product.reshape(length // 8, 8, LANES), axis=0)
            return carry

        lax.fori_loop(0, panels, step, 0)
        out[:, lanes] = jnp.sum(partial[...], axis=1)


def gated_body(flags, grad, low, high, lin, gate, weights, *refs, panels, length, taps):
    *outs, padded = refs
    fill_padded(flags, padded, grad, low, high, panels, length)

    def work(chunk, s, start, rows, lanes):
        total = shifted_sum(padded, weights, chunk, s, start, taps, True)
        sig = jax.nn.sigmoid(gate[rows, lanes])
        scaled = total * sig
        results = (scaled.astype(BF), (scaled * lin[rows, lanes] * (1.0 - sig)).astype(BF))
        for number, out in enumerate(outs):
            out[rows, lanes] = results[number % 2]

    tiles(grad.shape[1], panels, length, work)


def gated(flags, grad_depth, low, high, lin, gate, kernel, block, parities, parity, sizes, twice=False):
    rows, width = grad_depth.shape
    panels = sizes["panels"]
    column = lambda height: pl.BlockSpec((height, block), lambda j, idx: (0, j * parities + idx[2 * panels]))
    shapes = [jax.ShapeDtypeStruct((rows * times, width // parities), BF) for times in (1, 1, 2, 2)]
    shapes = shapes[: 4 if twice else 2]
    return pl.pallas_call(
        functools.partial(gated_body, **sizes),
        grid_spec=pltpu.PrefetchScalarGridSpec(
            num_scalar_prefetch=1,
            grid=(width // block // parities,),
            in_specs=[column(h) for h in (rows, RIM, RIM, rows, rows, kernel.shape[0])],
            out_specs=[pl.BlockSpec((rows, block), lambda j, idx: (0, j)) for _ in shapes],
            scratch_shapes=[
                pltpu.VMEM((block // LANES, panels, sizes["length"] + 2 * RIM, LANES), F32)
            ],
        ),
        out_shape=shapes,
        compiler_params=params(1),
        name="gated",
    )(jnp.append(flags, parity), grad_depth, low, high, lin, gate, kernel)


def back_body(source, *refs, grads, block, panels, piece):
    gradients = refs[:grads]
    w_ref, x_hbm, up_hbm, gain_ref, out_hbm, gain_out, total, xs, ups, outs, sems = refs[grads:]
    step = pl.program_id(0)

    def fetch(s):
        return (
            pltpu.make_async_copy(x_hbm.at[source[s]], xs.at[s], sems.at[s]),
            pltpu.make_async_copy(up_hbm.at[s], ups.at[s], sems.at[panels + s]),
        )

    def put(s):
        return pltpu.make_async_copy(outs.at[s], out_hbm.at[source[s]], sems.at[2 * panels + s])

    @pl.when(step == 0)
    def _():
        for s in range(panels):
            for copy in fetch(s):
                copy.start()

    acc = None
    for number, grad in enumerate(gradients):
        pieces = grad.shape[1] // piece
        for i in range(pieces):
            column = (number % 2 * pieces + i) * (grads // 2) * piece
            if grads > 2:
                column = column + (source[panels] ^ (number // 2)) * piece
                column = pl.multiple_of(column, LANES)
            term = lax.dot_general(
                grad[:, i * piece : (i + 1) * piece],
                w_ref[:, pl.ds(column, piece)],
                (((1,), (1,)), ((), ())),
                preferred_element_type=F32,
            )
            acc = term if acc is None else acc + term
    total[:, pl.ds(pl.multiple_of(step * block, block), block)] = acc

    @pl.when(step == pl.num_programs(0) - 1)
    def _():
        rows = xs.shape[1]
        gain = gain_ref[...]
        gain_sum = jnp.zeros_like(gain)
        for s in range(panels):
            for copy in fetch(s):
                copy.wait()

            x = xs[s].astype(F32)
            x = x - jnp.mean(x, axis=1, keepdims=True)
            scale = lax.rsqrt(jnp.mean(x * x, axis=1, keepdims=True) + 1e-05)
            unit = x * scale
            g = total[s * rows : (s + 1) * rows, :]
            gain_sum = gain_sum + jnp.sum(g * unit, axis=0, keepdims=True)
            q = g * gain
            mean_q = jnp.mean(q, axis=1, keepdims=True)
            mean_u = jnp.mean(q * unit, axis=1, keepdims=True)
            outs[s] = (ups[s].astype(F32) + scale * (q - mean_q - unit * mean_u)).astype(BF)
            put(s).start()
        gain_out[...] = gain_sum
        for s in range(panels):
            put(s).wait()


def back(gradients, core, full_in, arrived, source, upstream, gain, piece, block):
    _, rows, width = arrived.shape
    panels = upstream.shape[0]
    constant = lambda rank: (lambda n, idx: (0,) * rank)
    hbm = pl.BlockSpec(memory_space=pl.ANY)
    panel_scratch = pltpu.VMEM((panels, rows, width), BF)
    return pl.pallas_call(
        functools.partial(back_body, grads=len(gradients), block=block, panels=panels, piece=piece),
        grid_spec=pltpu.PrefetchScalarGridSpec(
            num_scalar_prefetch=1,
            grid=(width // block,),
            in_specs=[pl.BlockSpec(g.shape, constant(2)) for g in gradients]
            + [
                pl.BlockSpec((block, full_in.shape[1]), lambda n, idx: (n, 0)),
                hbm,
                hbm,
                pl.BlockSpec((1, width), constant(2)),
            ],
            out_specs=[hbm, pl.BlockSpec((1, width), constant(2))],
            scratch_shapes=[
                pltpu.VMEM((panels * rows, width), F32),
                panel_scratch,
                panel_scratch,
                panel_scratch,
                pltpu.SemaphoreType.DMA((3 * panels,)),
            ],
        ),
        out_shape=[
            jax.ShapeDtypeStruct(arrived.shape, BF),
            jax.ShapeDtypeStruct((1, width), F32),
        ],
        compiler_params=params(1),
        name="back",
    )(jnp.append(source, core), *gradients, full_in, arrived, upstream, gain.reshape(1, width))


def outer_sum(left, right):
    return lax.dot_general(
        left, right, (((0,), (0,)), ((), ())), preferred_element_type=F32
    ).astype(BF)


def halve(block, order):
    place = lax.axis_index("dp")
    count = lax.axis_size("dp")
    bits = len(bits_of(count))
    shape = block.shape[1:]
    block = block.reshape((2,) * bits + shape)
    live = list(reversed(range(bits)))
    for bit in order:
        dim = live.index(bit)
        mine = (place >> bit) & 1
        keep = lax.dynamic_index_in_dim(block, mine, dim, keepdims=False)
        send = lax.dynamic_index_in_dim(block, 1 - mine, dim, keepdims=False)
        got = lax.ppermute(send, "dp", flip_bit("dp", bit))
        block = (keep.astype(F32) + got.astype(F32)).astype(BF)
        live.remove(bit)
    return block


def sum_everywhere(values):
    steps = [("dp", bit) for bit in bits_of(lax.axis_size("dp"))] + [("tm", 0)]
    pad = -values.shape[0] % (1 << len(steps))
    rows = values.shape[0]
    values = jnp.pad(values, ((0, pad), (0, 0)))
    side = lambda axis, bit: (lax.axis_index(axis) >> bit) & 1
    for axis, bit in steps:
        halves = values.reshape(2, values.shape[0] // 2, values.shape[1])
        mine = side(axis, bit)
        send = lax.dynamic_index_in_dim(halves, 1 - mine, 0, keepdims=False)
        keep = lax.dynamic_index_in_dim(halves, mine, 0, keepdims=False)
        values = keep + lax.ppermute(send, axis, flip_bit(axis, bit))
    terms = [values]
    for mask in range(2, lax.axis_size("tm"), 2):
        terms.append(lax.ppermute(values, "tm", flip("tm", mask)))
    while len(terms) > 1:
        terms = [a + b for a, b in zip(terms[::2], terms[1::2])]
    values = terms[0]
    for axis, bit in steps[::-1]:
        got = lax.ppermute(values, axis, flip_bit(axis, bit))
        first = side(axis, bit) == 0
        values = jnp.concatenate([jnp.where(first, values, got), jnp.where(first, got, values)])
    return values[:rows]


def sum_across(share):
    count = share.shape[0]
    place = lax.axis_index("tm") // 2
    total = lax.dynamic_index_in_dim(share, place, 0, keepdims=False).astype(F32)
    for turn in range(1, count):
        piece = lax.dynamic_index_in_dim(share, place ^ turn, 0, keepdims=False)
        pairs = [(i, i ^ (2 * turn)) for i in range(2 * count)]
        total = total + lax.ppermute(piece, "tm", pairs).astype(F32)
    return total


def edges(values, width):
    count = lax.axis_size("tm")
    low = lax.ppermute(values[-width:], "tm", [(i, i + 1) for i in range(count - 1)])
    high = lax.ppermute(values[:width], "tm", [(i + 1, i) for i in range(count - 1)])
    return low, high


def local(frames, route, utterance, gain, w_in, kernel, cotangent):
    panels, length, width = frames.shape[2:]
    owners = lax.axis_size("tm")
    rows = panels * length
    taps = kernel.shape[0]
    reach = taps // 2
    assert reach < RIM and taps == 31
    loaded = frames[0, 0]
    target = route[0, 0]
    labels = utterance[0, 0]
    upstream = cotangent[0, 0]
    core = lax.axis_index("tm") % 2
    owner_of = target // panels
    pick = owner_of[None, :] == jnp.arange(owners, dtype=jnp.int32)[:, None]
    panel_of = jnp.sum(jnp.where(pick, jnp.arange(panels, dtype=jnp.int32)[None, :], 0), axis=1)
    outgoing = pick_panels(loaded, panel_of.astype(jnp.int32), owners)
    arrived = lax.all_to_all(outgoing, "tm", split_axis=0, concat_axis=0, tiled=True)
    me = lax.axis_index("tm")
    tags = jnp.stack([target, labels + 1])[None]
    tags = jnp.concatenate([tags, lax.ppermute(tags, "tm", flip_bit("tm", 0))])
    rest = [lax.ppermute(tags, "tm", flip("tm", i)) for i in range(2, owners, 2)]
    tags = jnp.concatenate([tags] + rest)
    loader = (jnp.arange(owners, dtype=jnp.int32) ^ me)[None, :, None]
    position = me * panels - 1 + jnp.arange(panels + 2, dtype=jnp.int32)
    found = tags[None, :, 0] == position[:, None, None]
    line = jnp.sum(jnp.where(found, tags[None, :, 1], 0), axis=(1, 2))
    source = jnp.sum(jnp.where(found[1:-1], loader, 0), axis=(1, 2)).astype(jnp.int32)
    flags = jnp.concatenate([line[1:-1] == line[:-2], line[1:-1] == line[2:]]).astype(jnp.int32)

    full_in = gather_weights(w_in, core)
    normed, both_normed, lin, gate, glu = forward(arrived, source, gain, full_in, panels, 2 * LANES)
    other_normed = lax.ppermute(normed, "tm", flip_bit("tm", 0))
    glu_low, glu_high = edges(glu, RIM)

    lane_block = 2 * LANES
    column = lambda height: pl.BlockSpec((height, lane_block), lambda j, idx: (0, j))
    sizes = dict(panels=panels, length=length, taps=taps)
    padded_of = lambda lanes: pltpu.VMEM((lanes // LANES, panels, length + 2 * RIM, LANES), F32)
    grad_depth = pl.pallas_call(
        functools.partial(depth_body, **sizes),
        grid_spec=pltpu.PrefetchScalarGridSpec(
            num_scalar_prefetch=1,
            grid=(width // lane_block,),
            in_specs=[column(rows), column(RIM), column(RIM), column(rows), column(taps)],
            out_specs=column(rows),
            scratch_shapes=[padded_of(lane_block)],
        ),
        out_shape=jax.ShapeDtypeStruct((rows, width), BF),
        compiler_params=params(1),
        name="depth",
    )(flags, glu, glu_low, glu_high, upstream.reshape(rows, width), kernel)
    grad_low, grad_high = edges(grad_depth, RIM)
    kernel_term = pl.pallas_call(
        functools.partial(taps_body, **sizes),
        grid_spec=pltpu.PrefetchScalarGridSpec(
            num_scalar_prefetch=1,
            grid=(width // lane_block,),
            in_specs=[column(rows), column(RIM), column(RIM), column(rows)],
            out_specs=column(taps + 1),
            scratch_shapes=[padded_of(lane_block), pltpu.VMEM((taps + 1, 8, LANES), F32)],
        ),
        out_shape=jax.ShapeDtypeStruct((taps + 1, width), F32),
        compiler_params=params(1),
        name="taps",
    )(flags, glu, glu_low, glu_high, grad_depth)

    piece = 2 * width // owners
    arguments = (flags, grad_depth, grad_low, grad_high, lin, gate, kernel)
    if piece % LANES == 0:
        give = gated(*arguments, piece, 2, 1 - core, sizes)
        others = [lax.ppermute(g, "tm", flip_bit("tm", 0)) for g in give]
        *own, first, second = gated(*arguments, piece, 2, core, sizes, True)
        gradients, run = (*own, *give), piece
        join = lambda base, other: lax.dynamic_update_slice(base, other, (rows, 0))
        mine = (first, second)
    else:
        gradients, run = tuple(gated(*arguments, lane_block, 1, 0, sizes)), width
        pick_parity = lambda values, parity: lax.dynamic_index_in_dim(
            values.reshape(rows, owners // 4, 2, piece), parity, 2, keepdims=False
        ).reshape(rows, width // 2)
        give = [pick_parity(g, 1 - core) for g in gradients]
        others = [lax.ppermute(g, "tm", flip_bit("tm", 0)) for g in give]
        mine = [pick_parity(g, core) for g in gradients]
        join = lambda base, other: jnp.concatenate([base, other], axis=0)
    both_normed = lax.dynamic_update_slice(both_normed, other_normed, (rows, 0))
    grad_slots, gain_term = back(
        gradients, core, full_in, arrived, source, upstream, gain, run, 2 * LANES
    )
    returned = lax.all_to_all(grad_slots, "tm", split_axis=0, concat_axis=0, tiled=True)
    count = lax.axis_size("dp")
    bits = bits_of(count)
    shares = []
    for side, order in ((0, bits), (1, bits[::-1])):
        term = outer_sum(both_normed, join(mine[side], others[side]))
        shares.append(halve(term.reshape(count, width // count, -1), order))
    share = jnp.concatenate(shares, axis=1)
    share = share.reshape(width // count, owners // 2, piece).transpose(1, 0, 2)
    shard_in = sum_across(share)
    grad_loaded = pick_panels(returned, owner_of.astype(jnp.int32), panels)
    sums = sum_everywhere(jnp.concatenate([kernel_term[:taps], gain_term], axis=0))
    return (grad_loaded[None, None], shard_in, sums[:taps], sums[taps])


def solution(mesh):
    in_specs = (
        P("dp", "tm", None, None, None),
        P("dp", "tm", None),
        P("dp", "tm", None),
        P(),
        P("dp", None),
        P(),
        P("dp", "tm", None, None, None),
    )
    out_specs = (P("dp", "tm", None, None, None), P("dp", "tm"), P(), P())
    return jax.shard_map(local, mesh=mesh, in_specs=in_specs, out_specs=out_specs, check_vma=False)
```

time: 593 us -> 305 us (0.51); the launches traced: 584 us -> 304 us
  waiting for transfers between devices: 287 us -> 129 us
  other arithmetic: 127 us -> 9.44 us
  Pallas kernels: 0 us -> 81.4 us
  blocking collectives: 42.7 us -> 0 us
  matrix products: 39.9 us -> 7.98 us
  starting transfers between devices: 34.3 us -> 51.5 us
  between operations: 15.7 us -> 1.12 us
  local copies, waits for them, and re-layouts: 37.9 us -> 23.4 us
    unnamed x5 -> x0, waiting for transfers between devices: 124 us -> none
    psum x1 -> x0, waiting for transfers between devices: 97.7 us -> none  [local(): kernel_sum, gain_sum = lax.psum((kernel_term, gain_term), ('dp', 'tm'))]
    pallas_call x0 -> x10, Pallas kernels: none -> 81.4 us  [the longest x2 15.4 us: gated(): pl.pallas_call(functools.partial(gated_body, **sizes), grid_spec=pltpu.Pr...]
    ppermute x6 -> x33, waiting for transfers between devices: 50 us -> 129 us  [the longest x4 37.3 us: gather_order(): got = lax.ppermute(have, 'dp', flip_bit('dp', bit))]
    reduce_sum x9 -> x3, other arithmetic: 72.8 us -> 0.53 us  [the longest x1 0.27 us: local(): line = jnp.sum(jnp.where(found, tags[None, :, 1], 0), axis=(1, 2))]
    another operation x2 -> x0, other arithmetic: 46 us -> none
    psum x1 -> x0, blocking collectives: 42.7 us -> none  [local(): kernel_sum, gain_sum = lax.psum((kernel_term, gain_term), ('dp', 'tm'))]
    dot_general x6 -> x0, matrix products: 32 us -> none  [the longest x1 11.1 us: times_transposed(): lax.dot_general(left, right, (((1,), (1,)), ((), ())), preferred_element_...]
  transfers between devices with their start and end apart: 13 -> 35, of which waited for: 6 -> 20; matrix products, arithmetic and copies ran while one was open for 14% -> 12% of each run, Pallas kernels for 0% -> 8%
where the time goes in v1:
time: 305 us; the launch traced here: 304 us
  waiting for transfers between devices  129 us (42%)
  Pallas kernels  81.4 us (27%)
  starting transfers between devices  51.5 us (17%)
  local copies, waits for them, and re-layouts  23.4 us (8%)
  other arithmetic  9.44 us (3%)
  matrix products  7.98 us (3%)
    ppermute x4, waiting for transfers between devices, gather_order(): got = lax.ppermute(have, 'dp', flip_bit('dp', bit))  37.3 us
    ppermute x3, waiting for transfers between devices, sum_everywhere(): got = lax.ppermute(values, axis, flip_bit(axis, bit))  26.9 us
    ppermute x3, waiting for transfers between devices, sum_across(): total = total + lax.ppermute(piece, 'tm', pairs).astype(F32)  22 us
    ppermute x3, waiting for transfers between devices, local(): lax.ppermute(tags, 'tm', flip('tm', i))  15.5 us
    pallas_call x2, Pallas kernels, gated(): pl.pallas_call(functools.partial(gated_body, **sizes), grid_spec=pltpu.Pr...  15.4 us
    pallas_call x1, Pallas kernels, back(): pl.pallas_call(functools.partial(back_body, grads=len(gradients), block=b...  14.5 us
    pallas_call x2, Pallas kernels, put(): pl.pallas_call(body, grid_spec=pltpu.PrefetchScalarGridSpec(num_scalar_pr...  14.3 us
    pallas_call x1, Pallas kernels, forward(): pl.pallas_call(functools.partial(forward_body, panels=panels), grid_spec=...  13.2 us
  transfers between devices with their start and end apart: 35, of which 20 were waited for; matrix products, arithmetic and copies ran while one was open for 12% of the time, Pallas kernels for 8%

profile of v1, /device:TPU:8, one launch (start us, length us, event | category | flops | bytes accessed | tf_op | source)
XLA Modules:
  0.0 304.0 jit_solution(2102355707611716787)
XLA Ops:
  2.8 3.8 %pick_panels.2 = bf16[8,128,1536]{2,1,0:T(8,128)(2,1)} custom-call(s32[8]{0:T(128)S(1)} %select_reduce_fusion.2._, bf16[4,128,1536]{2,1,0:T(8,128)(2,1)S(1)} %bitcast.98), custom_call_target="tpu_custom_call" | custom-call | tf_op jit(solution)/shard_map/pick_panels/pallas_call | solution.py:43
  6.6 5.5 %all-to-all-start = ((bf16[8,128,1536]{2,1,0:T(8,128)(2,1)}), bf16[8,128,1536]{2,1,0:T(8,128)(2,1)}, u32[]{:S(2)}, u32[]{:S(2)}) async-start(bf16[8,128,1536]{2,1,0:T(8,128)(2,1)} %pick_panels.2), calls=%async_computation | async-start | bytes 6291456 | tf_op jit(solution)/shard_map/all_to_all | solution.py:473
  15.3 12.3 %collective-permute-done.7 = bf16[1,96,3072]{2,1,0:T(8,128)(2,1)S(1)} collective-permute-done((bf16[1,96,3072]{2,1,0:T(8,128)(2,1)S(1)}, bf16[1,96,3072]{2,1,0:T(8,128)(2,1)S(1)}, u32[]{:S(2)}, u32[]{:S(2)}) %collective-permute-start.7) | collective-permute-done | bytes 589856 | tf_op jit(solution)/shard_map/ppermute | solution.py:61
  31.0 23.9 %collective-permute-done.8 = bf16[2,96,3072]{2,1,0:T(8,128)(2,1)S(1)} collective-permute-done((bf16[2,96,3072]{2,1,0:T(8,128)(2,1)S(1)}, bf16[2,96,3072]{2,1,0:T(8,128)(2,1)S(1)}, u32[]{:S(2)}, u32[]{:S(2)}) %collective-permute-start.8) | collective-permute-done | bytes 1179680 | tf_op jit(solution)/shard_map/ppermute | solution.py:61
  58.8 4.5 %collective-permute-done = s32[1,2,4]{2,1,0:T(2,128)S(1)} collective-permute-done((s32[1,2,4]{2,1,0:T(2,128)S(1)}, s32[1,2,4]{2,1,0:T(2,128)S(1)}, u32[]{:S(2)}, u32[]{:S(2)}) %collective-permute-start) | collective-permute-done | bytes 64 | tf_op jit(solution)/shard_map/ppermute | solution.py:476
  66.9 13.4 %collective-permute-done.2 = s32[2,2,4]{2,1,0:T(2,128)S(1)} collective-permute-done((s32[2,2,4]{2,1,0:T(2,128)S(1)}, s32[2,2,4]{2,1,0:T(2,128)S(1)}, u32[]{:S(2)}, u32[]{:S(2)}) %collective-permute-start.2) | collective-permute-done | bytes 96 | tf_op jit(solution)/shard_map/ppermute | solution.py:477
  83.1 6.3 %put_weights.2.rest_0_ = bf16[16,96,3072]{2,1,0:T(8,128)(2,1)} custom-call(s32[8]{0:T(128)S(1)} %stack.76._, bf16[4,96,3072]{2,1,0:T(8,128)(2,1)} %pad_maximum_fusion.a, bf16[4,96,3072]{2,1,0:T(8,128)(2,1)S(1)} %pad_maximum_fusion.1.b), custom_call_target="tpu_custom_call" | custom-call | tf_op jit(solution)/shard_map/put_weights/pallas_call | solution.py:103
  89.4 8.0 %put_weights.3 = bf16[16,96,3072]{2,1,0:T(8,128)(2,1)} custom-call(s32[8]{0:T(128)S(1)} %stack.67._, bf16[4,96,3072]{2,1,0:T(8,128)(2,1)} %collective-permute-done.6.a, bf16[4,96,3072]{2,1,0:T(8,128)(2,1)} %collective-permute-done.9.b, bf16[16,96,3072]{2,1,0:T(8,128)(2,1)} %put_weights.2.rest_0_), custom_call_target="tpu_custom_call", output_to_operand_aliasing={{}: (3, {})} | custom-call | tf_op jit(solution)/shard_map/put_weights/pallas_call | solution.py:103
  97.4 13.2 %forward.1 = (bf16[512,1536]{1,0:T(8,128)(2,1)}, bf16[1024,1536]{1,0:T(8,128)(2,1)}, f32[512,1536]{1,0:T(8,128)}, f32[512,1536]{1,0:T(8,128)}, bf16[512,1536]{1,0:T(8,128)(2,1)S(1)}) custom-call(s32[4]{0:T(128)S(1)} %select_reduce_fusion.1.source, bf16[8,128,1536]{2,1,0:T(8,128)(2,1)} %all-to-all-done.x_hbm.refs_5_, ...), custom_call_target="tpu_custom_call" | custom-call | tf_op jit(solution)/shard_map/forward/pallas_call | solution.py:158
  112.5 3.6 %collective-permute-start.11 = (bf16[16,1536]{1,0:T(8,128)(2,1)S(1)}, bf16[16,1536]{1,0:T(8,128)(2,1)S(1)}, u32[]{:S(2)}, u32[]{:S(2)}) collective-permute-start(bf16[16,1536]{1,0:T(8,128)(2,1)S(1)} %get-tuple-element.48), channel_id=1, source_target_pairs={{1,0},{2,1},{3,2},{4,3},{5,4},{6,5},{7,6},{9,8},{10,9},{11,10},{12... | collective-permute-start | bytes 147464 | tf_op jit(solution)/shard_map/ppermute | solution.py:453
  117.9 9.1 %depth.1.grad = bf16[512,1536]{1,0:T(8,128)(2,1)S(1)} custom-call(s32[8]{0:T(128)S(1)} %add_convert_fusion.flags, bf16[512,1536]{1,0:T(8,128)(2,1)S(1)} %get-tuple-element.17.glu, bf16[16,1536]{1,0:T(8,128)(2,1)S(1)} %collective-permute-done.10.low, bf16[16,1536]{1,0:T(8,128)(2,1)S(1)} %collective-permute-done.11.high, bf16[512,1536]{1,0:T(8,128)(2,1)S(1)} %bitcast.96, ...), custom_call_target="tpu_custom_call" | custom-call | tf_op jit(solution)/shard_map/depth/pallas_call | solution.py:495
  129.5 3.3 %collective-permute-start.13 = (bf16[16,1536]{1,0:T(8,128)(2,1)S(1)}, bf16[16,1536]{1,0:T(8,128)(2,1)S(1)}, u32[]{:S(2)}, u32[]{:S(2)}) collective-permute-start(bf16[16,1536]{1,0:T(8,128)(2,1)S(1)} %get-tuple-element.46), channel_id=1, source_target_pairs={{1,0},{2,1},{3,2},{4,3},{5,4},{6,5},{7,6},{9,8},{10,9},{11,10},{12... | collective-permute-start | bytes 147464 | tf_op jit(solution)/shard_map/ppermute | solution.py:453
  132.9 8.8 %taps.1 = f32[32,1536]{1,0:T(8,128)S(1)} custom-call(s32[8]{0:T(128)S(1)} %add_convert_fusion.flags, bf16[512,1536]{1,0:T(8,128)(2,1)S(1)} %get-tuple-element.17.glu, bf16[16,1536]{1,0:T(8,128)(2,1)S(1)} %collective-permute-done.10.low, bf16[16,1536]{1,0:T(8,128)(2,1)S(1)} %collective-permute-done.11.high, bf16[512,1536]{1,0:T(8,128)(2,1)S(1)} %depth.1.grad), custom_call_target="tpu_custom_call" | custom-call | tf_op jit(solution)/shard_map/taps/pallas_call | solution.py:509
  141.7 7.8 %gated.3 = (bf16[512,768]{1,0:T(8,128)(2,1)}, bf16[512,768]{1,0:T(8,128)(2,1)}) custom-call(s32[9]{0:T(128)S(1)} %get-tuple-element.61.flags, bf16[512,1536]{1,0:T(8,128)(2,1)S(1)} %depth.1.grad, bf16[16,1536]{1,0:T(8,128)(2,1)S(1)} %collective-permute-done.12.low, bf16[16,1536]{1,0:T(8,128)(2,1)S(1)} %collective-permute-done.13.high, ...), custom_call_target="tpu_custom_call" | custom-call | tf_op jit(solution)/shard_map/gated/pallas_call | solution.py:275
  149.5 7.6 %gated.2 = (bf16[512,768]{1,0:T(8,128)(2,1)S(1)}, bf16[512,768]{1,0:T(8,128)(2,1)S(1)}, bf16[1024,768]{1,0:T(8,128)(2,1)S(1)}, bf16[1024,768]{1,0:T(8,128)(2,1)S(1)}) custom-call(s32[9]{0:T(128)S(1)} %get-tuple-element.62.flags, bf16[512,1536]{1,0:T(8,128)(2,1)} %copy-done, bf16[16,1536]{1,0:T(8,128)(2,1)S(1)} %collective-permute-done.12.low, ...), custom_call_target="tpu_custom_call" | custom-call | tf_op jit(solution)/shard_map/gated/pallas_call | solution.py:275
  158.3 14.5 %back.1 = (bf16[8,128,1536]{2,1,0:T(8,128)(2,1)}, f32[1,1536]{1,0:T(1,128)S(1)}) custom-call(s32[5]{0:T(128)S(1)} %pad_add_fusion.1.source, bf16[512,768]{1,0:T(8,128)(2,1)S(1)} %get-tuple-element.20.refs_0_, bf16[512,768]{1,0:T(8,128)(2,1)S(1)} %get-tuple-element.21.refs_1_, bf16[512,768]{1,0:T(8,128)(2,1)} %get-tuple-element.22.refs_2_, ...), custom_call_target="tpu_custom_call" | custom-call | tf_op jit(solution)/shard_map/back/pallas_call | solution.py:360
  174.4 3.2 %collective-permute-done.24 = f32[16,1536]{1,0:T(8,128)S(1)} collective-permute-done((f32[16,1536]{1,0:T(8,128)S(1)}, f32[16,1536]{1,0:T(8,128)S(1)}, u32[]{:S(2)}, u32[]{:S(2)}) %collective-permute-start.24) | collective-permute-done | bytes 98336 | tf_op jit(solution)/shard_map/ppermute | solution.py:425
  189.7 6.2 %all-to-all-start.1 = ((bf16[8,128,1536]{2,1,0:T(8,128)(2,1)}), bf16[8,128,1536]{2,1,0:T(8,128)(2,1)S(1)}, u32[]{:S(2)}, u32[]{:S(2)}) async-start(bf16[8,128,1536]{2,1,0:T(8,128)(2,1)} %get-tuple-element.24), calls=%async_computation.1 | async-start | bytes 6291456 | tf_op jit(solution)/shard_map/all_to_all | solution.py:545
  209.0 5.0 %convolution_convert_fusion = bf16[1536,768]{1,0:T(8,128)(2,1)S(1)} fusion(bf16[1024,1536]{1,0:T(8,128)(2,1)} %copy-done.12, bf16[1024,768]{1,0:T(8,128)(2,1)} %get-tuple-element.65), kind=kOutput, calls=%fused_computation | convolution fusion | flops 2417098752 | bytes 7077888 | tf_op jit(solution)/shard_map/dot_general | solution.py:391
  220.1 26.9 %collective-permute-done.31 = f32[8,1536]{1,0:T(8,128)S(1)} collective-permute-done((f32[8,1536]{1,0:T(8,128)S(1)}, f32[8,1536]{1,0:T(8,128)S(1)}, u32[]{:S(2)}, u32[]{:S(2)}) %collective-permute-start.31) | collective-permute-done | bytes 49184 | tf_op jit(solution)/shard_map/ppermute | solution.py:433
  259.2 9.3 %collective-permute-done.17 = bf16[384,768]{0,1:T(8,128)(2,1)S(1)} collective-permute-done((bf16[384,768]{0,1:T(8,128)(2,1)S(1)}, bf16[384,768]{0,1:T(8,128)(2,1)S(1)}, u32[]{:S(2)}, u32[]{:S(2)}) %collective-permute-start.17) | collective-permute-done | bytes 589856 | tf_op jit(solution)/shard_map/ppermute | solution.py:408
  276.7 5.5 %collective-permute-done.21 = bf16[384,384]{0,1:T(8,128)(2,1)S(1)} collective-permute-done((bf16[384,384]{0,1:T(8,128)(2,1)S(1)}, bf16[384,384]{0,1:T(8,128)(2,1)S(1)}, u32[]{:S(2)}, u32[]{:S(2)}) %collective-permute-start.21) | collective-permute-done | bytes 294944 | tf_op jit(solution)/shard_map/ppermute | solution.py:446
  282.1 11.8 %collective-permute-done.22 = bf16[384,384]{0,1:T(8,128)(2,1)S(1)} collective-permute-done((bf16[384,384]{0,1:T(8,128)(2,1)S(1)}, bf16[384,384]{0,1:T(8,128)(2,1)S(1)}, u32[]{:S(2)}, u32[]{:S(2)}) %collective-permute-start.22) | collective-permute-done | bytes 294944 | tf_op jit(solution)/shard_map/ppermute | solution.py:446
  294.0 4.7 %collective-permute-done.23 = bf16[384,384]{0,1:T(8,128)(2,1)S(1)} collective-permute-done((bf16[384,384]{0,1:T(8,128)(2,1)S(1)}, bf16[384,384]{0,1:T(8,128)(2,1)S(1)}, u32[]{:S(2)}, u32[]{:S(2)}) %collective-permute-start.23) | collective-permute-done | bytes 294944 | tf_op jit(solution)/shard_map/ppermute | solution.py:446
  (151 shorter events, 84.6 us)
Async XLA Ops:
  6.6 90.8 %all-to-all-start = ((bf16[8,128,1536]{2,1,0:T(8,128)(2,1)}), bf16[8,128,1536]{2,1,0:T(8,128)(2,1)}, u32[]{:S(2)}, u32[]{:S(2)}) async-start(bf16[8,128,1536]{2,1,0:T(8,128)(2,1)} %pick_panels.2), calls=%async_computation | async-start | bytes 6291456 | tf_op jit(solution)/shard_map/all_to_all | solution.py:473
  12.2 15.4 %collective-permute-start.7 = (bf16[1,96,3072]{2,1,0:T(8,128)(2,1)S(1)}, bf16[1,96,3072]{2,1,0:T(8,128)(2,1)S(1)}, u32[]{:S(2)}, u32[]{:S(2)}) collective-permute-start(bf16[1,96,3072]{2,1,0:T(8,128)(2,1)S(1)} %get-tuple-element.44), channel_id=1, source_target_pairs={{0,16},{8,24},{16,0},{24,8},{1,17},{9,25},{17,1},{25,9},{2,18},{10... | collective-permute-start | bytes 1769480 | tf_op jit(solution)/shard_map/ppermute | solution.py:61
  13.8 15.5 %collective-permute-start.4 = (bf16[1,96,3072]{2,1,0:T(8,128)(2,1)S(1)}, bf16[1,96,3072]{2,1,0:T(8,128)(2,1)S(1)}, u32[]{:S(2)}, u32[]{:S(2)}) collective-permute-start(bf16[1,96,3072]{2,1,0:T(8,128)(2,1)S(1)} %get-tuple-element.45), channel_id=1, source_target_pairs={{0,8},{8,0},{16,24},{24,16},{1,9},{9,1},{17,25},{25,17},{2,10},{10... | collective-permute-start | bytes 1769480 | tf_op jit(solution)/shard_map/ppermute | solution.py:61
  27.7 27.2 %collective-permute-start.8 = (bf16[2,96,3072]{2,1,0:T(8,128)(2,1)S(1)}, bf16[2,96,3072]{2,1,0:T(8,128)(2,1)S(1)}, u32[]{:S(2)}, u32[]{:S(2)}) collective-permute-start(bf16[2,96,3072]{2,1,0:T(8,128)(2,1)S(1)} %pad_maximum_fusion.3), channel_id=1, source_target_pairs={{0,8},{8,0},{16,24},{24,16},{1,9},{9,1},{17,25},{25,17},{2,10},{10... | collective-permute-start | bytes 3538952 | tf_op jit(solution)/shard_map/ppermute | solution.py:61
  29.4 26.9 %collective-permute-start.5 = (bf16[2,96,3072]{2,1,0:T(8,128)(2,1)S(1)}, bf16[2,96,3072]{2,1,0:T(8,128)(2,1)S(1)}, u32[]{:S(2)}, u32[]{:S(2)}) collective-permute-start(bf16[2,96,3072]{2,1,0:T(8,128)(2,1)S(1)} %pad_maximum_fusion.2), channel_id=1, source_target_pairs={{0,16},{8,24},{16,0},{24,8},{1,17},{9,25},{17,1},{25,9},{2,18},{10... | collective-permute-start | bytes 3538952 | tf_op jit(solution)/shard_map/ppermute | solution.py:61
  55.2 34.2 %collective-permute-start.9 = (bf16[4,96,3072]{2,1,0:T(8,128)(2,1)S(1)}, bf16[4,96,3072]{2,1,0:T(8,128)(2,1)}, u32[]{:S(2)}, u32[]{:S(2)}) collective-permute-start(bf16[4,96,3072]{2,1,0:T(8,128)(2,1)S(1)} %pad_maximum_fusion.1.b), channel_id=1, source_target_pairs={{0,1},{1,0},{2,3},{3,2},{4,5},{5,4},{6,7},{7,6},{8,9},{9,8},{10,11... | collective-permute-start | bytes 7077896 | tf_op jit(solution)/shard_map/ppermute | solution.py:77
  58.0 31.4 %collective-permute-start.6 = (bf16[4,96,3072]{2,1,0:T(8,128)(2,1)}, bf16[4,96,3072]{2,1,0:T(8,128)(2,1)}, u32[]{:S(2)}, u32[]{:S(2)}) collective-permute-start(bf16[4,96,3072]{2,1,0:T(8,128)(2,1)} %pad_maximum_fusion.a), channel_id=1, source_target_pairs={{0,1},{1,0},{2,3},{3,2},{4,5},{5,4},{6,7},{7,6},{8,9},{9,8},{10,11... | collective-permute-start | bytes 7077896 | tf_op jit(solution)/shard_map/ppermute | solution.py:76
  64.2 16.1 %collective-permute-start.2 = (s32[2,2,4]{2,1,0:T(2,128)S(1)}, s32[2,2,4]{2,1,0:T(2,128)S(1)}, u32[]{:S(2)}, u32[]{:S(2)}) collective-permute-start(s32[2,2,4]{2,1,0:T(2,128)S(1)} %pad_add_fusion), channel_id=1, source_target_pairs={{0,4},{1,5},{2,6},{3,7},{4,0},{5,1},{6,2},{7,3},{8,12},{9,13},{10,... | collective-permute-start | bytes 200 | tf_op jit(solution)/shard_map/ppermute | solution.py:477
  66.2 16.1 %collective-permute-start.3 = (s32[2,2,4]{2,1,0:T(2,128)S(1)}, s32[2,2,4]{2,1,0:T(2,128)S(1)}, u32[]{:S(2)}, u32[]{:S(2)}) collective-permute-start(s32[2,2,4]{2,1,0:T(2,128)S(1)} %pad_add_fusion), channel_id=1, source_target_pairs={{0,6},{1,7},{2,4},{3,5},{4,2},{5,3},{6,0},{7,1},{8,14},{9,15},{10,... | collective-permute-start | bytes 200 | tf_op jit(solution)/shard_map/ppermute | solution.py:477
  127.0 14.7 %collective-permute-start.12 = (bf16[16,1536]{1,0:T(8,128)(2,1)S(1)}, bf16[16,1536]{1,0:T(8,128)(2,1)S(1)}, u32[]{:S(2)}, u32[]{:S(2)}) collective-permute-start(bf16[16,1536]{1,0:T(8,128)(2,1)S(1)} %get-tuple-element.47), channel_id=1, source_target_pairs={{0,1},{1,2},{2,3},{3,4},{4,5},{5,6},{6,7},{8,9},{9,10},{10,11},{11... | collective-permute-start | bytes 147464 | tf_op jit(solution)/shard_map/ppermute | solution.py:452
  129.5 12.2 %collective-permute-start.13 = (bf16[16,1536]{1,0:T(8,128)(2,1)S(1)}, bf16[16,1536]{1,0:T(8,128)(2,1)S(1)}, u32[]{:S(2)}, u32[]{:S(2)}) collective-permute-start(bf16[16,1536]{1,0:T(8,128)(2,1)S(1)} %get-tuple-element.46), channel_id=1, source_target_pairs={{1,0},{2,1},{3,2},{4,3},{5,4},{6,5},{7,6},{9,8},{10,9},{11,10},{12... | collective-permute-start | bytes 147464 | tf_op jit(solution)/shard_map/ppermute | solution.py:453
  181.9 16.8 %collective-permute-start.14 = (bf16[512,1536]{1,0:T(8,128)(2,1)}, bf16[512,1536]{1,0:T(8,128)(2,1)}, u32[]{:S(2)}, u32[]{:S(2)}) collective-permute-start(bf16[512,1536]{1,0:T(8,128)(2,1)} %get-tuple-element.26), channel_id=1, source_target_pairs={{0,1},{1,0},{2,3},{3,2},{4,5},{5,4},{6,7},{7,6},{8,9},{9,8},{10,11... | collective-permute-start | bytes 4718600 | tf_op jit(solution)/shard_map/ppermute | solution.py:488
  186.7 9.2 %collective-permute-start.15 = (bf16[512,768]{1,0:T(8,128)(2,1)}, bf16[512,768]{1,0:T(8,128)(2,1)}, u32[]{:S(2)}, u32[]{:S(2)}) collective-permute-start(bf16[512,768]{1,0:T(8,128)(2,1)} %get-tuple-element.22.refs_2_), channel_id=1, source_target_pairs={{0,1},{1,0},{2,3},{3,2},{4,5},{5,4},{6,7},{7,6},{8,9},{9,8},{10,11... | collective-permute-start | bytes 2359304 | tf_op jit(solution)/shard_map/ppermute | solution.py:527
  187.0 8.9 %collective-permute-start.18 = (bf16[512,768]{1,0:T(8,128)(2,1)}, bf16[512,768]{1,0:T(8,128)(2,1)}, u32[]{:S(2)}, u32[]{:S(2)}) collective-permute-start(bf16[512,768]{1,0:T(8,128)(2,1)} %get-tuple-element.23.refs_3_), channel_id=1, source_target_pairs={{0,1},{1,0},{2,3},{3,2},{4,5},{5,4},{6,7},{7,6},{8,9},{9,8},{10,11... | collective-permute-start | bytes 2359304 | tf_op jit(solution)/shard_map/ppermute | solution.py:527
  189.7 112.0 %all-to-all-start.1 = ((bf16[8,128,1536]{2,1,0:T(8,128)(2,1)}), bf16[8,128,1536]{2,1,0:T(8,128)(2,1)S(1)}, u32[]{:S(2)}, u32[]{:S(2)}) async-start(bf16[8,128,1536]{2,1,0:T(8,128)(2,1)} %get-tuple-element.24), calls=%async_computation.1 | async-start | bytes 6291456 | tf_op jit(solution)/shard_map/all_to_all | solution.py:545
  207.5 44.8 %collective-permute-start.16 = (bf16[2,384,768]{1,2,0:T(8,128)(2,1)}, bf16[2,384,768]{1,2,0:T(8,128)(2,1)}, u32[]{:S(2)}, u32[]{:S(2)}) collective-permute-start(bf16[2,384,768]{1,2,0:T(8,128)(2,1)} %bitcast.108), channel_id=1, source_target_pairs={{0,8},{8,0},{16,24},{24,16},{1,9},{9,1},{17,25},{25,17},{2,10},{10... | collective-permute-start | bytes 3538952 | tf_op jit(solution)/shard_map/ppermute | solution.py:408
  217.9 38.0 %collective-permute-start.19 = (bf16[2,384,768]{1,2,0:T(8,128)(2,1)}, bf16[2,384,768]{1,2,0:T(8,128)(2,1)}, u32[]{:S(2)}, u32[]{:S(2)}) collective-permute-start(bf16[2,384,768]{1,2,0:T(8,128)(2,1)} %bitcast.109), channel_id=1, source_target_pairs={{0,16},{8,24},{16,0},{24,8},{1,17},{9,25},{17,1},{25,9},{2,18},{10... | collective-permute-start | bytes 3538952 | tf_op jit(solution)/shard_map/ppermute | solution.py:408
  219.5 27.5 %collective-permute-start.31 = (f32[8,1536]{1,0:T(8,128)S(1)}, f32[8,1536]{1,0:T(8,128)S(1)}, u32[]{:S(2)}, u32[]{:S(2)}) collective-permute-start(f32[8,1536]{1,0:T(8,128)S(1)} %pad_maximum_fusion.8), channel_id=1, source_target_pairs={{0,16},{8,24},{16,0},{24,8},{1,17},{9,25},{17,1},{25,9},{2,18},{10... | collective-permute-start | bytes 147464 | tf_op jit(solution)/shard_map/ppermute | solution.py:433
  247.0 12.2 %collective-permute-start.32 = (f32[16,1536]{1,0:T(8,128)S(1)}, f32[16,1536]{1,0:T(8,128)S(1)}, u32[]{:S(2)}, u32[]{:S(2)}) collective-permute-start(f32[16,1536]{1,0:T(8,128)S(1)} %pad_maximum_fusion.7), channel_id=1, source_target_pairs={{0,8},{8,0},{16,24},{24,16},{1,9},{9,1},{17,25},{25,17},{2,10},{10... | collective-permute-start | bytes 294920 | tf_op jit(solution)/shard_map/ppermute | solution.py:433
  254.4 14.1 %collective-permute-start.17 = (bf16[384,768]{0,1:T(8,128)(2,1)S(1)}, bf16[384,768]{0,1:T(8,128)(2,1)S(1)}, u32[]{:S(2)}, u32[]{:S(2)}) collective-permute-start(bf16[384,768]{0,1:T(8,128)(2,1)S(1)} %dynamic-slice_bitcast_fusion.3), channel_id=1, source_target_pairs={{0,16},{8,24},{16,0},{24,8},{1,17},{9,25},{17,1},{25,9},{2,18},{10... | collective-permute-start | bytes 1769480 | tf_op jit(solution)/shard_map/ppermute | solution.py:408
  257.6 13.8 %collective-permute-start.20 = (bf16[384,768]{0,1:T(8,128)(2,1)S(1)}, bf16[384,768]{0,1:T(8,128)(2,1)S(1)}, u32[]{:S(2)}, u32[]{:S(2)}) collective-permute-start(bf16[384,768]{0,1:T(8,128)(2,1)S(1)} %dynamic-slice_bitcast_fusion.2), channel_id=1, source_target_pairs={{0,8},{8,0},{16,24},{24,16},{1,9},{9,1},{17,25},{25,17},{2,10},{10... | collective-permute-start | bytes 1769480 | tf_op jit(solution)/shard_map/ppermute | solution.py:408
  271.8 10.3 %collective-permute-start.21 = (bf16[384,384]{0,1:T(8,128)(2,1)S(1)}, bf16[384,384]{0,1:T(8,128)(2,1)S(1)}, u32[]{:S(2)}, u32[]{:S(2)}) collective-permute-start(bf16[384,384]{0,1:T(8,128)(2,1)S(1)} %get-tuple-element.50), channel_id=1, source_target_pairs={{0,2},{1,3},{2,0},{3,1},{4,6},{5,7},{6,4},{7,5},{8,10},{9,11},{10,... | collective-permute-start | bytes 884744 | tf_op jit(solution)/shard_map/ppermute | solution.py:446
  272.8 21.2 %collective-permute-start.22 = (bf16[384,384]{0,1:T(8,128)(2,1)S(1)}, bf16[384,384]{0,1:T(8,128)(2,1)S(1)}, u32[]{:S(2)}, u32[]{:S(2)}) collective-permute-start(bf16[384,384]{0,1:T(8,128)(2,1)S(1)} %get-tuple-element.52), channel_id=1, source_target_pairs={{0,4},{1,5},{2,6},{3,7},{4,0},{5,1},{6,2},{7,3},{8,12},{9,13},{10,... | collective-permute-start | bytes 884744 | tf_op jit(solution)/shard_map/ppermute | solution.py:446
  274.8 23.8 %collective-permute-start.23 = (bf16[384,384]{0,1:T(8,128)(2,1)S(1)}, bf16[384,384]{0,1:T(8,128)(2,1)S(1)}, u32[]{:S(2)}, u32[]{:S(2)}) collective-permute-start(bf16[384,384]{0,1:T(8,128)(2,1)S(1)} %get-tuple-element.51), channel_id=1, source_target_pairs={{0,6},{1,7},{2,4},{3,5},{4,2},{5,3},{6,0},{7,1},{8,14},{9,15},{10,... | collective-permute-start | bytes 884744 | tf_op jit(solution)/shard_map/ppermute | solution.py:446
  (25 other events, 148.0 us)

commit v2 on v1

--- a/solution.py
+++ b/solution.py
@@ -34,19 +34,27 @@
     return list(range(bits))
 
 
-def copy_body(_, source, target):
-    target[...] = source[...]
+def pick_body(index, source, target, sems, *, count):
+    copies = [
+        pltpu.make_async_copy(source.at[index[i]], target.at[i], sems.at[i]) for i in range(count)
+    ]
+    for copy in copies:
+        copy.start()
+    for copy in copies:
+        copy.wait()
 
 
 def pick_panels(source, index, count):
     _, rows, width = source.shape
+    hbm = pl.BlockSpec(memory_space=pl.ANY)
     return pl.pallas_call(
-        copy_body,
+        functools.partial(pick_body, count=count),
         grid_spec=pltpu.PrefetchScalarGridSpec(
             num_scalar_prefetch=1,
-            grid=(count,),
-            in_specs=[pl.BlockSpec((1, rows, width), lambda i, idx: (idx[i], 0, 0))],
-            out_specs=pl.BlockSpec((1, rows, width), lambda i, idx: (i, 0, 0)),
+            grid=(1,),
+            in_specs=[hbm],
+            out_specs=hbm,
+            scratch_shapes=[pltpu.SemaphoreType.DMA((count,))],
         ),
         out_shape=jax.ShapeDtypeStruct((count, rows, width), source.dtype),
         compiler_params=params(1),
@@ -122,7 +130,7 @@
     return full.reshape(4 * quarter * count, width)
 
 
-def forward_body(source, x_hbm, gain_ref, lin_w, gate_w, normed, pair, lin_out, gate_out, glu_out, xs, sems, *, panels):
+def forward_body(source, x_hbm, gain_ref, lin_w, gate_w, parts, lin_out, gate_out, glu_out, normed, xs, sems, *, panels):
     rows = xs.shape[1]
 
     def fetch(s):
@@ -140,7 +148,9 @@
             scale = lax.rsqrt(jnp.mean(x * x, axis=1, keepdims=True) + 1e-05)
             normed[s * rows : (s + 1) * rows, :] = (x * scale * gain_ref[...]).astype(BF)
 
-        pair[...] = normed[...]
+        count, _, shard = parts.shape
+        for block in range(count):
+            parts[block ^ source[panels]] = normed[:, block * shard : (block + 1) * shard]
 
     lin = jnp.dot(normed[...], lin_w[...], preferred_element_type=F32)
     lin_out[...] = lin
@@ -153,8 +163,9 @@
     _, rows, width = arrived.shape
     blocks = width // block
     column = pl.BlockSpec((panels * rows, block), lambda j, idx: (0, j))
-    whole = pl.BlockSpec((panels * rows, width), lambda j, idx: (0, 0))
-    wide = lambda dtype, times=1: jax.ShapeDtypeStruct((times * panels * rows, width), dtype)
+    wide = lambda dtype: jax.ShapeDtypeStruct((panels * rows, width), dtype)
+    count = lax.axis_size("dp")
+    parts = jax.ShapeDtypeStruct((count, panels * rows, width // count), BF)
     return pl.pallas_call(
         functools.partial(forward_body, panels=panels),
         grid_spec=pltpu.PrefetchScalarGridSpec(
@@ -167,29 +178,29 @@
                 pl.BlockSpec((width, block), lambda j, idx: (0, blocks + j)),
             ],
             out_specs=[
-                whole,
-                whole,
+                pl.BlockSpec(parts.shape, lambda j, idx: (0, 0, 0)),
                 column,
                 column,
                 column,
             ],
             scratch_shapes=[
+                pltpu.VMEM((panels * rows, width), BF),
                 pltpu.VMEM((panels, rows, width), BF),
                 pltpu.SemaphoreType.DMA((panels,)),
             ],
         ),
-        out_shape=[wide(BF), wide(BF, 2), wide(F32), wide(F32), wide(BF)],
+        out_shape=[parts, wide(F32), wide(F32), wide(BF)],
         compiler_params=params(1),
         name="forward",
-    )(source, arrived, gain.reshape(1, width), full_in, full_in)
+    )(jnp.append(source, lax.axis_index("dp")), arrived, gain.reshape(1, width), full_in, full_in)
 
 
 def fill_padded(flags, padded, main, low, high, panels, length):
     for s in range(panels):
         at = s * length
         middle = main[at : at + length, :].astype(F32)
-        before = low[...] if s == 0 else main[at - RIM : at, :]
-        after = high[...] if s == panels - 1 else main[at + length : at + length + RIM, :]
+        before = low[low.shape[0] - RIM :, :] if s == 0 else main[at - RIM : at, :]
+        after = high[:RIM, :] if s == panels - 1 else main[at + length : at + length + RIM, :]
         before = jnp.where(flags[s] > 0, before.astype(F32), 0.0)
         after = jnp.where(flags[panels + s] > 0, after.astype(F32), 0.0)
         for chunk in range(main.shape[1] // LANES):
@@ -199,12 +210,12 @@
             padded[chunk, s, RIM + length :, :] = after[:, lanes]
 
 
-def shifted_sum(padded, weights, chunk, s, start, taps, flip):
+def shifted_sum(padded, weights, chunk, s, start, taps, flip, height=TILE):
     lanes = pl.ds(chunk * LANES, LANES)
-    total = jnp.zeros((TILE, LANES), F32)
+    total = jnp.zeros((height, LANES), F32)
     for tap in range(taps):
         offset = taps - tap if flip else tap + 1
-        view = padded[chunk, s, pl.ds(start + offset, TILE), :]
+        view = padded[chunk, s, pl.ds(start + offset, height), :]
         total = total + weights[pl.ds(tap, 1), lanes] * view
     return total
 
@@ -221,14 +232,29 @@
         lax.fori_loop(0, panels, step, 0)
 
 
-def depth_body(flags, glu, low, high, upstream, weights, out, padded, *, panels, length, taps):
+def depth_body(
+    flags, glu, low, high, upstream, up_low, up_high, weights, out, out_low, out_high, padded, ends, *, panels, length, taps
+):
     fill_padded(flags, padded, glu, low, high, panels, length)
-
-    def work(chunk, s, start, rows, lanes):
+    rows = panels * length
+
+    def grad(depth, up):
+        sig = jax.nn.sigmoid(depth)
+        return (up.astype(F32) * sig * (1.0 + depth * (1.0 - sig))).astype(BF)
+
+    for chunk in range(glu.shape[1] // LANES):
+        lanes = slice(chunk * LANES, (chunk + 1) * LANES)
+        ends[chunk, 0, 0 : 2 * RIM, :] = low[:, lanes].astype(F32)
+        ends[chunk, 0, 2 * RIM :, :] = glu[0:RIM, lanes].astype(F32)
+        ends[chunk, 1, 0:RIM, :] = glu[rows - RIM : rows, lanes].astype(F32)
+        ends[chunk, 1, RIM:, :] = high[:, lanes].astype(F32)
+        for side, up, to in ((0, up_low, out_low), (1, up_high, out_high)):
+            depth = shifted_sum(ends, weights, chunk, side, 0, taps, False, RIM)
+            to[:, lanes] = grad(depth, up[:, lanes])
+
+    def work(chunk, s, start, at, lanes):
         depth = shifted_sum(padded, weights, chunk, s, start, taps, False)
-        sig = jax.nn.sigmoid(depth)
-        up = upstream[rows, lanes].astype(F32)
-        out[rows, lanes] = (up * sig * (1.0 + depth * (1.0 - sig))).astype(BF)
+        out[at, lanes] = grad(depth, upstream[at, lanes])
 
     tiles(glu.shape[1], panels, length, work)
 
@@ -259,19 +285,17 @@
         total = shifted_sum(padded, weights, chunk, s, start, taps, True)
         sig = jax.nn.sigmoid(gate[rows, lanes])
         scaled = total * sig
-        results = (scaled.astype(BF), (scaled * lin[rows, lanes] * (1.0 - sig)).astype(BF))
-        for number, out in enumerate(outs):
-            out[rows, lanes] = results[number % 2]
+        outs[0][rows, lanes] = scaled.astype(BF)
+        outs[1][rows, lanes] = (scaled * lin[rows, lanes] * (1.0 - sig)).astype(BF)
 
     tiles(grad.shape[1], panels, length, work)
 
 
-def gated(flags, grad_depth, low, high, lin, gate, kernel, block, parities, parity, sizes, twice=False):
+def gated(flags, grad_depth, low, high, lin, gate, kernel, block, parities, parity, sizes):
     rows, width = grad_depth.shape
     panels = sizes["panels"]
     column = lambda height: pl.BlockSpec((height, block), lambda j, idx: (0, j * parities + idx[2 * panels]))
-    shapes = [jax.ShapeDtypeStruct((rows * times, width // parities), BF) for times in (1, 1, 2, 2)]
-    shapes = shapes[: 4 if twice else 2]
+    shapes = [jax.ShapeDtypeStruct((rows, width // parities), BF)] * 2
     return pl.pallas_call(
         functools.partial(gated_body, **sizes),
         grid_spec=pltpu.PrefetchScalarGridSpec(
@@ -387,28 +411,32 @@
     )(jnp.append(source, core), *gradients, full_in, arrived, upstream, gain.reshape(1, width))
 
 
-def outer_sum(left, right):
-    return lax.dot_general(
-        left, right, (((0,), (0,)), ((), ())), preferred_element_type=F32
-    ).astype(BF)
-
-
-def halve(block, order):
-    place = lax.axis_index("dp")
-    count = lax.axis_size("dp")
-    bits = len(bits_of(count))
-    shape = block.shape[1:]
-    block = block.reshape((2,) * bits + shape)
-    live = list(reversed(range(bits)))
+def outer_sum(lefts, rights):
+    terms = [
+        lax.dot_general(a, b, (((1,), (0,)), ((), ())), preferred_element_type=F32)
+        for a, b in zip(lefts, rights)
+    ]
+    return (terms[0] + terms[1]).astype(BF)
+
+
+def outer_halved(lefts, rights, order):
+    count = lefts[0].shape[0]
+    rels = sorted(range(count), key=lambda r: [(r >> bit) & 1 for bit in order])
+    if rels != list(range(count)):
+        lefts = [jnp.concatenate([left[r : r + 1] for r in rels]) for left in lefts]
+    half = count // 2
+    send = outer_sum([left[half:] for left in lefts], rights)
+    keep = outer_sum([left[:half] for left in lefts], rights)
     for bit in order:
-        dim = live.index(bit)
-        mine = (place >> bit) & 1
-        keep = lax.dynamic_index_in_dim(block, mine, dim, keepdims=False)
-        send = lax.dynamic_index_in_dim(block, 1 - mine, dim, keepdims=False)
         got = lax.ppermute(send, "dp", flip_bit("dp", bit))
-        block = (keep.astype(F32) + got.astype(F32)).astype(BF)
-        live.remove(bit)
-    return block
+        half = half // 2
+        add = lambda a, b: (a.astype(F32) + b.astype(F32)).astype(BF)
+        if half:
+            send = add(keep[half:], got[half:])
+            keep = add(keep[:half], got[:half])
+        else:
+            keep = add(keep, got)
+    return keep[0]
 
 
 def sum_everywhere(values):
@@ -484,34 +512,38 @@
     flags = jnp.concatenate([line[1:-1] == line[:-2], line[1:-1] == line[2:]]).astype(jnp.int32)
 
     full_in = gather_weights(w_in, core)
-    normed, both_normed, lin, gate, glu = forward(arrived, source, gain, full_in, panels, 2 * LANES)
+    normed, lin, gate, glu = forward(arrived, source, gain, full_in, panels, 4 * LANES)
     other_normed = lax.ppermute(normed, "tm", flip_bit("tm", 0))
-    glu_low, glu_high = edges(glu, RIM)
+    glu_low, glu_high = edges(glu, 2 * RIM)
 
     lane_block = 2 * LANES
     column = lambda height: pl.BlockSpec((height, lane_block), lambda j, idx: (0, j))
     sizes = dict(panels=panels, length=length, taps=taps)
     padded_of = lambda lanes: pltpu.VMEM((lanes // LANES, panels, length + 2 * RIM, LANES), F32)
-    grad_depth = pl.pallas_call(
+    up_rows = upstream.reshape(rows, width)
+    up_low, up_high = edges(up_rows, RIM)
+    grad_depth, grad_low, grad_high = pl.pallas_call(
         functools.partial(depth_body, **sizes),
         grid_spec=pltpu.PrefetchScalarGridSpec(
             num_scalar_prefetch=1,
             grid=(width // lane_block,),
-            in_specs=[column(rows), column(RIM), column(RIM), column(rows), column(taps)],
-            out_specs=column(rows),
-            scratch_shapes=[padded_of(lane_block)],
+            in_specs=[column(h) for h in (rows, 2 * RIM, 2 * RIM, rows, RIM, RIM, taps)],
+            out_specs=[column(rows), column(RIM), column(RIM)],
+            scratch_shapes=[
+                padded_of(lane_block),
+                pltpu.VMEM((lane_block // LANES, 2, 3 * RIM, LANES), F32),
+            ],
         ),
-        out_shape=jax.ShapeDtypeStruct((rows, width), BF),
+        out_shape=[jax.ShapeDtypeStruct((h, width), BF) for h in (rows, RIM, RIM)],
         compiler_params=params(1),
         name="depth",
-    )(flags, glu, glu_low, glu_high, upstream.reshape(rows, width), kernel)
-    grad_low, grad_high = edges(grad_depth, RIM)
+    )(flags, glu, glu_low, glu_high, up_rows, up_low, up_high, kernel)
     kernel_term = pl.pallas_call(
         functools.partial(taps_body, **sizes),
         grid_spec=pltpu.PrefetchScalarGridSpec(
             num_scalar_prefetch=1,
             grid=(width // lane_block,),
-            in_specs=[column(rows), column(RIM), column(RIM), column(rows)],
+            in_specs=[column(h) for h in (rows, 2 * RIM, 2 * RIM, rows)],
             out_specs=column(taps + 1),
             scratch_shapes=[padded_of(lane_block), pltpu.VMEM((taps + 1, 8, LANES), F32)],
         ),
@@ -525,10 +557,8 @@
     if piece % LANES == 0:
         give = gated(*arguments, piece, 2, 1 - core, sizes)
         others = [lax.ppermute(g, "tm", flip_bit("tm", 0)) for g in give]
-        *own, first, second = gated(*arguments, piece, 2, core, sizes, True)
+        own = gated(*arguments, piece, 2, core, sizes)
         gradients, run = (*own, *give), piece
-        join = lambda base, other: lax.dynamic_update_slice(base, other, (rows, 0))
-        mine = (first, second)
     else:
         gradients, run = tuple(gated(*arguments, lane_block, 1, 0, sizes)), width
         pick_parity = lambda values, parity: lax.dynamic_index_in_dim(
@@ -536,19 +566,17 @@
         ).reshape(rows, width // 2)
         give = [pick_parity(g, 1 - core) for g in gradients]
         others = [lax.ppermute(g, "tm", flip_bit("tm", 0)) for g in give]
-        mine = [pick_parity(g, core) for g in gradients]
-        join = lambda base, other: jnp.concatenate([base, other], axis=0)
-    both_normed = lax.dynamic_update_slice(both_normed, other_normed, (rows, 0))
+        own = [pick_parity(g, core) for g in gradients]
     grad_slots, gain_term = back(
         gradients, core, full_in, arrived, source, upstream, gain, run, 2 * LANES
     )
     returned = lax.all_to_all(grad_slots, "tm", split_axis=0, concat_axis=0, tiled=True)
     count = lax.axis_size("dp")
     bits = bits_of(count)
-    shares = []
-    for side, order in ((0, bits), (1, bits[::-1])):
-        term = outer_sum(both_normed, join(mine[side], others[side]))
-        shares.append(halve(term.reshape(count, width // count, -1), order))
+    shares = [
+        outer_halved((normed, other_normed), (own[side], others[side]), order)
+        for side, order in ((0, bits), (1, bits[::-1]))
+    ]
     share = jnp.concatenate(shares, axis=1)
     share = share.reshape(width // count, owners // 2, piece).transpose(1, 0, 2)
     shard_in = sum_across(share)

time: 305 us -> 290 us (0.951)
  waiting for transfers between devices: 129 us -> 118 us
  local copies, waits for them, and re-layouts: 23.4 us -> 14 us
  matrix products: 7.98 us -> 13.4 us
  Pallas kernels: 81.4 us -> 78.3 us
    ppermute x3, waiting for transfers between devices: 26.9 us -> 1.89 us  [sum_everywhere(): got = lax.ppermute(values, axis, flip_bit(axis, bit))]
    ppermute x4, waiting for transfers between devices: 12.1 us -> 31.3 us  [outer_halved(): got = lax.ppermute(send, 'dp', flip_bit('dp', bit))]
    dynamic_slice x4 -> x0, local copies, waits for them, and re-layouts: 7.9 us -> none  [the longest x2 4.76 us: halve(): send = lax.dynamic_index_in_dim(block, 1 - mine, dim, keepdims=False)]
    unnamed x34 -> x36, local copies, waits for them, and re-layouts: 9.72 us -> 2.83 us
    dot_general x2 -> x8, matrix products: 7.98 us -> 13.4 us  [outer_sum(): lax.dot_general(a, b, (((1,), (0,)), ((), ())), preferred_element_type=F32)]
    concatenate x0 -> x3, local copies, waits for them, and re-layouts: none -> 5.13 us  [local(): share = jnp.concatenate(shares, axis=1)]
    ppermute x1, waiting for transfers between devices: 4.47 us -> 0.01 us  [local(): tags = jnp.concatenate([tags, lax.ppermute(tags, 'tm', flip_bit('tm', 0))])]
    dynamic_update_slice x2 -> x0, local copies, waits for them, and re-layouts: 4.4 us -> none  [the longest x1 2.77 us: local(): join = lambda base, other: lax.dynamic_update_slice(base, other, (rows, 0))]
  transfers between devices with their start and end apart: 35 -> 35, of which waited for: 20 -> 18; matrix products, arithmetic and copies ran while one was open for 12% -> 13% of each run, Pallas kernels for 8% -> 9%
where the time goes in v2:
time: 290 us; the launch traced here: 289 us
  waiting for transfers between devices  118 us (41%)
  Pallas kernels  78.3 us (27%)
  starting transfers between devices  52.7 us (18%)
  local copies, waits for them, and re-layouts  14 us (5%)
  matrix products  13.4 us (5%)
  other arithmetic  11.6 us (4%)
    ppermute x4, waiting for transfers between devices, gather_order(): got = lax.ppermute(have, 'dp', flip_bit('dp', bit))  37.2 us
    ppermute x4, waiting for transfers between devices, outer_halved(): got = lax.ppermute(send, 'dp', flip_bit('dp', bit))  31.3 us
    ppermute x3, waiting for transfers between devices, sum_across(): total = total + lax.ppermute(piece, 'tm', pairs).astype(F32)  23.7 us
    pallas_call x2, Pallas kernels, gated(): pl.pallas_call(functools.partial(gated_body, **sizes), grid_spec=pltpu.Pr...  14.8 us
    ppermute x3, waiting for transfers between devices, local(): lax.ppermute(tags, 'tm', flip('tm', i))  14.5 us
    pallas_call x2, Pallas kernels, put(): pl.pallas_call(body, grid_spec=pltpu.PrefetchScalarGridSpec(num_scalar_pr...  14.3 us
    pallas_call x1, Pallas kernels, back(): pl.pallas_call(functools.partial(back_body, grads=len(gradients), block=b...  14.3 us
    dot_general x8, matrix products, outer_sum(): lax.dot_general(a, b, (((1,), (0,)), ((), ())), preferred_element_type=F32)  13.4 us
  transfers between devices with their start and end apart: 35, of which 18 were waited for; matrix products, arithmetic and copies ran while one was open for 13% of the time, Pallas kernels for 9%

profile of v2, /device:TPU:8, one launch (start us, length us, event | category | flops | bytes accessed | tf_op | source)
XLA Modules:
  0.0 289.3 jit_solution(12365313084889578459)
XLA Ops:
  5.1 5.5 %all-to-all-start = ((bf16[8,128,1536]{2,1,0:T(8,128)(2,1)}), bf16[8,128,1536]{2,1,0:T(8,128)(2,1)}, u32[]{:S(2)}, u32[]{:S(2)}) async-start(bf16[8,128,1536]{2,1,0:T(8,128)(2,1)} %pick_panels.2), calls=%async_computation | async-start | bytes 6291456 | tf_op jit(solution)/shard_map/all_to_all | solution.py:501
  13.7 12.3 %collective-permute-done.7 = bf16[1,96,3072]{2,1,0:T(8,128)(2,1)S(1)} collective-permute-done((bf16[1,96,3072]{2,1,0:T(8,128)(2,1)S(1)}, bf16[1,96,3072]{2,1,0:T(8,128)(2,1)S(1)}, u32[]{:S(2)}, u32[]{:S(2)}) %collective-permute-start.7) | collective-permute-done | bytes 589856 | tf_op jit(solution)/shard_map/ppermute | solution.py:69
  29.5 23.8 %collective-permute-done.8 = bf16[2,96,3072]{2,1,0:T(8,128)(2,1)S(1)} collective-permute-done((bf16[2,96,3072]{2,1,0:T(8,128)(2,1)S(1)}, bf16[2,96,3072]{2,1,0:T(8,128)(2,1)S(1)}, u32[]{:S(2)}, u32[]{:S(2)}) %collective-permute-start.8) | collective-permute-done | bytes 1179680 | tf_op jit(solution)/shard_map/ppermute | solution.py:69
  59.7 3.1 %collective-permute-start.13 = (bf16[16,1536]{1,0:T(8,128)(2,1)S(1)}, bf16[16,1536]{1,0:T(8,128)(2,1)S(1)}, u32[]{:S(2)}, u32[]{:S(2)}) collective-permute-start(bf16[16,1536]{1,0:T(8,128)(2,1)S(1)} %get-tuple-element.42), channel_id=1, source_target_pairs={{1,0},{2,1},{3,2},{4,3},{5,4},{6,5},{7,6},{9,8},{10,9},{11,10},{12... | collective-permute-start | bytes 147464 | tf_op jit(solution)/shard_map/ppermute | solution.py:481
  63.3 3.6 %collective-permute-done.1 = s32[2,2,4]{2,1,0:T(2,128)S(1)} collective-permute-done((s32[2,2,4]{2,1,0:T(2,128)S(1)}, s32[2,2,4]{2,1,0:T(2,128)S(1)}, u32[]{:S(2)}, u32[]{:S(2)}) %collective-permute-start.1) | collective-permute-done | bytes 96 | tf_op jit(solution)/shard_map/ppermute | solution.py:505
  69.3 9.4 %collective-permute-done.2 = s32[2,2,4]{2,1,0:T(2,128)S(1)} collective-permute-done((s32[2,2,4]{2,1,0:T(2,128)S(1)}, s32[2,2,4]{2,1,0:T(2,128)S(1)}, u32[]{:S(2)}, u32[]{:S(2)}) %collective-permute-start.2) | collective-permute-done | bytes 96 | tf_op jit(solution)/shard_map/ppermute | solution.py:505
  83.2 6.3 %put_weights.2.rest_0_ = bf16[16,96,3072]{2,1,0:T(8,128)(2,1)} custom-call(s32[8]{0:T(128)S(1)} %stack.76._, bf16[4,96,3072]{2,1,0:T(8,128)(2,1)} %pad_maximum_fusion.a, bf16[4,96,3072]{2,1,0:T(8,128)(2,1)S(1)} %pad_maximum_fusion.1.b), custom_call_target="tpu_custom_call" | custom-call | tf_op jit(solution)/shard_map/put_weights/pallas_call | solution.py:111
  89.5 8.0 %put_weights.3 = bf16[16,96,3072]{2,1,0:T(8,128)(2,1)} custom-call(s32[8]{0:T(128)S(1)} %stack.67._, bf16[4,96,3072]{2,1,0:T(8,128)(2,1)} %collective-permute-done.6.a, bf16[4,96,3072]{2,1,0:T(8,128)(2,1)} %collective-permute-done.9.b, bf16[16,96,3072]{2,1,0:T(8,128)(2,1)} %put_weights.2.rest_0_), custom_call_target="tpu_custom_call", output_to_operand_aliasing={{}: (3, {})} | custom-call | tf_op jit(solution)/shard_map/put_weights/pallas_call | solution.py:111
  97.5 12.4 %forward.1 = (bf16[4,512,384]{2,1,0:T(8,128)(2,1)}, f32[512,1536]{1,0:T(8,128)}, f32[512,1536]{1,0:T(8,128)}, bf16[512,1536]{1,0:T(8,128)(2,1)S(1)}) custom-call(s32[5]{0:T(128)S(1)} %get-tuple-element.59.source, bf16[8,128,1536]{2,1,0:T(8,128)(2,1)} %all-to-all-done.x_hbm.refs_5_, f32[1,1536]{1,0:T(1,128)S(1)} %reshape.103.gain_ref.refs_7_, ...), custom_call_target="tpu_custom_call" | custom-call | tf_op jit(solution)/shard_map/forward/pallas_call | solution.py:169
  111.9 5.4 %collective-permute-start.11 = (bf16[32,1536]{1,0:T(8,128)(2,1)S(1)}, bf16[32,1536]{1,0:T(8,128)(2,1)S(1)}, u32[]{:S(2)}, u32[]{:S(2)}) collective-permute-start(bf16[32,1536]{1,0:T(8,128)(2,1)S(1)} %get-tuple-element.44), channel_id=1, source_target_pairs={{1,0},{2,1},{3,2},{4,3},{5,4},{6,5},{7,6},{9,8},{10,9},{11,10},{12... | collective-permute-start | bytes 294920 | tf_op jit(solution)/shard_map/ppermute | solution.py:481
  119.3 9.7 %depth.1 = (bf16[512,1536]{1,0:T(8,128)(2,1)S(1)}, bf16[16,1536]{1,0:T(8,128)(2,1)S(1)}, bf16[16,1536]{1,0:T(8,128)(2,1)S(1)}) custom-call(s32[8]{0:T(128)S(1)} %add_convert_fusion.10.flags, bf16[512,1536]{1,0:T(8,128)(2,1)S(1)} %get-tuple-element.17.glu, bf16[32,1536]{1,0:T(8,128)(2,1)S(1)} %collective-permute-done.10.low, ...), custom_call_target="tpu_custom_call" | custom-call | tf_op jit(solution)/shard_map/depth/pallas_call | solution.py:525
  129.0 7.7 %gated.3 = (bf16[512,768]{1,0:T(8,128)(2,1)S(1)}, bf16[512,768]{1,0:T(8,128)(2,1)}) custom-call(s32[9]{0:T(128)S(1)} %get-tuple-element.57.flags, bf16[512,1536]{1,0:T(8,128)(2,1)S(1)} %get-tuple-element.18.grad, bf16[16,1536]{1,0:T(8,128)(2,1)S(1)} %get-tuple-element.19.low, bf16[16,1536]{1,0:T(8,128)(2,1)S(1)} %get-tuple-element.20.high, ...), custom_call_target="tpu_custom_call" | custom-call | tf_op jit(solution)/shard_map/gated/pallas_call | solution.py:299
  136.7 7.0 %gated.2 = (bf16[512,768]{1,0:T(8,128)(2,1)S(1)}, bf16[512,768]{1,0:T(8,128)(2,1)S(1)}) custom-call(s32[9]{0:T(128)S(1)} %get-tuple-element.58.flags, bf16[512,1536]{1,0:T(8,128)(2,1)S(1)} %get-tuple-element.18.grad, bf16[16,1536]{1,0:T(8,128)(2,1)S(1)} %get-tuple-element.19.low, bf16[16,1536]{1,0:T(8,128)(2,1)S(1)} %get-tuple-element.20.high, ...), custom_call_target="tpu_custom_call" | custom-call | tf_op jit(solution)/shard_map/gated/pallas_call | solution.py:299
  143.8 8.8 %taps.1 = f32[32,1536]{1,0:T(8,128)S(1)} custom-call(s32[8]{0:T(128)S(1)} %add_convert_fusion.10.flags, bf16[512,1536]{1,0:T(8,128)(2,1)S(1)} %get-tuple-element.17.glu, bf16[32,1536]{1,0:T(8,128)(2,1)S(1)} %collective-permute-done.10.low, bf16[32,1536]{1,0:T(8,128)(2,1)S(1)} %collective-permute-done.11.high, bf16[512,1536]{1,0:T(8,128)(2,1)S(1)} %get-tuple-element.18.grad), custom_call_target="tpu_custom_call" | custom-call | tf_op jit(solution)/shard_map/taps/pallas_call | solution.py:541
  152.6 14.3 %back.1 = (bf16[8,128,1536]{2,1,0:T(8,128)(2,1)}, f32[1,1536]{1,0:T(1,128)S(1)}) custom-call(s32[5]{0:T(128)S(1)} %get-tuple-element.60.source, bf16[512,768]{1,0:T(8,128)(2,1)S(1)} %get-tuple-element.23.refs_0_, bf16[512,768]{1,0:T(8,128)(2,1)S(1)} %get-tuple-element.24.refs_1_, bf16[512,768]{1,0:T(8,128)(2,1)S(1)} %get-tuple-element.25.refs_2_, ...), custom_call_target="tpu_custom_call" | custom-call | tf_op jit(solution)/shard_map/back/pallas_call | solution.py:384
  168.5 3.9 %collective-permute-done.24 = f32[16,1536]{1,0:T(8,128)S(1)} collective-permute-done((f32[16,1536]{1,0:T(8,128)S(1)}, f32[16,1536]{1,0:T(8,128)S(1)}, u32[]{:S(2)}, u32[]{:S(2)}) %collective-permute-start.24) | collective-permute-done | bytes 98336 | tf_op jit(solution)/shard_map/ppermute | solution.py:453
  173.9 2.7 collective-permute-done.25
  184.4 6.6 %all-to-all-start.1 = ((bf16[8,128,1536]{2,1,0:T(8,128)(2,1)}), bf16[8,128,1536]{2,1,0:T(8,128)(2,1)S(1)}, u32[]{:S(2)}, u32[]{:S(2)}) async-start(bf16[8,128,1536]{2,1,0:T(8,128)(2,1)} %get-tuple-element.27), calls=%async_computation.1 | async-start | bytes 6291456 | tf_op jit(solution)/shard_map/all_to_all | solution.py:573
  214.5 17.1 %collective-permute-done.19 = bf16[2,384,768]{2,1,0:T(8,128)(2,1)S(1)} collective-permute-done((bf16[2,384,768]{2,1,0:T(8,128)(2,1)S(1)}, bf16[2,384,768]{2,1,0:T(8,128)(2,1)S(1)}, u32[]{:S(2)}, u32[]{:S(2)}) %collective-permute-start.19) | collective-permute-done | bytes 1179680 | tf_op jit(solution)/shard_map/ppermute | solution.py:431
  232.4 5.1 %collective-permute-done.16 = bf16[2,384,768]{2,1,0:T(8,128)(2,1)S(1)} collective-permute-done((bf16[2,384,768]{2,1,0:T(8,128)(2,1)S(1)}, bf16[2,384,768]{2,1,0:T(8,128)(2,1)S(1)}, u32[]{:S(2)}, u32[]{:S(2)}) %collective-permute-start.16) | collective-permute-done | bytes 1179680 | tf_op jit(solution)/shard_map/ppermute | solution.py:431
  238.7 9.1 %collective-permute-done.20 = bf16[1,384,768]{2,1,0:T(8,128)(2,1)S(1)} collective-permute-done((bf16[1,384,768]{2,1,0:T(8,128)(2,1)S(1)}, bf16[1,384,768]{2,1,0:T(8,128)(2,1)S(1)}, u32[]{:S(2)}, u32[]{:S(2)}) %collective-permute-start.20) | collective-permute-done | bytes 589856 | tf_op jit(solution)/shard_map/ppermute | solution.py:431
  262.7 11.1 %collective-permute-done.21 = bf16[384,384]{1,0:T(8,128)(2,1)S(1)} collective-permute-done((bf16[384,384]{1,0:T(8,128)(2,1)S(1)}, bf16[384,384]{1,0:T(8,128)(2,1)S(1)}, u32[]{:S(2)}, u32[]{:S(2)}) %collective-permute-start.21) | collective-permute-done | bytes 294944 | tf_op jit(solution)/shard_map/ppermute | solution.py:474
  273.9 6.4 %collective-permute-done.22 = bf16[384,384]{1,0:T(8,128)(2,1)S(1)} collective-permute-done((bf16[384,384]{1,0:T(8,128)(2,1)S(1)}, bf16[384,384]{1,0:T(8,128)(2,1)S(1)}, u32[]{:S(2)}, u32[]{:S(2)}) %collective-permute-start.22) | collective-permute-done | bytes 294944 | tf_op jit(solution)/shard_map/ppermute | solution.py:474
  280.3 6.2 %collective-permute-done.23 = bf16[384,384]{1,0:T(8,128)(2,1)S(1)} collective-permute-done((bf16[384,384]{1,0:T(8,128)(2,1)S(1)}, bf16[384,384]{1,0:T(8,128)(2,1)S(1)}, u32[]{:S(2)}, u32[]{:S(2)}) %collective-permute-start.23) | collective-permute-done | bytes 294944 | tf_op jit(solution)/shard_map/ppermute | solution.py:474
  (155 shorter events, 82.2 us)
Async XLA Ops:
  5.1 92.4 %all-to-all-start = ((bf16[8,128,1536]{2,1,0:T(8,128)(2,1)}), bf16[8,128,1536]{2,1,0:T(8,128)(2,1)}, u32[]{:S(2)}, u32[]{:S(2)}) async-start(bf16[8,128,1536]{2,1,0:T(8,128)(2,1)} %pick_panels.2), calls=%async_computation | async-start | bytes 6291456 | tf_op jit(solution)/shard_map/all_to_all | solution.py:501
  10.6 15.4 %collective-permute-start.7 = (bf16[1,96,3072]{2,1,0:T(8,128)(2,1)S(1)}, bf16[1,96,3072]{2,1,0:T(8,128)(2,1)S(1)}, u32[]{:S(2)}, u32[]{:S(2)}) collective-permute-start(bf16[1,96,3072]{2,1,0:T(8,128)(2,1)S(1)} %get-tuple-element.32), channel_id=1, source_target_pairs={{0,16},{8,24},{16,0},{24,8},{1,17},{9,25},{17,1},{25,9},{2,18},{10... | collective-permute-start | bytes 1769480 | tf_op jit(solution)/shard_map/ppermute | solution.py:69
  12.2 15.5 %collective-permute-start.4 = (bf16[1,96,3072]{2,1,0:T(8,128)(2,1)S(1)}, bf16[1,96,3072]{2,1,0:T(8,128)(2,1)S(1)}, u32[]{:S(2)}, u32[]{:S(2)}) collective-permute-start(bf16[1,96,3072]{2,1,0:T(8,128)(2,1)S(1)} %get-tuple-element.33), channel_id=1, source_target_pairs={{0,8},{8,0},{16,24},{24,16},{1,9},{9,1},{17,25},{25,17},{2,10},{10... | collective-permute-start | bytes 1769480 | tf_op jit(solution)/shard_map/ppermute | solution.py:69
  26.2 27.2 %collective-permute-start.8 = (bf16[2,96,3072]{2,1,0:T(8,128)(2,1)S(1)}, bf16[2,96,3072]{2,1,0:T(8,128)(2,1)S(1)}, u32[]{:S(2)}, u32[]{:S(2)}) collective-permute-start(bf16[2,96,3072]{2,1,0:T(8,128)(2,1)S(1)} %pad_maximum_fusion.3), channel_id=1, source_target_pairs={{0,8},{8,0},{16,24},{24,16},{1,9},{9,1},{17,25},{25,17},{2,10},{10... | collective-permute-start | bytes 3538952 | tf_op jit(solution)/shard_map/ppermute | solution.py:69
  27.9 26.9 %collective-permute-start.5 = (bf16[2,96,3072]{2,1,0:T(8,128)(2,1)S(1)}, bf16[2,96,3072]{2,1,0:T(8,128)(2,1)S(1)}, u32[]{:S(2)}, u32[]{:S(2)}) collective-permute-start(bf16[2,96,3072]{2,1,0:T(8,128)(2,1)S(1)} %pad_maximum_fusion.2), channel_id=1, source_target_pairs={{0,16},{8,24},{16,0},{24,8},{1,17},{9,25},{17,1},{25,9},{2,18},{10... | collective-permute-start | bytes 3538952 | tf_op jit(solution)/shard_map/ppermute | solution.py:69
  29.5 33.7 %collective-permute-start = (s32[1,2,4]{2,1,0:T(2,128)S(1)}, s32[1,2,4]{2,1,0:T(2,128)S(1)}, u32[]{:S(2)}, u32[]{:S(2)}) collective-permute-start(s32[1,2,4]{2,1,0:T(2,128)S(1)} %add_bitcast_fusion), channel_id=1, source_target_pairs={{0,1},{1,0},{2,3},{3,2},{4,5},{5,4},{6,7},{7,6},{8,9},{9,8},{10,11... | collective-permute-start | bytes 104 | tf_op jit(solution)/shard_map/ppermute | solution.py:504
  53.6 35.9 %collective-permute-start.9 = (bf16[4,96,3072]{2,1,0:T(8,128)(2,1)S(1)}, bf16[4,96,3072]{2,1,0:T(8,128)(2,1)}, u32[]{:S(2)}, u32[]{:S(2)}) collective-permute-start(bf16[4,96,3072]{2,1,0:T(8,128)(2,1)S(1)} %pad_maximum_fusion.1.b), channel_id=1, source_target_pairs={{0,1},{1,0},{2,3},{3,2},{4,5},{5,4},{6,7},{7,6},{8,9},{9,8},{10,11... | collective-permute-start | bytes 7077896 | tf_op jit(solution)/shard_map/ppermute | solution.py:85
  56.5 33.0 %collective-permute-start.6 = (bf16[4,96,3072]{2,1,0:T(8,128)(2,1)}, bf16[4,96,3072]{2,1,0:T(8,128)(2,1)}, u32[]{:S(2)}, u32[]{:S(2)}) collective-permute-start(bf16[4,96,3072]{2,1,0:T(8,128)(2,1)} %pad_maximum_fusion.a), channel_id=1, source_target_pairs={{0,1},{1,0},{2,3},{3,2},{4,5},{5,4},{6,7},{7,6},{8,9},{9,8},{10,11... | collective-permute-start | bytes 7077896 | tf_op jit(solution)/shard_map/ppermute | solution.py:84
  57.3 60.1 %collective-permute-start.12 = (bf16[16,1536]{1,0:T(8,128)(2,1)S(1)}, bf16[16,1536]{1,0:T(8,128)(2,1)S(1)}, u32[]{:S(2)}, u32[]{:S(2)}) collective-permute-start(bf16[16,1536]{1,0:T(8,128)(2,1)S(1)} %get-tuple-element.43), channel_id=1, source_target_pairs={{0,1},{1,2},{2,3},{3,4},{4,5},{5,6},{6,7},{8,9},{9,10},{10,11},{11... | collective-permute-start | bytes 147464 | tf_op jit(solution)/shard_map/ppermute | solution.py:480
  59.7 57.6 %collective-permute-start.13 = (bf16[16,1536]{1,0:T(8,128)(2,1)S(1)}, bf16[16,1536]{1,0:T(8,128)(2,1)S(1)}, u32[]{:S(2)}, u32[]{:S(2)}) collective-permute-start(bf16[16,1536]{1,0:T(8,128)(2,1)S(1)} %get-tuple-element.42), channel_id=1, source_target_pairs={{1,0},{2,1},{3,2},{4,3},{5,4},{6,5},{7,6},{9,8},{10,9},{11,10},{12... | collective-permute-start | bytes 147464 | tf_op jit(solution)/shard_map/ppermute | solution.py:481
  66.8 11.9 %collective-permute-start.2 = (s32[2,2,4]{2,1,0:T(2,128)S(1)}, s32[2,2,4]{2,1,0:T(2,128)S(1)}, u32[]{:S(2)}, u32[]{:S(2)}) collective-permute-start(s32[2,2,4]{2,1,0:T(2,128)S(1)} %pad_add_fusion), channel_id=1, source_target_pairs={{0,4},{1,5},{2,6},{3,7},{4,0},{5,1},{6,2},{7,3},{8,12},{9,13},{10,... | collective-permute-start | bytes 200 | tf_op jit(solution)/shard_map/ppermute | solution.py:505
  176.8 23.7 %collective-permute-start.14 = (bf16[4,512,384]{2,1,0:T(8,128)(2,1)}, bf16[4,512,384]{2,1,0:T(8,128)(2,1)}, u32[]{:S(2)}, u32[]{:S(2)}) collective-permute-start(bf16[4,512,384]{2,1,0:T(8,128)(2,1)} %get-tuple-element.28), channel_id=1, source_target_pairs={{0,1},{1,0},{2,3},{3,2},{4,5},{5,4},{6,7},{7,6},{8,9},{9,8},{10,11... | collective-permute-start | bytes 4718600 | tf_op jit(solution)/shard_map/ppermute | solution.py:516
  178.5 12.6 %collective-permute-start.27 = (f32[4,1536]{1,0:T(4,128)}, f32[4,1536]{1,0:T(4,128)}, u32[]{:S(2)}, u32[]{:S(2)}) collective-permute-start(f32[4,1536]{1,0:T(4,128)} %bitcast_add_fusion.2), channel_id=1, source_target_pairs={{0,2},{1,3},{2,0},{3,1},{4,6},{5,7},{6,4},{7,5},{8,10},{9,11},{10,... | collective-permute-start | bytes 73736 | tf_op jit(solution)/shard_map/ppermute | solution.py:456
  184.4 16.1 %collective-permute-start.18 = (bf16[512,768]{1,0:T(8,128)(2,1)}, bf16[512,768]{1,0:T(8,128)(2,1)}, u32[]{:S(2)}, u32[]{:S(2)}) collective-permute-start(bf16[512,768]{1,0:T(8,128)(2,1)} %get-tuple-element.26.refs_3_), channel_id=1, source_target_pairs={{0,1},{1,0},{2,3},{3,2},{4,5},{5,4},{6,7},{7,6},{8,9},{9,8},{10,11... | collective-permute-start | bytes 2359304 | tf_op jit(solution)/shard_map/ppermute | solution.py:559
  184.4 103.0 %all-to-all-start.1 = ((bf16[8,128,1536]{2,1,0:T(8,128)(2,1)}), bf16[8,128,1536]{2,1,0:T(8,128)(2,1)S(1)}, u32[]{:S(2)}, u32[]{:S(2)}) async-start(bf16[8,128,1536]{2,1,0:T(8,128)(2,1)} %get-tuple-element.27), calls=%async_computation.1 | async-start | bytes 6291456 | tf_op jit(solution)/shard_map/all_to_all | solution.py:573
  191.1 16.7 %collective-permute-start.15 = (bf16[512,768]{1,0:T(8,128)(2,1)}, bf16[512,768]{1,0:T(8,128)(2,1)S(1)}, u32[]{:S(2)}, u32[]{:S(2)}) collective-permute-start(bf16[512,768]{1,0:T(8,128)(2,1)} %copy-done.7), channel_id=1, source_target_pairs={{0,1},{1,0},{2,3},{3,2},{4,5},{5,4},{6,7},{7,6},{8,9},{9,8},{10,11... | collective-permute-start | bytes 2359304 | tf_op jit(solution)/shard_map/ppermute | solution.py:559
  199.0 39.7 %collective-permute-start.32 = (f32[16,1536]{1,0:T(8,128)S(1)}, f32[16,1536]{1,0:T(8,128)S(1)}, u32[]{:S(2)}, u32[]{:S(2)}) collective-permute-start(f32[16,1536]{1,0:T(8,128)S(1)} %pad_maximum_fusion.6), channel_id=1, source_target_pairs={{0,8},{8,0},{16,24},{24,16},{1,9},{9,1},{17,25},{25,17},{2,10},{10... | collective-permute-start | bytes 294920 | tf_op jit(solution)/shard_map/ppermute | solution.py:461
  204.6 26.9 %collective-permute-start.19 = (bf16[2,384,768]{2,1,0:T(8,128)(2,1)S(1)}, bf16[2,384,768]{2,1,0:T(8,128)(2,1)S(1)}, u32[]{:S(2)}, u32[]{:S(2)}) collective-permute-start(bf16[2,384,768]{2,1,0:T(8,128)(2,1)S(1)} %add_convert_fusion), channel_id=1, source_target_pairs={{0,16},{8,24},{16,0},{24,8},{1,17},{9,25},{17,1},{25,9},{2,18},{10... | collective-permute-start | bytes 3538952 | tf_op jit(solution)/shard_map/ppermute | solution.py:431
  208.6 28.9 %collective-permute-start.16 = (bf16[2,384,768]{2,1,0:T(8,128)(2,1)S(1)}, bf16[2,384,768]{2,1,0:T(8,128)(2,1)S(1)}, u32[]{:S(2)}, u32[]{:S(2)}) collective-permute-start(bf16[2,384,768]{2,1,0:T(8,128)(2,1)S(1)} %add_convert_fusion.2), channel_id=1, source_target_pairs={{0,8},{8,0},{16,24},{24,16},{1,9},{9,1},{17,25},{25,17},{2,10},{10... | collective-permute-start | bytes 3538952 | tf_op jit(solution)/shard_map/ppermute | solution.py:431
  231.7 16.2 %collective-permute-start.20 = (bf16[1,384,768]{2,1,0:T(8,128)(2,1)S(1)}, bf16[1,384,768]{2,1,0:T(8,128)(2,1)S(1)}, u32[]{:S(2)}, u32[]{:S(2)}) collective-permute-start(bf16[1,384,768]{2,1,0:T(8,128)(2,1)S(1)} %add_convert_fusion.5), channel_id=1, source_target_pairs={{0,8},{8,0},{16,24},{24,16},{1,9},{9,1},{17,25},{25,17},{2,10},{10... | collective-permute-start | bytes 1769480 | tf_op jit(solution)/shard_map/ppermute | solution.py:431
  238.7 12.7 %collective-permute-start.17 = (bf16[1,384,768]{2,1,0:T(8,128)(2,1)}, bf16[1,384,768]{2,1,0:T(8,128)(2,1)}, u32[]{:S(2)}, u32[]{:S(2)}) collective-permute-start(bf16[1,384,768]{2,1,0:T(8,128)(2,1)} %add_convert_fusion.8), channel_id=1, source_target_pairs={{0,16},{8,24},{16,0},{24,8},{1,17},{9,25},{17,1},{25,9},{2,18},{10... | collective-permute-start | bytes 1769480 | tf_op jit(solution)/shard_map/ppermute | solution.py:431
  257.8 16.0 %collective-permute-start.21 = (bf16[384,384]{1,0:T(8,128)(2,1)S(1)}, bf16[384,384]{1,0:T(8,128)(2,1)S(1)}, u32[]{:S(2)}, u32[]{:S(2)}) collective-permute-start(bf16[384,384]{1,0:T(8,128)(2,1)S(1)} %get-tuple-element.46), channel_id=1, source_target_pairs={{0,2},{1,3},{2,0},{3,1},{4,6},{5,7},{6,4},{7,5},{8,10},{9,11},{10,... | collective-permute-start | bytes 884744 | tf_op jit(solution)/shard_map/ppermute | solution.py:474
  258.3 22.0 %collective-permute-start.22 = (bf16[384,384]{1,0:T(8,128)(2,1)S(1)}, bf16[384,384]{1,0:T(8,128)(2,1)S(1)}, u32[]{:S(2)}, u32[]{:S(2)}) collective-permute-start(bf16[384,384]{1,0:T(8,128)(2,1)S(1)} %get-tuple-element.48), channel_id=1, source_target_pairs={{0,4},{1,5},{2,6},{3,7},{4,0},{5,1},{6,2},{7,3},{8,12},{9,13},{10,... | collective-permute-start | bytes 884744 | tf_op jit(solution)/shard_map/ppermute | solution.py:474
  260.8 25.6 %collective-permute-start.23 = (bf16[384,384]{1,0:T(8,128)(2,1)S(1)}, bf16[384,384]{1,0:T(8,128)(2,1)S(1)}, u32[]{:S(2)}, u32[]{:S(2)}) collective-permute-start(bf16[384,384]{1,0:T(8,128)(2,1)S(1)} %get-tuple-element.47), channel_id=1, source_target_pairs={{0,6},{1,7},{2,4},{3,5},{4,2},{5,3},{6,0},{7,1},{8,14},{9,15},{10,... | collective-permute-start | bytes 884744 | tf_op jit(solution)/shard_map/ppermute | solution.py:474
  (27 other events, 202.5 us)

commit v3 on v2

--- a/solution.py
+++ b/solution.py
@@ -59,6 +59,26 @@
         out_shape=jax.ShapeDtypeStruct((count, rows, width), source.dtype),
         compiler_params=params(1),
         name="pick_panels",
+    )(index, source)
+
+
+def copy_body(_, source, target):
+    target[...] = source[...]
+
+
+def pick_blocks(source, index, count):
+    _, rows, width = source.shape
+    return pl.pallas_call(
+        copy_body,
+        grid_spec=pltpu.PrefetchScalarGridSpec(
+            num_scalar_prefetch=1,
+            grid=(count,),
+            in_specs=[pl.BlockSpec((1, rows, width), lambda i, idx: (idx[i], 0, 0))],
+            out_specs=pl.BlockSpec((1, rows, width), lambda i, idx: (i, 0, 0)),
+        ),
+        out_shape=jax.ShapeDtypeStruct((count, rows, width), source.dtype),
+        compiler_params=params(1),
+        name="pick_blocks",
     )(index, source)
 
 
@@ -422,15 +442,14 @@
 def outer_halved(lefts, rights, order):
     count = lefts[0].shape[0]
     rels = sorted(range(count), key=lambda r: [(r >> bit) & 1 for bit in order])
-    if rels != list(range(count)):
-        lefts = [jnp.concatenate([left[r : r + 1] for r in rels]) for left in lefts]
     half = count // 2
-    send = outer_sum([left[half:] for left in lefts], rights)
-    keep = outer_sum([left[:half] for left in lefts], rights)
+    pick = lambda left, some: jnp.concatenate([left[r : r + 1] for r in some])
+    send = outer_sum([pick(left, rels[half:]) for left in lefts], rights)
+    keep = outer_sum([pick(left, rels[:half]) for left in lefts], rights)
+    add = lambda a, b: (a.astype(F32) + b.astype(F32)).astype(BF)
     for bit in order:
         got = lax.ppermute(send, "dp", flip_bit("dp", bit))
         half = half // 2
-        add = lambda a, b: (a.astype(F32) + b.astype(F32)).astype(BF)
         if half:
             send = add(keep[half:], got[half:])
             keep = add(keep[:half], got[:half])
@@ -580,7 +599,7 @@
     share = jnp.concatenate(shares, axis=1)
     share = share.reshape(width // count, owners // 2, piece).transpose(1, 0, 2)
     shard_in = sum_across(share)
-    grad_loaded = pick_panels(returned, owner_of.astype(jnp.int32), panels)
+    grad_loaded = pick_blocks(returned, owner_of.astype(jnp.int32), panels)
     sums = sum_everywhere(jnp.concatenate([kernel_term[:taps], gain_term], axis=0))
     return (grad_loaded[None, None], shard_in, sums[:taps], sums[taps])
 

time: 290 us -> 291 us (level)
  no operation moved by 1% of the time
where the time goes in v3:
time: 291 us; the launch traced here: 290 us
  waiting for transfers between devices  118 us (41%)
  Pallas kernels  78.8 us (27%)
  starting transfers between devices  52.7 us (18%)
  local copies, waits for them, and re-layouts  14 us (5%)
  matrix products  13.4 us (5%)
  other arithmetic  11.6 us (4%)
    ppermute x4, waiting for transfers between devices, gather_order(): got = lax.ppermute(have, 'dp', flip_bit('dp', bit))  37.2 us
    ppermute x4, waiting for transfers between devices, outer_halved(): got = lax.ppermute(send, 'dp', flip_bit('dp', bit))  31.3 us
    ppermute x3, waiting for transfers between devices, sum_across(): total = total + lax.ppermute(piece, 'tm', pairs).astype(F32)  23.7 us
    pallas_call x2, Pallas kernels, gated(): pl.pallas_call(functools.partial(gated_body, **sizes), grid_spec=pltpu.Pr...  14.8 us
    ppermute x3, waiting for transfers between devices, local(): lax.ppermute(tags, 'tm', flip('tm', i))  14.5 us
    pallas_call x2, Pallas kernels, put(): pl.pallas_call(body, grid_spec=pltpu.PrefetchScalarGridSpec(num_scalar_pr...  14.3 us
    pallas_call x1, Pallas kernels, back(): pl.pallas_call(functools.partial(back_body, grads=len(gradients), block=b...  14.3 us
    dot_general x8, matrix products, outer_sum(): lax.dot_general(a, b, (((1,), (0,)), ((), ())), preferred_element_type=F32)  13.4 us
  transfers between devices with their start and end apart: 35, of which 18 were waited for; matrix products, arithmetic and copies ran while one was open for 13% of the time, Pallas kernels for 9%

profile of v3, /device:TPU:8, one launch (start us, length us, event | category | flops | bytes accessed | tf_op | source)
XLA Modules:
  0.0 289.6 jit_solution(7140705421755527354)
XLA Ops:
  5.1 5.5 %all-to-all-start = ((bf16[8,128,1536]{2,1,0:T(8,128)(2,1)}), bf16[8,128,1536]{2,1,0:T(8,128)(2,1)}, u32[]{:S(2)}, u32[]{:S(2)}) async-start(bf16[8,128,1536]{2,1,0:T(8,128)(2,1)} %pick_panels.1), calls=%async_computation | async-start | bytes 6291456 | tf_op jit(solution)/shard_map/all_to_all | solution.py:520
  13.7 12.3 %collective-permute-done.7 = bf16[1,96,3072]{2,1,0:T(8,128)(2,1)S(1)} collective-permute-done((bf16[1,96,3072]{2,1,0:T(8,128)(2,1)S(1)}, bf16[1,96,3072]{2,1,0:T(8,128)(2,1)S(1)}, u32[]{:S(2)}, u32[]{:S(2)}) %collective-permute-start.7) | collective-permute-done | bytes 589856 | tf_op jit(solution)/shard_map/ppermute | solution.py:89
  29.5 23.8 %collective-permute-done.8 = bf16[2,96,3072]{2,1,0:T(8,128)(2,1)S(1)} collective-permute-done((bf16[2,96,3072]{2,1,0:T(8,128)(2,1)S(1)}, bf16[2,96,3072]{2,1,0:T(8,128)(2,1)S(1)}, u32[]{:S(2)}, u32[]{:S(2)}) %collective-permute-start.8) | collective-permute-done | bytes 1179680 | tf_op jit(solution)/shard_map/ppermute | solution.py:89
  59.7 3.1 %collective-permute-start.13 = (bf16[16,1536]{1,0:T(8,128)(2,1)S(1)}, bf16[16,1536]{1,0:T(8,128)(2,1)S(1)}, u32[]{:S(2)}, u32[]{:S(2)}) collective-permute-start(bf16[16,1536]{1,0:T(8,128)(2,1)S(1)} %get-tuple-element.42), channel_id=1, source_target_pairs={{1,0},{2,1},{3,2},{4,3},{5,4},{6,5},{7,6},{9,8},{10,9},{11,10},{12... | collective-permute-start | bytes 147464 | tf_op jit(solution)/shard_map/ppermute | solution.py:500
  63.3 3.6 %collective-permute-done.1 = s32[2,2,4]{2,1,0:T(2,128)S(1)} collective-permute-done((s32[2,2,4]{2,1,0:T(2,128)S(1)}, s32[2,2,4]{2,1,0:T(2,128)S(1)}, u32[]{:S(2)}, u32[]{:S(2)}) %collective-permute-start.1) | collective-permute-done | bytes 96 | tf_op jit(solution)/shard_map/ppermute | solution.py:524
  69.3 9.4 %collective-permute-done.2 = s32[2,2,4]{2,1,0:T(2,128)S(1)} collective-permute-done((s32[2,2,4]{2,1,0:T(2,128)S(1)}, s32[2,2,4]{2,1,0:T(2,128)S(1)}, u32[]{:S(2)}, u32[]{:S(2)}) %collective-permute-start.2) | collective-permute-done | bytes 96 | tf_op jit(solution)/shard_map/ppermute | solution.py:524
  83.2 6.3 %put_weights.2.rest_0_ = bf16[16,96,3072]{2,1,0:T(8,128)(2,1)} custom-call(s32[8]{0:T(128)S(1)} %stack.76._, bf16[4,96,3072]{2,1,0:T(8,128)(2,1)} %pad_maximum_fusion.a, bf16[4,96,3072]{2,1,0:T(8,128)(2,1)S(1)} %pad_maximum_fusion.1.b), custom_call_target="tpu_custom_call" | custom-call | tf_op jit(solution)/shard_map/put_weights/pallas_call | solution.py:131
  89.5 8.0 %put_weights.3 = bf16[16,96,3072]{2,1,0:T(8,128)(2,1)} custom-call(s32[8]{0:T(128)S(1)} %stack.67._, bf16[4,96,3072]{2,1,0:T(8,128)(2,1)} %collective-permute-done.6.a, bf16[4,96,3072]{2,1,0:T(8,128)(2,1)} %collective-permute-done.9.b, bf16[16,96,3072]{2,1,0:T(8,128)(2,1)} %put_weights.2.rest_0_), custom_call_target="tpu_custom_call", output_to_operand_aliasing={{}: (3, {})} | custom-call | tf_op jit(solution)/shard_map/put_weights/pallas_call | solution.py:131
  97.5 12.4 %forward.1 = (bf16[4,512,384]{2,1,0:T(8,128)(2,1)}, f32[512,1536]{1,0:T(8,128)}, f32[512,1536]{1,0:T(8,128)}, bf16[512,1536]{1,0:T(8,128)(2,1)S(1)}) custom-call(s32[5]{0:T(128)S(1)} %get-tuple-element.59.source, bf16[8,128,1536]{2,1,0:T(8,128)(2,1)} %all-to-all-done.x_hbm.refs_5_, f32[1,1536]{1,0:T(1,128)S(1)} %reshape.103.gain_ref.refs_7_, ...), custom_call_target="tpu_custom_call" | custom-call | tf_op jit(solution)/shard_map/forward/pallas_call | solution.py:189
  111.9 5.4 %collective-permute-start.11 = (bf16[32,1536]{1,0:T(8,128)(2,1)S(1)}, bf16[32,1536]{1,0:T(8,128)(2,1)S(1)}, u32[]{:S(2)}, u32[]{:S(2)}) collective-permute-start(bf16[32,1536]{1,0:T(8,128)(2,1)S(1)} %get-tuple-element.44), channel_id=1, source_target_pairs={{1,0},{2,1},{3,2},{4,3},{5,4},{6,5},{7,6},{9,8},{10,9},{11,10},{12... | collective-permute-start | bytes 294920 | tf_op jit(solution)/shard_map/ppermute | solution.py:500
  119.3 9.7 %depth.1 = (bf16[512,1536]{1,0:T(8,128)(2,1)S(1)}, bf16[16,1536]{1,0:T(8,128)(2,1)S(1)}, bf16[16,1536]{1,0:T(8,128)(2,1)S(1)}) custom-call(s32[8]{0:T(128)S(1)} %add_convert_fusion.10.flags, bf16[512,1536]{1,0:T(8,128)(2,1)S(1)} %get-tuple-element.17.glu, bf16[32,1536]{1,0:T(8,128)(2,1)S(1)} %collective-permute-done.10.low, ...), custom_call_target="tpu_custom_call" | custom-call | tf_op jit(solution)/shard_map/depth/pallas_call | solution.py:544
  129.0 7.7 %gated.3 = (bf16[512,768]{1,0:T(8,128)(2,1)S(1)}, bf16[512,768]{1,0:T(8,128)(2,1)}) custom-call(s32[9]{0:T(128)S(1)} %get-tuple-element.57.flags, bf16[512,1536]{1,0:T(8,128)(2,1)S(1)} %get-tuple-element.18.grad, bf16[16,1536]{1,0:T(8,128)(2,1)S(1)} %get-tuple-element.19.low, bf16[16,1536]{1,0:T(8,128)(2,1)S(1)} %get-tuple-element.20.high, ...), custom_call_target="tpu_custom_call" | custom-call | tf_op jit(solution)/shard_map/gated/pallas_call | solution.py:319
  136.7 7.0 %gated.2 = (bf16[512,768]{1,0:T(8,128)(2,1)S(1)}, bf16[512,768]{1,0:T(8,128)(2,1)S(1)}) custom-call(s32[9]{0:T(128)S(1)} %get-tuple-element.58.flags, bf16[512,1536]{1,0:T(8,128)(2,1)S(1)} %get-tuple-element.18.grad, bf16[16,1536]{1,0:T(8,128)(2,1)S(1)} %get-tuple-element.19.low, bf16[16,1536]{1,0:T(8,128)(2,1)S(1)} %get-tuple-element.20.high, ...), custom_call_target="tpu_custom_call" | custom-call | tf_op jit(solution)/shard_map/gated/pallas_call | solution.py:319
  143.8 8.8 %taps.1 = f32[32,1536]{1,0:T(8,128)S(1)} custom-call(s32[8]{0:T(128)S(1)} %add_convert_fusion.10.flags, bf16[512,1536]{1,0:T(8,128)(2,1)S(1)} %get-tuple-element.17.glu, bf16[32,1536]{1,0:T(8,128)(2,1)S(1)} %collective-permute-done.10.low, bf16[32,1536]{1,0:T(8,128)(2,1)S(1)} %collective-permute-done.11.high, bf16[512,1536]{1,0:T(8,128)(2,1)S(1)} %get-tuple-element.18.grad), custom_call_target="tpu_custom_call" | custom-call | tf_op jit(solution)/shard_map/taps/pallas_call | solution.py:560
  152.6 14.3 %back.1 = (bf16[8,128,1536]{2,1,0:T(8,128)(2,1)}, f32[1,1536]{1,0:T(1,128)S(1)}) custom-call(s32[5]{0:T(128)S(1)} %get-tuple-element.60.source, bf16[512,768]{1,0:T(8,128)(2,1)S(1)} %get-tuple-element.23.refs_0_, bf16[512,768]{1,0:T(8,128)(2,1)S(1)} %get-tuple-element.24.refs_1_, bf16[512,768]{1,0:T(8,128)(2,1)S(1)} %get-tuple-element.25.refs_2_, ...), custom_call_target="tpu_custom_call" | custom-call | tf_op jit(solution)/shard_map/back/pallas_call | solution.py:404
  168.5 3.9 %collective-permute-done.24 = f32[16,1536]{1,0:T(8,128)S(1)} collective-permute-done((f32[16,1536]{1,0:T(8,128)S(1)}, f32[16,1536]{1,0:T(8,128)S(1)}, u32[]{:S(2)}, u32[]{:S(2)}) %collective-permute-start.24) | collective-permute-done | bytes 98336 | tf_op jit(solution)/shard_map/ppermute | solution.py:472
  173.9 2.7 collective-permute-done.25
  184.4 6.6 %all-to-all-start.1 = ((bf16[8,128,1536]{2,1,0:T(8,128)(2,1)}), bf16[8,128,1536]{2,1,0:T(8,128)(2,1)S(1)}, u32[]{:S(2)}, u32[]{:S(2)}) async-start(bf16[8,128,1536]{2,1,0:T(8,128)(2,1)} %get-tuple-element.27), calls=%async_computation.1 | async-start | bytes 6291456 | tf_op jit(solution)/shard_map/all_to_all | solution.py:592
  214.5 17.1 %collective-permute-done.19 = bf16[2,384,768]{2,1,0:T(8,128)(2,1)S(1)} collective-permute-done((bf16[2,384,768]{2,1,0:T(8,128)(2,1)S(1)}, bf16[2,384,768]{2,1,0:T(8,128)(2,1)S(1)}, u32[]{:S(2)}, u32[]{:S(2)}) %collective-permute-start.19) | collective-permute-done | bytes 1179680 | tf_op jit(solution)/shard_map/ppermute | solution.py:451
  232.4 5.1 %collective-permute-done.16 = bf16[2,384,768]{2,1,0:T(8,128)(2,1)S(1)} collective-permute-done((bf16[2,384,768]{2,1,0:T(8,128)(2,1)S(1)}, bf16[2,384,768]{2,1,0:T(8,128)(2,1)S(1)}, u32[]{:S(2)}, u32[]{:S(2)}) %collective-permute-start.16) | collective-permute-done | bytes 1179680 | tf_op jit(solution)/shard_map/ppermute | solution.py:451
  238.7 9.1 %collective-permute-done.20 = bf16[1,384,768]{2,1,0:T(8,128)(2,1)S(1)} collective-permute-done((bf16[1,384,768]{2,1,0:T(8,128)(2,1)S(1)}, bf16[1,384,768]{2,1,0:T(8,128)(2,1)S(1)}, u32[]{:S(2)}, u32[]{:S(2)}) %collective-permute-start.20) | collective-permute-done | bytes 589856 | tf_op jit(solution)/shard_map/ppermute | solution.py:451
  262.7 11.1 %collective-permute-done.21 = bf16[384,384]{1,0:T(8,128)(2,1)S(1)} collective-permute-done((bf16[384,384]{1,0:T(8,128)(2,1)S(1)}, bf16[384,384]{1,0:T(8,128)(2,1)S(1)}, u32[]{:S(2)}, u32[]{:S(2)}) %collective-permute-start.21) | collective-permute-done | bytes 294944 | tf_op jit(solution)/shard_map/ppermute | solution.py:493
  273.9 6.4 %collective-permute-done.22 = bf16[384,384]{1,0:T(8,128)(2,1)S(1)} collective-permute-done((bf16[384,384]{1,0:T(8,128)(2,1)S(1)}, bf16[384,384]{1,0:T(8,128)(2,1)S(1)}, u32[]{:S(2)}, u32[]{:S(2)}) %collective-permute-start.22) | collective-permute-done | bytes 294944 | tf_op jit(solution)/shard_map/ppermute | solution.py:493
  280.3 6.2 %collective-permute-done.23 = bf16[384,384]{1,0:T(8,128)(2,1)S(1)} collective-permute-done((bf16[384,384]{1,0:T(8,128)(2,1)S(1)}, bf16[384,384]{1,0:T(8,128)(2,1)S(1)}, u32[]{:S(2)}, u32[]{:S(2)}) %collective-permute-start.23) | collective-permute-done | bytes 294944 | tf_op jit(solution)/shard_map/ppermute | solution.py:493
  (155 shorter events, 82.8 us)
Async XLA Ops:
  5.1 92.4 %all-to-all-start = ((bf16[8,128,1536]{2,1,0:T(8,128)(2,1)}), bf16[8,128,1536]{2,1,0:T(8,128)(2,1)}, u32[]{:S(2)}, u32[]{:S(2)}) async-start(bf16[8,128,1536]{2,1,0:T(8,128)(2,1)} %pick_panels.1), calls=%async_computation | async-start | bytes 6291456 | tf_op jit(solution)/shard_map/all_to_all | solution.py:520
  10.6 15.4 %collective-permute-start.7 = (bf16[1,96,3072]{2,1,0:T(8,128)(2,1)S(1)}, bf16[1,96,3072]{2,1,0:T(8,128)(2,1)S(1)}, u32[]{:S(2)}, u32[]{:S(2)}) collective-permute-start(bf16[1,96,3072]{2,1,0:T(8,128)(2,1)S(1)} %get-tuple-element.32), channel_id=1, source_target_pairs={{0,16},{8,24},{16,0},{24,8},{1,17},{9,25},{17,1},{25,9},{2,18},{10... | collective-permute-start | bytes 1769480 | tf_op jit(solution)/shard_map/ppermute | solution.py:89
  12.2 15.5 %collective-permute-start.4 = (bf16[1,96,3072]{2,1,0:T(8,128)(2,1)S(1)}, bf16[1,96,3072]{2,1,0:T(8,128)(2,1)S(1)}, u32[]{:S(2)}, u32[]{:S(2)}) collective-permute-start(bf16[1,96,3072]{2,1,0:T(8,128)(2,1)S(1)} %get-tuple-element.33), channel_id=1, source_target_pairs={{0,8},{8,0},{16,24},{24,16},{1,9},{9,1},{17,25},{25,17},{2,10},{10... | collective-permute-start | bytes 1769480 | tf_op jit(solution)/shard_map/ppermute | solution.py:89
  26.2 27.2 %collective-permute-start.8 = (bf16[2,96,3072]{2,1,0:T(8,128)(2,1)S(1)}, bf16[2,96,3072]{2,1,0:T(8,128)(2,1)S(1)}, u32[]{:S(2)}, u32[]{:S(2)}) collective-permute-start(bf16[2,96,3072]{2,1,0:T(8,128)(2,1)S(1)} %pad_maximum_fusion.3), channel_id=1, source_target_pairs={{0,8},{8,0},{16,24},{24,16},{1,9},{9,1},{17,25},{25,17},{2,10},{10... | collective-permute-start | bytes 3538952 | tf_op jit(solution)/shard_map/ppermute | solution.py:89
  27.9 26.9 %collective-permute-start.5 = (bf16[2,96,3072]{2,1,0:T(8,128)(2,1)S(1)}, bf16[2,96,3072]{2,1,0:T(8,128)(2,1)S(1)}, u32[]{:S(2)}, u32[]{:S(2)}) collective-permute-start(bf16[2,96,3072]{2,1,0:T(8,128)(2,1)S(1)} %pad_maximum_fusion.2), channel_id=1, source_target_pairs={{0,16},{8,24},{16,0},{24,8},{1,17},{9,25},{17,1},{25,9},{2,18},{10... | collective-permute-start | bytes 3538952 | tf_op jit(solution)/shard_map/ppermute | solution.py:89
  29.5 33.7 %collective-permute-start = (s32[1,2,4]{2,1,0:T(2,128)S(1)}, s32[1,2,4]{2,1,0:T(2,128)S(1)}, u32[]{:S(2)}, u32[]{:S(2)}) collective-permute-start(s32[1,2,4]{2,1,0:T(2,128)S(1)} %add_bitcast_fusion), channel_id=1, source_target_pairs={{0,1},{1,0},{2,3},{3,2},{4,5},{5,4},{6,7},{7,6},{8,9},{9,8},{10,11... | collective-permute-start | bytes 104 | tf_op jit(solution)/shard_map/ppermute | solution.py:523
  53.6 35.9 %collective-permute-start.9 = (bf16[4,96,3072]{2,1,0:T(8,128)(2,1)S(1)}, bf16[4,96,3072]{2,1,0:T(8,128)(2,1)}, u32[]{:S(2)}, u32[]{:S(2)}) collective-permute-start(bf16[4,96,3072]{2,1,0:T(8,128)(2,1)S(1)} %pad_maximum_fusion.1.b), channel_id=1, source_target_pairs={{0,1},{1,0},{2,3},{3,2},{4,5},{5,4},{6,7},{7,6},{8,9},{9,8},{10,11... | collective-permute-start | bytes 7077896 | tf_op jit(solution)/shard_map/ppermute | solution.py:105
  56.5 33.0 %collective-permute-start.6 = (bf16[4,96,3072]{2,1,0:T(8,128)(2,1)}, bf16[4,96,3072]{2,1,0:T(8,128)(2,1)}, u32[]{:S(2)}, u32[]{:S(2)}) collective-permute-start(bf16[4,96,3072]{2,1,0:T(8,128)(2,1)} %pad_maximum_fusion.a), channel_id=1, source_target_pairs={{0,1},{1,0},{2,3},{3,2},{4,5},{5,4},{6,7},{7,6},{8,9},{9,8},{10,11... | collective-permute-start | bytes 7077896 | tf_op jit(solution)/shard_map/ppermute | solution.py:104
  57.3 60.1 %collective-permute-start.12 = (bf16[16,1536]{1,0:T(8,128)(2,1)S(1)}, bf16[16,1536]{1,0:T(8,128)(2,1)S(1)}, u32[]{:S(2)}, u32[]{:S(2)}) collective-permute-start(bf16[16,1536]{1,0:T(8,128)(2,1)S(1)} %get-tuple-element.43), channel_id=1, source_target_pairs={{0,1},{1,2},{2,3},{3,4},{4,5},{5,6},{6,7},{8,9},{9,10},{10,11},{11... | collective-permute-start | bytes 147464 | tf_op jit(solution)/shard_map/ppermute | solution.py:499
  59.7 57.6 %collective-permute-start.13 = (bf16[16,1536]{1,0:T(8,128)(2,1)S(1)}, bf16[16,1536]{1,0:T(8,128)(2,1)S(1)}, u32[]{:S(2)}, u32[]{:S(2)}) collective-permute-start(bf16[16,1536]{1,0:T(8,128)(2,1)S(1)} %get-tuple-element.42), channel_id=1, source_target_pairs={{1,0},{2,1},{3,2},{4,3},{5,4},{6,5},{7,6},{9,8},{10,9},{11,10},{12... | collective-permute-start | bytes 147464 | tf_op jit(solution)/shard_map/ppermute | solution.py:500
  66.8 11.9 %collective-permute-start.2 = (s32[2,2,4]{2,1,0:T(2,128)S(1)}, s32[2,2,4]{2,1,0:T(2,128)S(1)}, u32[]{:S(2)}, u32[]{:S(2)}) collective-permute-start(s32[2,2,4]{2,1,0:T(2,128)S(1)} %pad_add_fusion), channel_id=1, source_target_pairs={{0,4},{1,5},{2,6},{3,7},{4,0},{5,1},{6,2},{7,3},{8,12},{9,13},{10,... | collective-permute-start | bytes 200 | tf_op jit(solution)/shard_map/ppermute | solution.py:524
  176.8 23.7 %collective-permute-start.14 = (bf16[4,512,384]{2,1,0:T(8,128)(2,1)}, bf16[4,512,384]{2,1,0:T(8,128)(2,1)}, u32[]{:S(2)}, u32[]{:S(2)}) collective-permute-start(bf16[4,512,384]{2,1,0:T(8,128)(2,1)} %get-tuple-element.28), channel_id=1, source_target_pairs={{0,1},{1,0},{2,3},{3,2},{4,5},{5,4},{6,7},{7,6},{8,9},{9,8},{10,11... | collective-permute-start | bytes 4718600 | tf_op jit(solution)/shard_map/ppermute | solution.py:535
  178.5 12.6 %collective-permute-start.27 = (f32[4,1536]{1,0:T(4,128)}, f32[4,1536]{1,0:T(4,128)}, u32[]{:S(2)}, u32[]{:S(2)}) collective-permute-start(f32[4,1536]{1,0:T(4,128)} %bitcast_add_fusion.2), channel_id=1, source_target_pairs={{0,2},{1,3},{2,0},{3,1},{4,6},{5,7},{6,4},{7,5},{8,10},{9,11},{10,... | collective-permute-start | bytes 73736 | tf_op jit(solution)/shard_map/ppermute | solution.py:475
  184.4 16.1 %collective-permute-start.18 = (bf16[512,768]{1,0:T(8,128)(2,1)}, bf16[512,768]{1,0:T(8,128)(2,1)}, u32[]{:S(2)}, u32[]{:S(2)}) collective-permute-start(bf16[512,768]{1,0:T(8,128)(2,1)} %get-tuple-element.26.refs_3_), channel_id=1, source_target_pairs={{0,1},{1,0},{2,3},{3,2},{4,5},{5,4},{6,7},{7,6},{8,9},{9,8},{10,11... | collective-permute-start | bytes 2359304 | tf_op jit(solution)/shard_map/ppermute | solution.py:578
  184.4 103.0 %all-to-all-start.1 = ((bf16[8,128,1536]{2,1,0:T(8,128)(2,1)}), bf16[8,128,1536]{2,1,0:T(8,128)(2,1)S(1)}, u32[]{:S(2)}, u32[]{:S(2)}) async-start(bf16[8,128,1536]{2,1,0:T(8,128)(2,1)} %get-tuple-element.27), calls=%async_computation.1 | async-start | bytes 6291456 | tf_op jit(solution)/shard_map/all_to_all | solution.py:592
  191.1 16.7 %collective-permute-start.15 = (bf16[512,768]{1,0:T(8,128)(2,1)}, bf16[512,768]{1,0:T(8,128)(2,1)S(1)}, u32[]{:S(2)}, u32[]{:S(2)}) collective-permute-start(bf16[512,768]{1,0:T(8,128)(2,1)} %copy-done.7), channel_id=1, source_target_pairs={{0,1},{1,0},{2,3},{3,2},{4,5},{5,4},{6,7},{7,6},{8,9},{9,8},{10,11... | collective-permute-start | bytes 2359304 | tf_op jit(solution)/shard_map/ppermute | solution.py:578
  199.0 39.7 %collective-permute-start.32 = (f32[16,1536]{1,0:T(8,128)S(1)}, f32[16,1536]{1,0:T(8,128)S(1)}, u32[]{:S(2)}, u32[]{:S(2)}) collective-permute-start(f32[16,1536]{1,0:T(8,128)S(1)} %pad_maximum_fusion.6), channel_id=1, source_target_pairs={{0,8},{8,0},{16,24},{24,16},{1,9},{9,1},{17,25},{25,17},{2,10},{10... | collective-permute-start | bytes 294920 | tf_op jit(solution)/shard_map/ppermute | solution.py:480
  204.6 26.9 %collective-permute-start.19 = (bf16[2,384,768]{2,1,0:T(8,128)(2,1)S(1)}, bf16[2,384,768]{2,1,0:T(8,128)(2,1)S(1)}, u32[]{:S(2)}, u32[]{:S(2)}) collective-permute-start(bf16[2,384,768]{2,1,0:T(8,128)(2,1)S(1)} %add_convert_fusion), channel_id=1, source_target_pairs={{0,16},{8,24},{16,0},{24,8},{1,17},{9,25},{17,1},{25,9},{2,18},{10... | collective-permute-start | bytes 3538952 | tf_op jit(solution)/shard_map/ppermute | solution.py:451
  208.6 28.9 %collective-permute-start.16 = (bf16[2,384,768]{2,1,0:T(8,128)(2,1)S(1)}, bf16[2,384,768]{2,1,0:T(8,128)(2,1)S(1)}, u32[]{:S(2)}, u32[]{:S(2)}) collective-permute-start(bf16[2,384,768]{2,1,0:T(8,128)(2,1)S(1)} %add_convert_fusion.2), channel_id=1, source_target_pairs={{0,8},{8,0},{16,24},{24,16},{1,9},{9,1},{17,25},{25,17},{2,10},{10... | collective-permute-start | bytes 3538952 | tf_op jit(solution)/shard_map/ppermute | solution.py:451
  231.7 16.2 %collective-permute-start.20 = (bf16[1,384,768]{2,1,0:T(8,128)(2,1)S(1)}, bf16[1,384,768]{2,1,0:T(8,128)(2,1)S(1)}, u32[]{:S(2)}, u32[]{:S(2)}) collective-permute-start(bf16[1,384,768]{2,1,0:T(8,128)(2,1)S(1)} %add_convert_fusion.5), channel_id=1, source_target_pairs={{0,8},{8,0},{16,24},{24,16},{1,9},{9,1},{17,25},{25,17},{2,10},{10... | collective-permute-start | bytes 1769480 | tf_op jit(solution)/shard_map/ppermute | solution.py:451
  238.7 12.7 %collective-permute-start.17 = (bf16[1,384,768]{2,1,0:T(8,128)(2,1)}, bf16[1,384,768]{2,1,0:T(8,128)(2,1)}, u32[]{:S(2)}, u32[]{:S(2)}) collective-permute-start(bf16[1,384,768]{2,1,0:T(8,128)(2,1)} %add_convert_fusion.8), channel_id=1, source_target_pairs={{0,16},{8,24},{16,0},{24,8},{1,17},{9,25},{17,1},{25,9},{2,18},{10... | collective-permute-start | bytes 1769480 | tf_op jit(solution)/shard_map/ppermute | solution.py:451
  257.8 16.0 %collective-permute-start.21 = (bf16[384,384]{1,0:T(8,128)(2,1)S(1)}, bf16[384,384]{1,0:T(8,128)(2,1)S(1)}, u32[]{:S(2)}, u32[]{:S(2)}) collective-permute-start(bf16[384,384]{1,0:T(8,128)(2,1)S(1)} %get-tuple-element.46), channel_id=1, source_target_pairs={{0,2},{1,3},{2,0},{3,1},{4,6},{5,7},{6,4},{7,5},{8,10},{9,11},{10,... | collective-permute-start | bytes 884744 | tf_op jit(solution)/shard_map/ppermute | solution.py:493
  258.3 22.0 %collective-permute-start.22 = (bf16[384,384]{1,0:T(8,128)(2,1)S(1)}, bf16[384,384]{1,0:T(8,128)(2,1)S(1)}, u32[]{:S(2)}, u32[]{:S(2)}) collective-permute-start(bf16[384,384]{1,0:T(8,128)(2,1)S(1)} %get-tuple-element.48), channel_id=1, source_target_pairs={{0,4},{1,5},{2,6},{3,7},{4,0},{5,1},{6,2},{7,3},{8,12},{9,13},{10,... | collective-permute-start | bytes 884744 | tf_op jit(solution)/shard_map/ppermute | solution.py:493
  260.8 25.6 %collective-permute-start.23 = (bf16[384,384]{1,0:T(8,128)(2,1)S(1)}, bf16[384,384]{1,0:T(8,128)(2,1)S(1)}, u32[]{:S(2)}, u32[]{:S(2)}) collective-permute-start(bf16[384,384]{1,0:T(8,128)(2,1)S(1)} %get-tuple-element.47), channel_id=1, source_target_pairs={{0,6},{1,7},{2,4},{3,5},{4,2},{5,3},{6,0},{7,1},{8,14},{9,15},{10,... | collective-permute-start | bytes 884744 | tf_op jit(solution)/shard_map/ppermute | solution.py:493
  (27 other events, 202.5 us)

commit v4 on v3

--- a/solution.py
+++ b/solution.py
@@ -14,7 +14,7 @@
 TILE = 32
 
 
-def params(count, mib=48):
+def params(count, mib):
     return pltpu.CompilerParams(
         dimension_semantics=("arbitrary",) * count, vmem_limit_bytes=mib << 20
     )
@@ -46,7 +46,7 @@
 
 def pick_panels(source, index, count):
     _, rows, width = source.shape
-    hbm = pl.BlockSpec(memory_space=pl.ANY)
+    hbm = pl.BlockSpec(memory_space=pltpu.HBM)
     return pl.pallas_call(
         functools.partial(pick_body, count=count),
         grid_spec=pltpu.PrefetchScalarGridSpec(
@@ -57,7 +57,7 @@
             scratch_shapes=[pltpu.SemaphoreType.DMA((count,))],
         ),
         out_shape=jax.ShapeDtypeStruct((count, rows, width), source.dtype),
-        compiler_params=params(1),
+        compiler_params=params(1, 58),
         name="pick_panels",
     )(index, source)
 
@@ -77,7 +77,7 @@
             out_specs=pl.BlockSpec((1, rows, width), lambda i, idx: (i, 0, 0)),
         ),
         out_shape=jax.ShapeDtypeStruct((count, rows, width), source.dtype),
-        compiler_params=params(1),
+        compiler_params=params(1, 8),
         name="pick_blocks",
     )(index, source)
 
@@ -141,7 +141,7 @@
             ),
             out_shape=jax.ShapeDtypeStruct((4 * count, quarter, width), w_in.dtype),
             input_output_aliases={3: 0} if base else {},
-            compiler_params=params(2),
+            compiler_params=params(2, 48),
             name="put_weights",
         )(out_index(side), *pair, *base)
 
@@ -210,7 +210,7 @@
             ],
         ),
         out_shape=[parts, wide(F32), wide(F32), wide(BF)],
-        compiler_params=params(1),
+        compiler_params=params(1, 58),
         name="forward",
     )(jnp.append(source, lax.axis_index("dp")), arrived, gain.reshape(1, width), full_in, full_in)
 
@@ -328,7 +328,7 @@
             ],
         ),
         out_shape=shapes,
-        compiler_params=params(1),
+        compiler_params=params(1, 58),
         name="gated",
     )(jnp.append(flags, parity), grad_depth, low, high, lin, gate, kernel)
 
@@ -426,7 +426,7 @@
             jax.ShapeDtypeStruct(arrived.shape, BF),
             jax.ShapeDtypeStruct((1, width), F32),
         ],
-        compiler_params=params(1),
+        compiler_params=params(1, 58),
         name="back",
     )(jnp.append(source, core), *gradients, full_in, arrived, upstream, gain.reshape(1, width))
 
@@ -459,28 +459,22 @@
 
 
 def sum_everywhere(values):
-    steps = [("dp", bit) for bit in bits_of(lax.axis_size("dp"))] + [("tm", 0)]
-    pad = -values.shape[0] % (1 << len(steps))
-    rows = values.shape[0]
-    values = jnp.pad(values, ((0, pad), (0, 0)))
-    side = lambda axis, bit: (lax.axis_index(axis) >> bit) & 1
-    for axis, bit in steps:
-        halves = values.reshape(2, values.shape[0] // 2, values.shape[1])
-        mine = side(axis, bit)
-        send = lax.dynamic_index_in_dim(halves, 1 - mine, 0, keepdims=False)
-        keep = lax.dynamic_index_in_dim(halves, mine, 0, keepdims=False)
-        values = keep + lax.ppermute(send, axis, flip_bit(axis, bit))
+    for bit in bits_of(lax.axis_size("dp")):
+        values = values + lax.ppermute(values, "dp", flip_bit("dp", bit))
+    halves = values.reshape(2, values.shape[0] // 2, values.shape[1])
+    core = lax.axis_index("tm") % 2
+    send = lax.dynamic_index_in_dim(halves, 1 - core, 0, keepdims=False)
+    keep = lax.dynamic_index_in_dim(halves, core, 0, keepdims=False)
+    values = (keep + lax.ppermute(send, "tm", flip_bit("tm", 0))).astype(BF)
     terms = [values]
     for mask in range(2, lax.axis_size("tm"), 2):
         terms.append(lax.ppermute(values, "tm", flip("tm", mask)))
+    terms = [term.astype(F32) for term in terms]
     while len(terms) > 1:
         terms = [a + b for a, b in zip(terms[::2], terms[1::2])]
     values = terms[0]
-    for axis, bit in steps[::-1]:
-        got = lax.ppermute(values, axis, flip_bit(axis, bit))
-        first = side(axis, bit) == 0
-        values = jnp.concatenate([jnp.where(first, values, got), jnp.where(first, got, values)])
-    return values[:rows]
+    got = lax.ppermute(values, "tm", flip_bit("tm", 0))
+    return jnp.concatenate([jnp.where(core == 0, values, got), jnp.where(core == 0, got, values)])
 
 
 def sum_across(share):
@@ -554,7 +548,7 @@
             ],
         ),
         out_shape=[jax.ShapeDtypeStruct((h, width), BF) for h in (rows, RIM, RIM)],
-        compiler_params=params(1),
+        compiler_params=params(1, 58),
         name="depth",
     )(flags, glu, glu_low, glu_high, up_rows, up_low, up_high, kernel)
     kernel_term = pl.pallas_call(
@@ -567,7 +561,7 @@
             scratch_shapes=[padded_of(lane_block), pltpu.VMEM((taps + 1, 8, LANES), F32)],
         ),
         out_shape=jax.ShapeDtypeStruct((taps + 1, width), F32),
-        compiler_params=params(1),
+        compiler_params=params(1, 48),
         name="taps",
     )(flags, glu, glu_low, glu_high, grad_depth)
 

time: 291 us -> 452 us (1.55)
  Pallas kernels: 78.8 us -> 179 us
  waiting for transfers between devices: 118 us -> 177 us
    pallas_call x1, Pallas kernels: 2.27 us -> 97.1 us  [pick_panels(): pl.pallas_call(functools.partial(pick_body, count=count), grid_spec=pltpu...]
    ppermute x3, waiting for transfers between devices: 0.01 us -> 66.3 us  [sum_everywhere(): terms.append(lax.ppermute(values, 'tm', flip('tm', mask)))]
    ppermute x6 -> x4, waiting for transfers between devices: 9.16 us -> 5.67 us  [the longest x2 5.66 us: sum_everywhere(): values = values + lax.ppermute(values, 'dp', flip_bit('dp', bit))]
  transfers between devices with their start and end apart: 35 -> 33, of which waited for: 18 -> 17; matrix products, arithmetic and copies ran while one was open for 13% -> 9% of each run, Pallas kernels for 9% -> 6%
where the time goes in v4:
time: 452 us; the launch traced here: 450 us
  Pallas kernels  179 us (40%)
  waiting for transfers between devices  177 us (39%)
  starting transfers between devices  50 us (11%)
  other arithmetic  14.9 us (3%)
  local copies, waits for them, and re-layouts  14.7 us (3%)
  matrix products  13.5 us (3%)
    pallas_call x1, Pallas kernels, pick_panels(): pl.pallas_call(functools.partial(pick_body, count=count), grid_spec=pltpu...  97.1 us
    ppermute x3, waiting for transfers between devices, sum_everywhere(): terms.append(lax.ppermute(values, 'tm', flip('tm', mask)))  66.3 us
    ppermute x4, waiting for transfers between devices, gather_order(): got = lax.ppermute(have, 'dp', flip_bit('dp', bit))  37.2 us
    ppermute x4, waiting for transfers between devices, outer_halved(): got = lax.ppermute(send, 'dp', flip_bit('dp', bit))  29 us
    ppermute x3, waiting for transfers between devices, sum_across(): total = total + lax.ppermute(piece, 'tm', pairs).astype(F32)  23.5 us
    pallas_call x2, Pallas kernels, gated(): pl.pallas_call(functools.partial(gated_body, **sizes), grid_spec=pltpu.Pr...  16.4 us
    pallas_call x1, Pallas kernels, back(): pl.pallas_call(functools.partial(back_body, grads=len(gradients), block=b...  15.4 us
    pallas_call x2, Pallas kernels, put(): pl.pallas_call(body, grid_spec=pltpu.PrefetchScalarGridSpec(num_scalar_pr...  14.3 us
  transfers between devices with their start and end apart: 33, of which 17 were waited for; matrix products, arithmetic and copies ran while one was open for 9% of the time, Pallas kernels for 6%

profile of v4, /device:TPU:8, one launch (start us, length us, event | category | flops | bytes accessed | tf_op | source)
XLA Modules:
  0.0 450.2 jit_solution(2445380467001619448)
XLA Ops:
  1.9 97.1 %pick_panels.1 = bf16[8,128,1536]{2,1,0:T(8,128)(2,1)} custom-call(s32[8]{0:T(128)} %select_reduce_fusion.2.index, bf16[4,128,1536]{2,1,0:T(8,128)(2,1)} %bitcast.94), custom_call_target="tpu_custom_call" | custom-call | tf_op jit(solution)/shard_map/pick_panels/pallas_call | solution.py:50
  99.0 5.5 %all-to-all-start = ((bf16[8,128,1536]{2,1,0:T(8,128)(2,1)}), bf16[8,128,1536]{2,1,0:T(8,128)(2,1)}, u32[]{:S(2)}, u32[]{:S(2)}) async-start(bf16[8,128,1536]{2,1,0:T(8,128)(2,1)} %pick_panels.1), calls=%async_computation | async-start | bytes 6291456 | tf_op jit(solution)/shard_map/all_to_all | solution.py:514
  107.7 12.3 %collective-permute-done.7 = bf16[1,96,3072]{2,1,0:T(8,128)(2,1)S(1)} collective-permute-done((bf16[1,96,3072]{2,1,0:T(8,128)(2,1)S(1)}, bf16[1,96,3072]{2,1,0:T(8,128)(2,1)S(1)}, u32[]{:S(2)}, u32[]{:S(2)}) %collective-permute-start.7) | collective-permute-done | bytes 589856 | tf_op jit(solution)/shard_map/ppermute | solution.py:89
  123.5 23.8 %collective-permute-done.8 = bf16[2,96,3072]{2,1,0:T(8,128)(2,1)S(1)} collective-permute-done((bf16[2,96,3072]{2,1,0:T(8,128)(2,1)S(1)}, bf16[2,96,3072]{2,1,0:T(8,128)(2,1)S(1)}, u32[]{:S(2)}, u32[]{:S(2)}) %collective-permute-start.8) | collective-permute-done | bytes 1179680 | tf_op jit(solution)/shard_map/ppermute | solution.py:89
  157.8 3.6 collective-permute-done.1
  163.8 8.8 %collective-permute-done.2 = s32[2,2,4]{2,1,0:T(2,128)S(1)} collective-permute-done((s32[2,2,4]{2,1,0:T(2,128)S(1)}, s32[2,2,4]{2,1,0:T(2,128)S(1)}, u32[]{:S(2)}, u32[]{:S(2)}) %collective-permute-start.2) | collective-permute-done | bytes 96 | tf_op jit(solution)/shard_map/ppermute | solution.py:518
  177.7 6.3 %put_weights.2.rest_0_ = bf16[16,96,3072]{2,1,0:T(8,128)(2,1)} custom-call(s32[8]{0:T(128)S(1)} %stack.76._, bf16[4,96,3072]{2,1,0:T(8,128)(2,1)} %pad_maximum_fusion.a, bf16[4,96,3072]{2,1,0:T(8,128)(2,1)S(1)} %pad_maximum_fusion.1.b), custom_call_target="tpu_custom_call" | custom-call | tf_op jit(solution)/shard_map/put_weights/pallas_call | solution.py:131
  184.0 8.0 %put_weights.3 = bf16[16,96,3072]{2,1,0:T(8,128)(2,1)} custom-call(s32[8]{0:T(128)S(1)} %stack.67._, bf16[4,96,3072]{2,1,0:T(8,128)(2,1)} %collective-permute-done.6.a, bf16[4,96,3072]{2,1,0:T(8,128)(2,1)} %collective-permute-done.9.b, bf16[16,96,3072]{2,1,0:T(8,128)(2,1)} %put_weights.2.rest_0_), custom_call_target="tpu_custom_call", output_to_operand_aliasing={{}: (3, {})} | custom-call | tf_op jit(solution)/shard_map/put_weights/pallas_call | solution.py:131
  192.0 13.1 %forward.1 = (bf16[4,512,384]{2,1,0:T(8,128)(2,1)}, f32[512,1536]{1,0:T(8,128)}, f32[512,1536]{1,0:T(8,128)}, bf16[512,1536]{1,0:T(8,128)(2,1)}) custom-call(s32[5]{0:T(128)} %get-tuple-element.55.source, bf16[8,128,1536]{2,1,0:T(8,128)(2,1)} %all-to-all-done.x_hbm.refs_5_, f32[1,1536]{1,0:T(1,128)} %reshape.97.gain_ref.refs_7_, ...), custom_call_target="tpu_custom_call" | custom-call | tf_op jit(solution)/shard_map/forward/pallas_call | solution.py:189
  208.1 5.2 %collective-permute-start.11 = (bf16[32,1536]{1,0:T(8,128)(2,1)S(1)}, bf16[32,1536]{1,0:T(8,128)(2,1)S(1)}, u32[]{:S(2)}, u32[]{:S(2)}) collective-permute-start(bf16[32,1536]{1,0:T(8,128)(2,1)S(1)} %get-tuple-element.44), channel_id=1, source_target_pairs={{1,0},{2,1},{3,2},{4,3},{5,4},{6,5},{7,6},{9,8},{10,9},{11,10},{12... | collective-permute-start | bytes 294920 | tf_op jit(solution)/shard_map/ppermute | solution.py:494
  216.1 11.3 %depth.1 = (bf16[512,1536]{1,0:T(8,128)(2,1)}, bf16[16,1536]{1,0:T(8,128)(2,1)}, bf16[16,1536]{1,0:T(8,128)(2,1)}) custom-call(s32[8]{0:T(128)} %copy-done.6, bf16[512,1536]{1,0:T(8,128)(2,1)} %get-tuple-element.17.glu, bf16[32,1536]{1,0:T(8,128)(2,1)} %copy-done.2, bf16[32,1536]{1,0:T(8,128)(2,1)} %copy-done.4, bf16[512,1536]{1,0:T(8,128)(2,1)} %bitcast.92, ...), custom_call_target="tpu_custom_call" | custom-call | tf_op jit(solution)/shard_map/depth/pallas_call | solution.py:538
  227.4 8.0 %gated.3 = (bf16[512,768]{1,0:T(8,128)(2,1)}, bf16[512,768]{1,0:T(8,128)(2,1)}) custom-call(s32[9]{0:T(128)} %get-tuple-element.53.flags, bf16[512,1536]{1,0:T(8,128)(2,1)} %get-tuple-element.18.grad, bf16[16,1536]{1,0:T(8,128)(2,1)} %get-tuple-element.19.low, bf16[16,1536]{1,0:T(8,128)(2,1)} %get-tuple-element.20.high, f32[512,1536]{1,0:T(8,128)} %get-tuple-element.21.lin, ...), custom_call_target="tpu_custom_call" | custom-call | tf_op jit(solution)/shard_map/gated/pallas_call | solution.py:319
  235.5 8.4 %gated.2 = (bf16[512,768]{1,0:T(8,128)(2,1)}, bf16[512,768]{1,0:T(8,128)(2,1)}) custom-call(s32[9]{0:T(128)} %get-tuple-element.54.flags, bf16[512,1536]{1,0:T(8,128)(2,1)} %get-tuple-element.18.grad, bf16[16,1536]{1,0:T(8,128)(2,1)} %get-tuple-element.19.low, bf16[16,1536]{1,0:T(8,128)(2,1)} %get-tuple-element.20.high, f32[512,1536]{1,0:T(8,128)} %get-tuple-element.21.lin, ...), custom_call_target="tpu_custom_call" | custom-call | tf_op jit(solution)/shard_map/gated/pallas_call | solution.py:319
  243.9 8.8 %taps.1 = f32[32,1536]{1,0:T(8,128)S(1)} custom-call(s32[8]{0:T(128)S(1)} %copy-done.7, bf16[512,1536]{1,0:T(8,128)(2,1)S(1)} %copy-done.1, bf16[32,1536]{1,0:T(8,128)(2,1)S(1)} %copy-done.3, bf16[32,1536]{1,0:T(8,128)(2,1)S(1)} %copy-done.5, bf16[512,1536]{1,0:T(8,128)(2,1)S(1)} %copy-done), custom_call_target="tpu_custom_call" | custom-call | tf_op jit(solution)/shard_map/taps/pallas_call | solution.py:554
  252.7 15.4 %back.1 = (bf16[8,128,1536]{2,1,0:T(8,128)(2,1)}, f32[1,1536]{1,0:T(1,128)}) custom-call(s32[5]{0:T(128)} %get-tuple-element.56.source, bf16[512,768]{1,0:T(8,128)(2,1)} %get-tuple-element.23.refs_0_, bf16[512,768]{1,0:T(8,128)(2,1)} %get-tuple-element.24.refs_1_, bf16[512,768]{1,0:T(8,128)(2,1)} %get-tuple-element.25.refs_2_, ...), custom_call_target="tpu_custom_call" | custom-call | tf_op jit(solution)/shard_map/back/pallas_call | solution.py:404
  270.7 5.7 %collective-permute-done.24 = f32[32,1536]{1,0:T(8,128)S(1)} collective-permute-done((f32[32,1536]{1,0:T(8,128)S(1)}, f32[32,1536]{1,0:T(8,128)S(1)}, u32[]{:S(2)}, u32[]{:S(2)}) %collective-permute-start.24) | collective-permute-done | bytes 196640 | tf_op jit(solution)/shard_map/ppermute | solution.py:463
  281.6 4.6 %all-to-all-start.1 = ((bf16[8,128,1536]{2,1,0:T(8,128)(2,1)}), bf16[8,128,1536]{2,1,0:T(8,128)(2,1)S(1)}, u32[]{:S(2)}, u32[]{:S(2)}) async-start(bf16[8,128,1536]{2,1,0:T(8,128)(2,1)} %get-tuple-element.27), calls=%async_computation.1 | async-start | bytes 6291456 | tf_op jit(solution)/shard_map/all_to_all | solution.py:586
  294.2 45.4 %collective-permute-done.27 = bf16[16,1536]{1,0:T(8,128)(2,1)S(1)} collective-permute-done((bf16[16,1536]{1,0:T(8,128)(2,1)S(1)}, bf16[16,1536]{1,0:T(8,128)(2,1)S(1)}, u32[]{:S(2)}, u32[]{:S(2)}) %collective-permute-start.27) | collective-permute-done | bytes 49184 | tf_op jit(solution)/shard_map/ppermute | solution.py:471
  339.6 17.8 %collective-permute-done.28 = bf16[16,1536]{1,0:T(8,128)(2,1)S(1)} collective-permute-done((bf16[16,1536]{1,0:T(8,128)(2,1)S(1)}, bf16[16,1536]{1,0:T(8,128)(2,1)S(1)}, u32[]{:S(2)}, u32[]{:S(2)}) %collective-permute-start.28) | collective-permute-done | bytes 49184 | tf_op jit(solution)/shard_map/ppermute | solution.py:471
  374.8 18.4 %collective-permute-done.19 = bf16[2,384,768]{2,1,0:T(8,128)(2,1)S(1)} collective-permute-done((bf16[2,384,768]{2,1,0:T(8,128)(2,1)S(1)}, bf16[2,384,768]{2,1,0:T(8,128)(2,1)S(1)}, u32[]{:S(2)}, u32[]{:S(2)}) %collective-permute-start.19) | collective-permute-done | bytes 1179680 | tf_op jit(solution)/shard_map/ppermute | solution.py:451
  399.4 9.2 %collective-permute-done.20 = bf16[1,384,768]{2,1,0:T(8,128)(2,1)S(1)} collective-permute-done((bf16[1,384,768]{2,1,0:T(8,128)(2,1)S(1)}, bf16[1,384,768]{2,1,0:T(8,128)(2,1)S(1)}, u32[]{:S(2)}, u32[]{:S(2)}) %collective-permute-start.20) | collective-permute-done | bytes 589856 | tf_op jit(solution)/shard_map/ppermute | solution.py:451
  423.4 6.5 %collective-permute-done.21 = bf16[384,384]{1,0:T(8,128)(2,1)S(1)} collective-permute-done((bf16[384,384]{1,0:T(8,128)(2,1)S(1)}, bf16[384,384]{1,0:T(8,128)(2,1)S(1)}, u32[]{:S(2)}, u32[]{:S(2)}) %collective-permute-start.21) | collective-permute-done | bytes 294944 | tf_op jit(solution)/shard_map/ppermute | solution.py:487
  429.9 10.6 %collective-permute-done.22 = bf16[384,384]{1,0:T(8,128)(2,1)S(1)} collective-permute-done((bf16[384,384]{1,0:T(8,128)(2,1)S(1)}, bf16[384,384]{1,0:T(8,128)(2,1)S(1)}, u32[]{:S(2)}, u32[]{:S(2)}) %collective-permute-start.22) | collective-permute-done | bytes 294944 | tf_op jit(solution)/shard_map/ppermute | solution.py:487
  440.5 6.4 %collective-permute-done.23 = bf16[384,384]{1,0:T(8,128)(2,1)S(1)} collective-permute-done((bf16[384,384]{1,0:T(8,128)(2,1)S(1)}, bf16[384,384]{1,0:T(8,128)(2,1)S(1)}, u32[]{:S(2)}, u32[]{:S(2)}) %collective-permute-start.23) | collective-permute-done | bytes 294944 | tf_op jit(solution)/shard_map/ppermute | solution.py:487
  (154 shorter events, 88.8 us)
Async XLA Ops:
  99.0 93.0 %all-to-all-start = ((bf16[8,128,1536]{2,1,0:T(8,128)(2,1)}), bf16[8,128,1536]{2,1,0:T(8,128)(2,1)}, u32[]{:S(2)}, u32[]{:S(2)}) async-start(bf16[8,128,1536]{2,1,0:T(8,128)(2,1)} %pick_panels.1), calls=%async_computation | async-start | bytes 6291456 | tf_op jit(solution)/shard_map/all_to_all | solution.py:514
  104.6 15.4 %collective-permute-start.7 = (bf16[1,96,3072]{2,1,0:T(8,128)(2,1)S(1)}, bf16[1,96,3072]{2,1,0:T(8,128)(2,1)S(1)}, u32[]{:S(2)}, u32[]{:S(2)}) collective-permute-start(bf16[1,96,3072]{2,1,0:T(8,128)(2,1)S(1)} %get-tuple-element.32), channel_id=1, source_target_pairs={{0,16},{8,24},{16,0},{24,8},{1,17},{9,25},{17,1},{25,9},{2,18},{10... | collective-permute-start | bytes 1769480 | tf_op jit(solution)/shard_map/ppermute | solution.py:89
  106.2 15.5 %collective-permute-start.4 = (bf16[1,96,3072]{2,1,0:T(8,128)(2,1)S(1)}, bf16[1,96,3072]{2,1,0:T(8,128)(2,1)S(1)}, u32[]{:S(2)}, u32[]{:S(2)}) collective-permute-start(bf16[1,96,3072]{2,1,0:T(8,128)(2,1)S(1)} %get-tuple-element.33), channel_id=1, source_target_pairs={{0,8},{8,0},{16,24},{24,16},{1,9},{9,1},{17,25},{25,17},{2,10},{10... | collective-permute-start | bytes 1769480 | tf_op jit(solution)/shard_map/ppermute | solution.py:89
  120.1 27.2 %collective-permute-start.8 = (bf16[2,96,3072]{2,1,0:T(8,128)(2,1)S(1)}, bf16[2,96,3072]{2,1,0:T(8,128)(2,1)S(1)}, u32[]{:S(2)}, u32[]{:S(2)}) collective-permute-start(bf16[2,96,3072]{2,1,0:T(8,128)(2,1)S(1)} %pad_maximum_fusion.3), channel_id=1, source_target_pairs={{0,8},{8,0},{16,24},{24,16},{1,9},{9,1},{17,25},{25,17},{2,10},{10... | collective-permute-start | bytes 3538952 | tf_op jit(solution)/shard_map/ppermute | solution.py:89
  121.8 26.9 %collective-permute-start.5 = (bf16[2,96,3072]{2,1,0:T(8,128)(2,1)S(1)}, bf16[2,96,3072]{2,1,0:T(8,128)(2,1)S(1)}, u32[]{:S(2)}, u32[]{:S(2)}) collective-permute-start(bf16[2,96,3072]{2,1,0:T(8,128)(2,1)S(1)} %pad_maximum_fusion.2), channel_id=1, source_target_pairs={{0,16},{8,24},{16,0},{24,8},{1,17},{9,25},{17,1},{25,9},{2,18},{10... | collective-permute-start | bytes 3538952 | tf_op jit(solution)/shard_map/ppermute | solution.py:89
  123.4 34.2 %collective-permute-start = (s32[1,2,4]{2,1,0:T(2,128)S(1)}, s32[1,2,4]{2,1,0:T(2,128)S(1)}, u32[]{:S(2)}, u32[]{:S(2)}) collective-permute-start(s32[1,2,4]{2,1,0:T(2,128)S(1)} %add_bitcast_fusion), channel_id=1, source_target_pairs={{0,1},{1,0},{2,3},{3,2},{4,5},{5,4},{6,7},{7,6},{8,9},{9,8},{10,11... | collective-permute-start | bytes 104 | tf_op jit(solution)/shard_map/ppermute | solution.py:517
  147.6 36.4 %collective-permute-start.9 = (bf16[4,96,3072]{2,1,0:T(8,128)(2,1)S(1)}, bf16[4,96,3072]{2,1,0:T(8,128)(2,1)}, u32[]{:S(2)}, u32[]{:S(2)}) collective-permute-start(bf16[4,96,3072]{2,1,0:T(8,128)(2,1)S(1)} %pad_maximum_fusion.1.b), channel_id=1, source_target_pairs={{0,1},{1,0},{2,3},{3,2},{4,5},{5,4},{6,7},{7,6},{8,9},{9,8},{10,11... | collective-permute-start | bytes 7077896 | tf_op jit(solution)/shard_map/ppermute | solution.py:105
  150.4 33.6 %collective-permute-start.6 = (bf16[4,96,3072]{2,1,0:T(8,128)(2,1)}, bf16[4,96,3072]{2,1,0:T(8,128)(2,1)}, u32[]{:S(2)}, u32[]{:S(2)}) collective-permute-start(bf16[4,96,3072]{2,1,0:T(8,128)(2,1)} %pad_maximum_fusion.a), channel_id=1, source_target_pairs={{0,1},{1,0},{2,3},{3,2},{4,5},{5,4},{6,7},{7,6},{8,9},{9,8},{10,11... | collective-permute-start | bytes 7077896 | tf_op jit(solution)/shard_map/ppermute | solution.py:104
  151.3 62.6 %collective-permute-start.12 = (bf16[16,1536]{1,0:T(8,128)(2,1)S(1)}, bf16[16,1536]{1,0:T(8,128)(2,1)S(1)}, u32[]{:S(2)}, u32[]{:S(2)}) collective-permute-start(bf16[16,1536]{1,0:T(8,128)(2,1)S(1)} %get-tuple-element.43), channel_id=1, source_target_pairs={{0,1},{1,2},{2,3},{3,4},{4,5},{5,6},{6,7},{8,9},{9,10},{10,11},{11... | collective-permute-start | bytes 147464 | tf_op jit(solution)/shard_map/ppermute | solution.py:493
  153.7 60.2 %collective-permute-start.13 = (bf16[16,1536]{1,0:T(8,128)(2,1)S(1)}, bf16[16,1536]{1,0:T(8,128)(2,1)S(1)}, u32[]{:S(2)}, u32[]{:S(2)}) collective-permute-start(bf16[16,1536]{1,0:T(8,128)(2,1)S(1)} %get-tuple-element.42), channel_id=1, source_target_pairs={{1,0},{2,1},{3,2},{4,3},{5,4},{6,5},{7,6},{9,8},{10,9},{11,10},{12... | collective-permute-start | bytes 147464 | tf_op jit(solution)/shard_map/ppermute | solution.py:494
  270.3 90.3 %collective-permute-start.14 = (bf16[4,512,384]{2,1,0:T(8,128)(2,1)}, bf16[4,512,384]{2,1,0:T(8,128)(2,1)}, u32[]{:S(2)}, u32[]{:S(2)}) collective-permute-start(bf16[4,512,384]{2,1,0:T(8,128)(2,1)} %get-tuple-element.28), channel_id=1, source_target_pairs={{0,1},{1,0},{2,3},{3,2},{4,5},{5,4},{6,7},{7,6},{8,9},{9,8},{10,11... | collective-permute-start | bytes 4718600 | tf_op jit(solution)/shard_map/ppermute | solution.py:529
  281.6 79.0 %collective-permute-start.18 = (bf16[512,768]{1,0:T(8,128)(2,1)}, bf16[512,768]{1,0:T(8,128)(2,1)}, u32[]{:S(2)}, u32[]{:S(2)}) collective-permute-start(bf16[512,768]{1,0:T(8,128)(2,1)} %get-tuple-element.26.refs_3_), channel_id=1, source_target_pairs={{0,1},{1,0},{2,3},{3,2},{4,5},{5,4},{6,7},{7,6},{8,9},{9,8},{10,11... | collective-permute-start | bytes 2359304 | tf_op jit(solution)/shard_map/ppermute | solution.py:572
  281.6 166.3 %all-to-all-start.1 = ((bf16[8,128,1536]{2,1,0:T(8,128)(2,1)}), bf16[8,128,1536]{2,1,0:T(8,128)(2,1)S(1)}, u32[]{:S(2)}, u32[]{:S(2)}) async-start(bf16[8,128,1536]{2,1,0:T(8,128)(2,1)} %get-tuple-element.27), calls=%async_computation.1 | async-start | bytes 6291456 | tf_op jit(solution)/shard_map/all_to_all | solution.py:586
  289.8 49.8 %collective-permute-start.27 = (bf16[16,1536]{1,0:T(8,128)(2,1)S(1)}, bf16[16,1536]{1,0:T(8,128)(2,1)S(1)}, u32[]{:S(2)}, u32[]{:S(2)}) collective-permute-start(bf16[16,1536]{1,0:T(8,128)(2,1)S(1)} %fusion.26), channel_id=1, source_target_pairs={{0,2},{1,3},{2,0},{3,1},{4,6},{5,7},{6,4},{7,5},{8,10},{9,11},{10,... | collective-permute-start | bytes 147464 | tf_op jit(solution)/shard_map/ppermute | solution.py:471
  290.2 67.1 %collective-permute-start.28 = (bf16[16,1536]{1,0:T(8,128)(2,1)S(1)}, bf16[16,1536]{1,0:T(8,128)(2,1)S(1)}, u32[]{:S(2)}, u32[]{:S(2)}) collective-permute-start(bf16[16,1536]{1,0:T(8,128)(2,1)S(1)} %fusion.26), channel_id=1, source_target_pairs={{0,4},{1,5},{2,6},{3,7},{4,0},{5,1},{6,2},{7,3},{8,12},{9,13},{10,... | collective-permute-start | bytes 147464 | tf_op jit(solution)/shard_map/ppermute | solution.py:471
  292.8 67.7 %collective-permute-start.29 = (bf16[16,1536]{1,0:T(8,128)(2,1)S(1)}, bf16[16,1536]{1,0:T(8,128)(2,1)S(1)}, u32[]{:S(2)}, u32[]{:S(2)}) collective-permute-start(bf16[16,1536]{1,0:T(8,128)(2,1)S(1)} %fusion.26), channel_id=1, source_target_pairs={{0,6},{1,7},{2,4},{3,5},{4,2},{5,3},{6,0},{7,1},{8,14},{9,15},{10,... | collective-permute-start | bytes 147464 | tf_op jit(solution)/shard_map/ppermute | solution.py:471
  339.6 27.4 %collective-permute-start.15 = (bf16[512,768]{1,0:T(8,128)(2,1)S(1)}, bf16[512,768]{1,0:T(8,128)(2,1)S(1)}, u32[]{:S(2)}, u32[]{:S(2)}) collective-permute-start(bf16[512,768]{1,0:T(8,128)(2,1)S(1)} %copy-done.14), channel_id=1, source_target_pairs={{0,1},{1,0},{2,3},{3,2},{4,5},{5,4},{6,7},{7,6},{8,9},{9,8},{10,11... | collective-permute-start | bytes 2359304 | tf_op jit(solution)/shard_map/ppermute | solution.py:572
  360.5 38.9 %collective-permute-start.30 = (f32[16,1536]{1,0:T(8,128)S(1)}, f32[16,1536]{1,0:T(8,128)S(1)}, u32[]{:S(2)}, u32[]{:S(2)}) collective-permute-start(f32[16,1536]{1,0:T(8,128)S(1)} %add_add_fusion), channel_id=1, source_target_pairs={{0,1},{1,0},{2,3},{3,2},{4,5},{5,4},{6,7},{7,6},{8,9},{9,8},{10,11... | collective-permute-start | bytes 294920 | tf_op jit(solution)/shard_map/ppermute | solution.py:476
  364.8 28.4 %collective-permute-start.19 = (bf16[2,384,768]{2,1,0:T(8,128)(2,1)S(1)}, bf16[2,384,768]{2,1,0:T(8,128)(2,1)S(1)}, u32[]{:S(2)}, u32[]{:S(2)}) collective-permute-start(bf16[2,384,768]{2,1,0:T(8,128)(2,1)S(1)} %add_convert_fusion), channel_id=1, source_target_pairs={{0,16},{8,24},{16,0},{24,8},{1,17},{9,25},{17,1},{25,9},{2,18},{10... | collective-permute-start | bytes 3538952 | tf_op jit(solution)/shard_map/ppermute | solution.py:451
  367.9 28.5 %collective-permute-start.16 = (bf16[2,384,768]{2,1,0:T(8,128)(2,1)S(1)}, bf16[2,384,768]{2,1,0:T(8,128)(2,1)S(1)}, u32[]{:S(2)}, u32[]{:S(2)}) collective-permute-start(bf16[2,384,768]{2,1,0:T(8,128)(2,1)S(1)} %add_convert_fusion.2), channel_id=1, source_target_pairs={{0,8},{8,0},{16,24},{24,16},{1,9},{9,1},{17,25},{25,17},{2,10},{10... | collective-permute-start | bytes 3538952 | tf_op jit(solution)/shard_map/ppermute | solution.py:451
  393.3 15.3 %collective-permute-start.20 = (bf16[1,384,768]{2,1,0:T(8,128)(2,1)S(1)}, bf16[1,384,768]{2,1,0:T(8,128)(2,1)S(1)}, u32[]{:S(2)}, u32[]{:S(2)}) collective-permute-start(bf16[1,384,768]{2,1,0:T(8,128)(2,1)S(1)} %add_convert_fusion.5), channel_id=1, source_target_pairs={{0,8},{8,0},{16,24},{24,16},{1,9},{9,1},{17,25},{25,17},{2,10},{10... | collective-permute-start | bytes 1769480 | tf_op jit(solution)/shard_map/ppermute | solution.py:451
  397.6 14.6 %collective-permute-start.17 = (bf16[1,384,768]{2,1,0:T(8,128)(2,1)}, bf16[1,384,768]{2,1,0:T(8,128)(2,1)}, u32[]{:S(2)}, u32[]{:S(2)}) collective-permute-start(bf16[1,384,768]{2,1,0:T(8,128)(2,1)} %add_convert_fusion.8), channel_id=1, source_target_pairs={{0,16},{8,24},{16,0},{24,8},{1,17},{9,25},{17,1},{25,9},{2,18},{10... | collective-permute-start | bytes 1769480 | tf_op jit(solution)/shard_map/ppermute | solution.py:451
  419.6 21.0 %collective-permute-start.22 = (bf16[384,384]{1,0:T(8,128)(2,1)S(1)}, bf16[384,384]{1,0:T(8,128)(2,1)S(1)}, u32[]{:S(2)}, u32[]{:S(2)}) collective-permute-start(bf16[384,384]{1,0:T(8,128)(2,1)S(1)} %get-tuple-element.48), channel_id=1, source_target_pairs={{0,4},{1,5},{2,6},{3,7},{4,0},{5,1},{6,2},{7,3},{8,12},{9,13},{10,... | collective-permute-start | bytes 884744 | tf_op jit(solution)/shard_map/ppermute | solution.py:487
  420.5 26.5 %collective-permute-start.23 = (bf16[384,384]{1,0:T(8,128)(2,1)S(1)}, bf16[384,384]{1,0:T(8,128)(2,1)S(1)}, u32[]{:S(2)}, u32[]{:S(2)}) collective-permute-start(bf16[384,384]{1,0:T(8,128)(2,1)S(1)} %get-tuple-element.47), channel_id=1, source_target_pairs={{0,6},{1,7},{2,4},{3,5},{4,2},{5,3},{6,0},{7,1},{8,14},{9,15},{10,... | collective-permute-start | bytes 884744 | tf_op jit(solution)/shard_map/ppermute | solution.py:487
  (30 other events, 257.4 us)

commit v5 on v4

--- a/solution.py
+++ b/solution.py
@@ -46,18 +46,17 @@
 
 def pick_panels(source, index, count):
     _, rows, width = source.shape
-    hbm = pl.BlockSpec(memory_space=pltpu.HBM)
     return pl.pallas_call(
         functools.partial(pick_body, count=count),
         grid_spec=pltpu.PrefetchScalarGridSpec(
             num_scalar_prefetch=1,
             grid=(1,),
-            in_specs=[hbm],
-            out_specs=hbm,
+            in_specs=[pl.BlockSpec(source.shape, lambda i, idx: (0, 0, 0))],
+            out_specs=pl.BlockSpec(memory_space=pltpu.HBM),
             scratch_shapes=[pltpu.SemaphoreType.DMA((count,))],
         ),
         out_shape=jax.ShapeDtypeStruct((count, rows, width), source.dtype),
-        compiler_params=params(1, 58),
+        compiler_params=params(1, 48),
         name="pick_panels",
     )(index, source)
 
@@ -77,7 +76,7 @@
             out_specs=pl.BlockSpec((1, rows, width), lambda i, idx: (i, 0, 0)),
         ),
         out_shape=jax.ShapeDtypeStruct((count, rows, width), source.dtype),
-        compiler_params=params(1, 8),
+        compiler_params=params(1, 48),
         name="pick_blocks",
     )(index, source)
 
@@ -210,7 +209,7 @@
             ],
         ),
         out_shape=[parts, wide(F32), wide(F32), wide(BF)],
-        compiler_params=params(1, 58),
+        compiler_params=params(1, 48),
         name="forward",
     )(jnp.append(source, lax.axis_index("dp")), arrived, gain.reshape(1, width), full_in, full_in)
 
@@ -328,7 +327,7 @@
             ],
         ),
         out_shape=shapes,
-        compiler_params=params(1, 58),
+        compiler_params=params(1, 48),
         name="gated",
     )(jnp.append(flags, parity), grad_depth, low, high, lin, gate, kernel)
 
@@ -426,7 +425,7 @@
             jax.ShapeDtypeStruct(arrived.shape, BF),
             jax.ShapeDtypeStruct((1, width), F32),
         ],
-        compiler_params=params(1, 58),
+        compiler_params=params(1, 48),
         name="back",
     )(jnp.append(source, core), *gradients, full_in, arrived, upstream, gain.reshape(1, width))
 
@@ -548,7 +547,7 @@
             ],
         ),
         out_shape=[jax.ShapeDtypeStruct((h, width), BF) for h in (rows, RIM, RIM)],
-        compiler_params=params(1, 58),
+        compiler_params=params(1, 48),
         name="depth",
     )(flags, glu, glu_low, glu_high, up_rows, up_low, up_high, kernel)
     kernel_term = pl.pallas_call(

time: 452 us -> 349 us (0.77)
  Pallas kernels: 179 us -> 78.8 us
    pallas_call x1, Pallas kernels: 97.1 us -> 2.25 us  [pick_panels(): pl.pallas_call(functools.partial(pick_body, count=count), grid_spec=pltpu...]
  transfers between devices with their start and end apart: 33 -> 33, of which waited for: 17 -> 18; matrix products, arithmetic and copies ran while one was open for 9% -> 11% of each run, Pallas kernels for 6% -> 8%
where the time goes in v5:
time: 349 us; the launch traced here: 348 us
  waiting for transfers between devices  178 us (51%)
  Pallas kernels  78.8 us (23%)
  starting transfers between devices  50.3 us (14%)
  local copies, waits for them, and re-layouts  13.9 us (4%)
  matrix products  13.5 us (4%)
  other arithmetic  11.9 us (3%)
    ppermute x3, waiting for transfers between devices, sum_everywhere(): terms.append(lax.ppermute(values, 'tm', flip('tm', mask)))  66.3 us
    ppermute x4, waiting for transfers between devices, gather_order(): got = lax.ppermute(have, 'dp', flip_bit('dp', bit))  37.2 us
    ppermute x4, waiting for transfers between devices, outer_halved(): got = lax.ppermute(send, 'dp', flip_bit('dp', bit))  28.9 us
    ppermute x3, waiting for transfers between devices, sum_across(): total = total + lax.ppermute(piece, 'tm', pairs).astype(F32)  23.5 us
    pallas_call x2, Pallas kernels, gated(): pl.pallas_call(functools.partial(gated_body, **sizes), grid_spec=pltpu.Pr...  14.8 us
    ppermute x3, waiting for transfers between devices, local(): lax.ppermute(tags, 'tm', flip('tm', i))  14.5 us
    pallas_call x2, Pallas kernels, put(): pl.pallas_call(body, grid_spec=pltpu.PrefetchScalarGridSpec(num_scalar_pr...  14.3 us
    pallas_call x1, Pallas kernels, back(): pl.pallas_call(functools.partial(back_body, grads=len(gradients), block=b...  14.3 us
  transfers between devices with their start and end apart: 33, of which 18 were waited for; matrix products, arithmetic and copies ran while one was open for 11% of the time, Pallas kernels for 8%

profile of v5, /device:TPU:8, one launch (start us, length us, event | category | flops | bytes accessed | tf_op | source)
XLA Modules:
  0.0 347.5 jit_solution(7191229262727402411)
XLA Ops:
  5.1 5.5 %all-to-all-start = ((bf16[8,128,1536]{2,1,0:T(8,128)(2,1)}), bf16[8,128,1536]{2,1,0:T(8,128)(2,1)}, u32[]{:S(2)}, u32[]{:S(2)}) async-start(bf16[8,128,1536]{2,1,0:T(8,128)(2,1)} %pick_panels.1), calls=%async_computation | async-start | bytes 6291456 | tf_op jit(solution)/shard_map/all_to_all | solution.py:513
  13.7 12.3 %collective-permute-done.7 = bf16[1,96,3072]{2,1,0:T(8,128)(2,1)S(1)} collective-permute-done((bf16[1,96,3072]{2,1,0:T(8,128)(2,1)S(1)}, bf16[1,96,3072]{2,1,0:T(8,128)(2,1)S(1)}, u32[]{:S(2)}, u32[]{:S(2)}) %collective-permute-start.7) | collective-permute-done | bytes 589856 | tf_op jit(solution)/shard_map/ppermute | solution.py:88
  29.5 23.8 %collective-permute-done.8 = bf16[2,96,3072]{2,1,0:T(8,128)(2,1)S(1)} collective-permute-done((bf16[2,96,3072]{2,1,0:T(8,128)(2,1)S(1)}, bf16[2,96,3072]{2,1,0:T(8,128)(2,1)S(1)}, u32[]{:S(2)}, u32[]{:S(2)}) %collective-permute-start.8) | collective-permute-done | bytes 1179680 | tf_op jit(solution)/shard_map/ppermute | solution.py:88
  59.7 3.1 collective-permute-start.13
  63.2 3.6 %collective-permute-done.1 = s32[2,2,4]{2,1,0:T(2,128)S(1)} collective-permute-done((s32[2,2,4]{2,1,0:T(2,128)S(1)}, s32[2,2,4]{2,1,0:T(2,128)S(1)}, u32[]{:S(2)}, u32[]{:S(2)}) %collective-permute-start.1) | collective-permute-done | bytes 96 | tf_op jit(solution)/shard_map/ppermute | solution.py:517
  69.3 9.4 %collective-permute-done.2 = s32[2,2,4]{2,1,0:T(2,128)S(1)} collective-permute-done((s32[2,2,4]{2,1,0:T(2,128)S(1)}, s32[2,2,4]{2,1,0:T(2,128)S(1)}, u32[]{:S(2)}, u32[]{:S(2)}) %collective-permute-start.2) | collective-permute-done | bytes 96 | tf_op jit(solution)/shard_map/ppermute | solution.py:517
  83.2 6.3 %put_weights.2.rest_0_ = bf16[16,96,3072]{2,1,0:T(8,128)(2,1)} custom-call(s32[8]{0:T(128)S(1)} %stack.76._, bf16[4,96,3072]{2,1,0:T(8,128)(2,1)} %pad_maximum_fusion.a, bf16[4,96,3072]{2,1,0:T(8,128)(2,1)S(1)} %pad_maximum_fusion.1.b), custom_call_target="tpu_custom_call" | custom-call | tf_op jit(solution)/shard_map/put_weights/pallas_call | solution.py:130
  89.5 8.0 %put_weights.3 = bf16[16,96,3072]{2,1,0:T(8,128)(2,1)} custom-call(s32[8]{0:T(128)S(1)} %stack.67._, bf16[4,96,3072]{2,1,0:T(8,128)(2,1)} %collective-permute-done.6.a, bf16[4,96,3072]{2,1,0:T(8,128)(2,1)} %collective-permute-done.9.b, bf16[16,96,3072]{2,1,0:T(8,128)(2,1)} %put_weights.2.rest_0_), custom_call_target="tpu_custom_call", output_to_operand_aliasing={{}: (3, {})} | custom-call | tf_op jit(solution)/shard_map/put_weights/pallas_call | solution.py:130
  97.5 12.4 %forward.1 = (bf16[4,512,384]{2,1,0:T(8,128)(2,1)}, f32[512,1536]{1,0:T(8,128)}, f32[512,1536]{1,0:T(8,128)}, bf16[512,1536]{1,0:T(8,128)(2,1)S(1)}) custom-call(s32[5]{0:T(128)S(1)} %get-tuple-element.55.source, bf16[8,128,1536]{2,1,0:T(8,128)(2,1)} %all-to-all-done.x_hbm.refs_5_, f32[1,1536]{1,0:T(1,128)S(1)} %reshape.97.gain_ref.refs_7_, ...), custom_call_target="tpu_custom_call" | custom-call | tf_op jit(solution)/shard_map/forward/pallas_call | solution.py:188
  111.9 5.4 %collective-permute-start.11 = (bf16[32,1536]{1,0:T(8,128)(2,1)S(1)}, bf16[32,1536]{1,0:T(8,128)(2,1)S(1)}, u32[]{:S(2)}, u32[]{:S(2)}) collective-permute-start(bf16[32,1536]{1,0:T(8,128)(2,1)S(1)} %get-tuple-element.44), channel_id=1, source_target_pairs={{1,0},{2,1},{3,2},{4,3},{5,4},{6,5},{7,6},{9,8},{10,9},{11,10},{12... | collective-permute-start | bytes 294920 | tf_op jit(solution)/shard_map/ppermute | solution.py:493
  119.2 9.7 %depth.1 = (bf16[512,1536]{1,0:T(8,128)(2,1)S(1)}, bf16[16,1536]{1,0:T(8,128)(2,1)S(1)}, bf16[16,1536]{1,0:T(8,128)(2,1)S(1)}) custom-call(s32[8]{0:T(128)S(1)} %add_convert_fusion.10.flags, bf16[512,1536]{1,0:T(8,128)(2,1)S(1)} %get-tuple-element.17.glu, bf16[32,1536]{1,0:T(8,128)(2,1)S(1)} %collective-permute-done.10.low, ...), custom_call_target="tpu_custom_call" | custom-call | tf_op jit(solution)/shard_map/depth/pallas_call | solution.py:537
  128.9 7.7 %gated.3 = (bf16[512,768]{1,0:T(8,128)(2,1)S(1)}, bf16[512,768]{1,0:T(8,128)(2,1)}) custom-call(s32[9]{0:T(128)S(1)} %get-tuple-element.53.flags, bf16[512,1536]{1,0:T(8,128)(2,1)S(1)} %get-tuple-element.18.grad, bf16[16,1536]{1,0:T(8,128)(2,1)S(1)} %get-tuple-element.19.low, bf16[16,1536]{1,0:T(8,128)(2,1)S(1)} %get-tuple-element.20.high, ...), custom_call_target="tpu_custom_call" | custom-call | tf_op jit(solution)/shard_map/gated/pallas_call | solution.py:318
  136.7 7.0 %gated.2 = (bf16[512,768]{1,0:T(8,128)(2,1)S(1)}, bf16[512,768]{1,0:T(8,128)(2,1)S(1)}) custom-call(s32[9]{0:T(128)S(1)} %get-tuple-element.54.flags, bf16[512,1536]{1,0:T(8,128)(2,1)S(1)} %get-tuple-element.18.grad, bf16[16,1536]{1,0:T(8,128)(2,1)S(1)} %get-tuple-element.19.low, bf16[16,1536]{1,0:T(8,128)(2,1)S(1)} %get-tuple-element.20.high, ...), custom_call_target="tpu_custom_call" | custom-call | tf_op jit(solution)/shard_map/gated/pallas_call | solution.py:318
  143.8 8.8 %taps.1 = f32[32,1536]{1,0:T(8,128)S(1)} custom-call(s32[8]{0:T(128)S(1)} %add_convert_fusion.10.flags, bf16[512,1536]{1,0:T(8,128)(2,1)S(1)} %get-tuple-element.17.glu, bf16[32,1536]{1,0:T(8,128)(2,1)S(1)} %collective-permute-done.10.low, bf16[32,1536]{1,0:T(8,128)(2,1)S(1)} %collective-permute-done.11.high, bf16[512,1536]{1,0:T(8,128)(2,1)S(1)} %get-tuple-element.18.grad), custom_call_target="tpu_custom_call" | custom-call | tf_op jit(solution)/shard_map/taps/pallas_call | solution.py:553
  152.6 14.3 %back.1 = (bf16[8,128,1536]{2,1,0:T(8,128)(2,1)}, f32[1,1536]{1,0:T(1,128)S(1)}) custom-call(s32[5]{0:T(128)S(1)} %get-tuple-element.56.source, bf16[512,768]{1,0:T(8,128)(2,1)S(1)} %get-tuple-element.23.refs_0_, bf16[512,768]{1,0:T(8,128)(2,1)S(1)} %get-tuple-element.24.refs_1_, bf16[512,768]{1,0:T(8,128)(2,1)S(1)} %get-tuple-element.25.refs_2_, ...), custom_call_target="tpu_custom_call" | custom-call | tf_op jit(solution)/shard_map/back/pallas_call | solution.py:403
  168.8 5.6 %collective-permute-done.24 = f32[32,1536]{1,0:T(8,128)S(1)} collective-permute-done((f32[32,1536]{1,0:T(8,128)S(1)}, f32[32,1536]{1,0:T(8,128)S(1)}, u32[]{:S(2)}, u32[]{:S(2)}) %collective-permute-start.24) | collective-permute-done | bytes 196640 | tf_op jit(solution)/shard_map/ppermute | solution.py:462
  179.0 4.7 %all-to-all-start.1 = ((bf16[8,128,1536]{2,1,0:T(8,128)(2,1)}), bf16[8,128,1536]{2,1,0:T(8,128)(2,1)S(1)}, u32[]{:S(2)}, u32[]{:S(2)}) async-start(bf16[8,128,1536]{2,1,0:T(8,128)(2,1)} %get-tuple-element.27), calls=%async_computation.1 | async-start | bytes 6291456 | tf_op jit(solution)/shard_map/all_to_all | solution.py:585
  191.6 45.4 %collective-permute-done.27 = bf16[16,1536]{1,0:T(8,128)(2,1)S(1)} collective-permute-done((bf16[16,1536]{1,0:T(8,128)(2,1)S(1)}, bf16[16,1536]{1,0:T(8,128)(2,1)S(1)}, u32[]{:S(2)}, u32[]{:S(2)}) %collective-permute-start.27) | collective-permute-done | bytes 49184 | tf_op jit(solution)/shard_map/ppermute | solution.py:470
  237.1 17.7 %collective-permute-done.28 = bf16[16,1536]{1,0:T(8,128)(2,1)S(1)} collective-permute-done((bf16[16,1536]{1,0:T(8,128)(2,1)S(1)}, bf16[16,1536]{1,0:T(8,128)(2,1)S(1)}, u32[]{:S(2)}, u32[]{:S(2)}) %collective-permute-start.28) | collective-permute-done | bytes 49184 | tf_op jit(solution)/shard_map/ppermute | solution.py:470
  272.2 18.4 %collective-permute-done.19 = bf16[2,384,768]{2,1,0:T(8,128)(2,1)S(1)} collective-permute-done((bf16[2,384,768]{2,1,0:T(8,128)(2,1)S(1)}, bf16[2,384,768]{2,1,0:T(8,128)(2,1)S(1)}, u32[]{:S(2)}, u32[]{:S(2)}) %collective-permute-start.19) | collective-permute-done | bytes 1179680 | tf_op jit(solution)/shard_map/ppermute | solution.py:450
  296.8 9.1 %collective-permute-done.20 = bf16[1,384,768]{2,1,0:T(8,128)(2,1)S(1)} collective-permute-done((bf16[1,384,768]{2,1,0:T(8,128)(2,1)S(1)}, bf16[1,384,768]{2,1,0:T(8,128)(2,1)S(1)}, u32[]{:S(2)}, u32[]{:S(2)}) %collective-permute-start.20) | collective-permute-done | bytes 589856 | tf_op jit(solution)/shard_map/ppermute | solution.py:450
  320.8 6.5 %collective-permute-done.21 = bf16[384,384]{1,0:T(8,128)(2,1)S(1)} collective-permute-done((bf16[384,384]{1,0:T(8,128)(2,1)S(1)}, bf16[384,384]{1,0:T(8,128)(2,1)S(1)}, u32[]{:S(2)}, u32[]{:S(2)}) %collective-permute-start.21) | collective-permute-done | bytes 294944 | tf_op jit(solution)/shard_map/ppermute | solution.py:486
  327.3 10.7 %collective-permute-done.22 = bf16[384,384]{1,0:T(8,128)(2,1)S(1)} collective-permute-done((bf16[384,384]{1,0:T(8,128)(2,1)S(1)}, bf16[384,384]{1,0:T(8,128)(2,1)S(1)}, u32[]{:S(2)}, u32[]{:S(2)}) %collective-permute-start.22) | collective-permute-done | bytes 294944 | tf_op jit(solution)/shard_map/ppermute | solution.py:486
  338.0 6.3 %collective-permute-done.23 = bf16[384,384]{1,0:T(8,128)(2,1)S(1)} collective-permute-done((bf16[384,384]{1,0:T(8,128)(2,1)S(1)}, bf16[384,384]{1,0:T(8,128)(2,1)S(1)}, u32[]{:S(2)}, u32[]{:S(2)}) %collective-permute-start.23) | collective-permute-done | bytes 294944 | tf_op jit(solution)/shard_map/ppermute | solution.py:486
  (146 shorter events, 84.5 us)
Async XLA Ops:
  5.1 92.4 %all-to-all-start = ((bf16[8,128,1536]{2,1,0:T(8,128)(2,1)}), bf16[8,128,1536]{2,1,0:T(8,128)(2,1)}, u32[]{:S(2)}, u32[]{:S(2)}) async-start(bf16[8,128,1536]{2,1,0:T(8,128)(2,1)} %pick_panels.1), calls=%async_computation | async-start | bytes 6291456 | tf_op jit(solution)/shard_map/all_to_all | solution.py:513
  10.6 15.4 %collective-permute-start.7 = (bf16[1,96,3072]{2,1,0:T(8,128)(2,1)S(1)}, bf16[1,96,3072]{2,1,0:T(8,128)(2,1)S(1)}, u32[]{:S(2)}, u32[]{:S(2)}) collective-permute-start(bf16[1,96,3072]{2,1,0:T(8,128)(2,1)S(1)} %get-tuple-element.32), channel_id=1, source_target_pairs={{0,16},{8,24},{16,0},{24,8},{1,17},{9,25},{17,1},{25,9},{2,18},{10... | collective-permute-start | bytes 1769480 | tf_op jit(solution)/shard_map/ppermute | solution.py:88
  12.2 15.5 %collective-permute-start.4 = (bf16[1,96,3072]{2,1,0:T(8,128)(2,1)S(1)}, bf16[1,96,3072]{2,1,0:T(8,128)(2,1)S(1)}, u32[]{:S(2)}, u32[]{:S(2)}) collective-permute-start(bf16[1,96,3072]{2,1,0:T(8,128)(2,1)S(1)} %get-tuple-element.33), channel_id=1, source_target_pairs={{0,8},{8,0},{16,24},{24,16},{1,9},{9,1},{17,25},{25,17},{2,10},{10... | collective-permute-start | bytes 1769480 | tf_op jit(solution)/shard_map/ppermute | solution.py:88
  26.2 27.2 %collective-permute-start.8 = (bf16[2,96,3072]{2,1,0:T(8,128)(2,1)S(1)}, bf16[2,96,3072]{2,1,0:T(8,128)(2,1)S(1)}, u32[]{:S(2)}, u32[]{:S(2)}) collective-permute-start(bf16[2,96,3072]{2,1,0:T(8,128)(2,1)S(1)} %pad_maximum_fusion.3), channel_id=1, source_target_pairs={{0,8},{8,0},{16,24},{24,16},{1,9},{9,1},{17,25},{25,17},{2,10},{10... | collective-permute-start | bytes 3538952 | tf_op jit(solution)/shard_map/ppermute | solution.py:88
  27.8 26.9 %collective-permute-start.5 = (bf16[2,96,3072]{2,1,0:T(8,128)(2,1)S(1)}, bf16[2,96,3072]{2,1,0:T(8,128)(2,1)S(1)}, u32[]{:S(2)}, u32[]{:S(2)}) collective-permute-start(bf16[2,96,3072]{2,1,0:T(8,128)(2,1)S(1)} %pad_maximum_fusion.2), channel_id=1, source_target_pairs={{0,16},{8,24},{16,0},{24,8},{1,17},{9,25},{17,1},{25,9},{2,18},{10... | collective-permute-start | bytes 3538952 | tf_op jit(solution)/shard_map/ppermute | solution.py:88
  29.4 33.7 %collective-permute-start = (s32[1,2,4]{2,1,0:T(2,128)S(1)}, s32[1,2,4]{2,1,0:T(2,128)S(1)}, u32[]{:S(2)}, u32[]{:S(2)}) collective-permute-start(s32[1,2,4]{2,1,0:T(2,128)S(1)} %add_bitcast_fusion), channel_id=1, source_target_pairs={{0,1},{1,0},{2,3},{3,2},{4,5},{5,4},{6,7},{7,6},{8,9},{9,8},{10,11... | collective-permute-start | bytes 104 | tf_op jit(solution)/shard_map/ppermute | solution.py:516
  53.6 35.8 %collective-permute-start.9 = (bf16[4,96,3072]{2,1,0:T(8,128)(2,1)S(1)}, bf16[4,96,3072]{2,1,0:T(8,128)(2,1)}, u32[]{:S(2)}, u32[]{:S(2)}) collective-permute-start(bf16[4,96,3072]{2,1,0:T(8,128)(2,1)S(1)} %pad_maximum_fusion.1.b), channel_id=1, source_target_pairs={{0,1},{1,0},{2,3},{3,2},{4,5},{5,4},{6,7},{7,6},{8,9},{9,8},{10,11... | collective-permute-start | bytes 7077896 | tf_op jit(solution)/shard_map/ppermute | solution.py:104
  56.4 33.0 %collective-permute-start.6 = (bf16[4,96,3072]{2,1,0:T(8,128)(2,1)}, bf16[4,96,3072]{2,1,0:T(8,128)(2,1)}, u32[]{:S(2)}, u32[]{:S(2)}) collective-permute-start(bf16[4,96,3072]{2,1,0:T(8,128)(2,1)} %pad_maximum_fusion.a), channel_id=1, source_target_pairs={{0,1},{1,0},{2,3},{3,2},{4,5},{5,4},{6,7},{7,6},{8,9},{9,8},{10,11... | collective-permute-start | bytes 7077896 | tf_op jit(solution)/shard_map/ppermute | solution.py:103
  57.3 60.0 %collective-permute-start.12 = (bf16[16,1536]{1,0:T(8,128)(2,1)S(1)}, bf16[16,1536]{1,0:T(8,128)(2,1)S(1)}, u32[]{:S(2)}, u32[]{:S(2)}) collective-permute-start(bf16[16,1536]{1,0:T(8,128)(2,1)S(1)} %get-tuple-element.43), channel_id=1, source_target_pairs={{0,1},{1,2},{2,3},{3,4},{4,5},{5,6},{6,7},{8,9},{9,10},{10,11},{11... | collective-permute-start | bytes 147464 | tf_op jit(solution)/shard_map/ppermute | solution.py:492
  59.7 57.6 %collective-permute-start.13 = (bf16[16,1536]{1,0:T(8,128)(2,1)S(1)}, bf16[16,1536]{1,0:T(8,128)(2,1)S(1)}, u32[]{:S(2)}, u32[]{:S(2)}) collective-permute-start(bf16[16,1536]{1,0:T(8,128)(2,1)S(1)} %get-tuple-element.42), channel_id=1, source_target_pairs={{1,0},{2,1},{3,2},{4,3},{5,4},{6,5},{7,6},{9,8},{10,9},{11,10},{12... | collective-permute-start | bytes 147464 | tf_op jit(solution)/shard_map/ppermute | solution.py:493
  168.4 89.6 %collective-permute-start.14 = (bf16[4,512,384]{2,1,0:T(8,128)(2,1)}, bf16[4,512,384]{2,1,0:T(8,128)(2,1)}, u32[]{:S(2)}, u32[]{:S(2)}) collective-permute-start(bf16[4,512,384]{2,1,0:T(8,128)(2,1)} %get-tuple-element.28), channel_id=1, source_target_pairs={{0,1},{1,0},{2,3},{3,2},{4,5},{5,4},{6,7},{7,6},{8,9},{9,8},{10,11... | collective-permute-start | bytes 4718600 | tf_op jit(solution)/shard_map/ppermute | solution.py:528
  179.0 79.0 %collective-permute-start.18 = (bf16[512,768]{1,0:T(8,128)(2,1)}, bf16[512,768]{1,0:T(8,128)(2,1)}, u32[]{:S(2)}, u32[]{:S(2)}) collective-permute-start(bf16[512,768]{1,0:T(8,128)(2,1)} %get-tuple-element.26.refs_3_), channel_id=1, source_target_pairs={{0,1},{1,0},{2,3},{3,2},{4,5},{5,4},{6,7},{7,6},{8,9},{9,8},{10,11... | collective-permute-start | bytes 2359304 | tf_op jit(solution)/shard_map/ppermute | solution.py:571
  179.0 166.3 %all-to-all-start.1 = ((bf16[8,128,1536]{2,1,0:T(8,128)(2,1)}), bf16[8,128,1536]{2,1,0:T(8,128)(2,1)S(1)}, u32[]{:S(2)}, u32[]{:S(2)}) async-start(bf16[8,128,1536]{2,1,0:T(8,128)(2,1)} %get-tuple-element.27), calls=%async_computation.1 | async-start | bytes 6291456 | tf_op jit(solution)/shard_map/all_to_all | solution.py:585
  187.2 49.8 %collective-permute-start.27 = (bf16[16,1536]{1,0:T(8,128)(2,1)S(1)}, bf16[16,1536]{1,0:T(8,128)(2,1)S(1)}, u32[]{:S(2)}, u32[]{:S(2)}) collective-permute-start(bf16[16,1536]{1,0:T(8,128)(2,1)S(1)} %fusion.26), channel_id=1, source_target_pairs={{0,2},{1,3},{2,0},{3,1},{4,6},{5,7},{6,4},{7,5},{8,10},{9,11},{10,... | collective-permute-start | bytes 147464 | tf_op jit(solution)/shard_map/ppermute | solution.py:470
  187.7 67.1 %collective-permute-start.28 = (bf16[16,1536]{1,0:T(8,128)(2,1)S(1)}, bf16[16,1536]{1,0:T(8,128)(2,1)S(1)}, u32[]{:S(2)}, u32[]{:S(2)}) collective-permute-start(bf16[16,1536]{1,0:T(8,128)(2,1)S(1)} %fusion.26), channel_id=1, source_target_pairs={{0,4},{1,5},{2,6},{3,7},{4,0},{5,1},{6,2},{7,3},{8,12},{9,13},{10,... | collective-permute-start | bytes 147464 | tf_op jit(solution)/shard_map/ppermute | solution.py:470
  190.2 67.7 %collective-permute-start.29 = (bf16[16,1536]{1,0:T(8,128)(2,1)S(1)}, bf16[16,1536]{1,0:T(8,128)(2,1)S(1)}, u32[]{:S(2)}, u32[]{:S(2)}) collective-permute-start(bf16[16,1536]{1,0:T(8,128)(2,1)S(1)} %fusion.26), channel_id=1, source_target_pairs={{0,6},{1,7},{2,4},{3,5},{4,2},{5,3},{6,0},{7,1},{8,14},{9,15},{10,... | collective-permute-start | bytes 147464 | tf_op jit(solution)/shard_map/ppermute | solution.py:470
  237.1 27.3 %collective-permute-start.15 = (bf16[512,768]{1,0:T(8,128)(2,1)S(1)}, bf16[512,768]{1,0:T(8,128)(2,1)S(1)}, u32[]{:S(2)}, u32[]{:S(2)}) collective-permute-start(bf16[512,768]{1,0:T(8,128)(2,1)S(1)} %copy-done.8), channel_id=1, source_target_pairs={{0,1},{1,0},{2,3},{3,2},{4,5},{5,4},{6,7},{7,6},{8,9},{9,8},{10,11... | collective-permute-start | bytes 2359304 | tf_op jit(solution)/shard_map/ppermute | solution.py:571
  257.9 38.9 %collective-permute-start.30 = (f32[16,1536]{1,0:T(8,128)S(1)}, f32[16,1536]{1,0:T(8,128)S(1)}, u32[]{:S(2)}, u32[]{:S(2)}) collective-permute-start(f32[16,1536]{1,0:T(8,128)S(1)} %add_add_fusion), channel_id=1, source_target_pairs={{0,1},{1,0},{2,3},{3,2},{4,5},{5,4},{6,7},{7,6},{8,9},{9,8},{10,11... | collective-permute-start | bytes 294920 | tf_op jit(solution)/shard_map/ppermute | solution.py:475
  262.3 28.4 %collective-permute-start.19 = (bf16[2,384,768]{2,1,0:T(8,128)(2,1)S(1)}, bf16[2,384,768]{2,1,0:T(8,128)(2,1)S(1)}, u32[]{:S(2)}, u32[]{:S(2)}) collective-permute-start(bf16[2,384,768]{2,1,0:T(8,128)(2,1)S(1)} %add_convert_fusion), channel_id=1, source_target_pairs={{0,16},{8,24},{16,0},{24,8},{1,17},{9,25},{17,1},{25,9},{2,18},{10... | collective-permute-start | bytes 3538952 | tf_op jit(solution)/shard_map/ppermute | solution.py:450
  265.3 28.4 %collective-permute-start.16 = (bf16[2,384,768]{2,1,0:T(8,128)(2,1)S(1)}, bf16[2,384,768]{2,1,0:T(8,128)(2,1)S(1)}, u32[]{:S(2)}, u32[]{:S(2)}) collective-permute-start(bf16[2,384,768]{2,1,0:T(8,128)(2,1)S(1)} %add_convert_fusion.2), channel_id=1, source_target_pairs={{0,8},{8,0},{16,24},{24,16},{1,9},{9,1},{17,25},{25,17},{2,10},{10... | collective-permute-start | bytes 3538952 | tf_op jit(solution)/shard_map/ppermute | solution.py:450
  290.8 15.2 %collective-permute-start.20 = (bf16[1,384,768]{2,1,0:T(8,128)(2,1)S(1)}, bf16[1,384,768]{2,1,0:T(8,128)(2,1)S(1)}, u32[]{:S(2)}, u32[]{:S(2)}) collective-permute-start(bf16[1,384,768]{2,1,0:T(8,128)(2,1)S(1)} %add_convert_fusion.5), channel_id=1, source_target_pairs={{0,8},{8,0},{16,24},{24,16},{1,9},{9,1},{17,25},{25,17},{2,10},{10... | collective-permute-start | bytes 1769480 | tf_op jit(solution)/shard_map/ppermute | solution.py:450
  294.9 14.7 %collective-permute-start.17 = (bf16[1,384,768]{2,1,0:T(8,128)(2,1)}, bf16[1,384,768]{2,1,0:T(8,128)(2,1)}, u32[]{:S(2)}, u32[]{:S(2)}) collective-permute-start(bf16[1,384,768]{2,1,0:T(8,128)(2,1)} %add_convert_fusion.8), channel_id=1, source_target_pairs={{0,16},{8,24},{16,0},{24,8},{1,17},{9,25},{17,1},{25,9},{2,18},{10... | collective-permute-start | bytes 1769480 | tf_op jit(solution)/shard_map/ppermute | solution.py:450
  317.0 21.0 %collective-permute-start.22 = (bf16[384,384]{1,0:T(8,128)(2,1)S(1)}, bf16[384,384]{1,0:T(8,128)(2,1)S(1)}, u32[]{:S(2)}, u32[]{:S(2)}) collective-permute-start(bf16[384,384]{1,0:T(8,128)(2,1)S(1)} %get-tuple-element.48), channel_id=1, source_target_pairs={{0,4},{1,5},{2,6},{3,7},{4,0},{5,1},{6,2},{7,3},{8,12},{9,13},{10,... | collective-permute-start | bytes 884744 | tf_op jit(solution)/shard_map/ppermute | solution.py:486
  318.0 26.3 %collective-permute-start.23 = (bf16[384,384]{1,0:T(8,128)(2,1)S(1)}, bf16[384,384]{1,0:T(8,128)(2,1)S(1)}, u32[]{:S(2)}, u32[]{:S(2)}) collective-permute-start(bf16[384,384]{1,0:T(8,128)(2,1)S(1)} %get-tuple-element.47), channel_id=1, source_target_pairs={{0,6},{1,7},{2,4},{3,5},{4,2},{5,3},{6,0},{7,1},{8,14},{9,15},{10,... | collective-permute-start | bytes 884744 | tf_op jit(solution)/shard_map/ppermute | solution.py:486
  (26 other events, 252.5 us)

commit v6 on v5

--- a/solution.py
+++ b/solution.py
@@ -296,40 +296,59 @@
         out[:, lanes] = jnp.sum(partial[...], axis=1)
 
 
-def gated_body(flags, grad, low, high, lin, gate, weights, *refs, panels, length, taps):
+def gated_body(flags, grad, low, high, lin, gate, weights, *refs, panels, length, taps, steps):
     *outs, padded = refs
     fill_padded(flags, padded, grad, low, high, panels, length)
 
-    def work(chunk, s, start, rows, lanes):
-        total = shifted_sum(padded, weights, chunk, s, start, taps, True)
-        sig = jax.nn.sigmoid(gate[rows, lanes])
-        scaled = total * sig
-        outs[0][rows, lanes] = scaled.astype(BF)
-        outs[1][rows, lanes] = (scaled * lin[rows, lanes] * (1.0 - sig)).astype(BF)
-
-    tiles(grad.shape[1], panels, length, work)
-
-
-def gated(flags, grad_depth, low, high, lin, gate, kernel, block, parities, parity, sizes):
+    def run(first, second):
+        def work(chunk, s, start, rows, lanes):
+            total = shifted_sum(padded, weights, chunk, s, start, taps, True)
+            sig = jax.nn.sigmoid(gate[rows, lanes])
+            scaled = total * sig
+            first[rows, lanes] = scaled.astype(BF)
+            second[rows, lanes] = (scaled * lin[rows, lanes] * (1.0 - sig)).astype(BF)
+
+        tiles(grad.shape[1], panels, length, work)
+
+    for part in range(len(outs) // 2):
+
+        @pl.when(pl.program_id(0) // steps == part)
+        def _():
+            run(*outs[2 * part : 2 * part + 2])
+
+
+def gated(flags, grad_depth, low, high, lin, gate, kernel, block, parts, core, sizes):
     rows, width = grad_depth.shape
     panels = sizes["panels"]
-    column = lambda height: pl.BlockSpec((height, block), lambda j, idx: (0, j * parities + idx[2 * panels]))
-    shapes = [jax.ShapeDtypeStruct((rows, width // parities), BF)] * 2
+    steps = width // block // parts
+
+    def column(height):
+        def index(j, idx):
+            if parts == 1:
+                return (0, j)
+            parity = jnp.where(j < steps, 1 - idx[2 * panels], idx[2 * panels])
+            return (0, 2 * (j % steps) + parity)
+
+        return pl.BlockSpec((height, block), index)
+
+    def out(part):
+        return pl.BlockSpec((rows, block), lambda j, idx: (0, jnp.clip(j - part * steps, 0, steps - 1)))
+
     return pl.pallas_call(
-        functools.partial(gated_body, **sizes),
+        functools.partial(gated_body, steps=steps, **sizes),
         grid_spec=pltpu.PrefetchScalarGridSpec(
             num_scalar_prefetch=1,
-            grid=(width // block // parities,),
+            grid=(parts * steps,),
             in_specs=[column(h) for h in (rows, RIM, RIM, rows, rows, kernel.shape[0])],
-            out_specs=[pl.BlockSpec((rows, block), lambda j, idx: (0, j)) for _ in shapes],
+            out_specs=[out(part) for part in range(parts) for _ in range(2)],
             scratch_shapes=[
                 pltpu.VMEM((block // LANES, panels, sizes["length"] + 2 * RIM, LANES), F32)
             ],
         ),
-        out_shape=shapes,
+        out_shape=[jax.ShapeDtypeStruct((rows, width // parts), BF)] * (2 * parts),
         compiler_params=params(1, 48),
         name="gated",
-    )(jnp.append(flags, parity), grad_depth, low, high, lin, gate, kernel)
+    )(jnp.append(flags, core), grad_depth, low, high, lin, gate, kernel)
 
 
 def back_body(source, *refs, grads, block, panels, piece):
@@ -477,14 +496,15 @@
 
 
 def sum_across(share):
-    count = share.shape[0]
     place = lax.axis_index("tm") // 2
-    total = lax.dynamic_index_in_dim(share, place, 0, keepdims=False).astype(F32)
-    for turn in range(1, count):
-        piece = lax.dynamic_index_in_dim(share, place ^ turn, 0, keepdims=False)
-        pairs = [(i, i ^ (2 * turn)) for i in range(2 * count)]
-        total = total + lax.ppermute(piece, "tm", pairs).astype(F32)
-    return total
+    for bit in bits_of(share.shape[0]):
+        pairs = share.reshape(share.shape[0] // 2, 2, *share.shape[1:])
+        mine = (place >> bit) & 1
+        send = lax.dynamic_index_in_dim(pairs, 1 - mine, 1, keepdims=False).astype(BF)
+        keep = lax.dynamic_index_in_dim(pairs, mine, 1, keepdims=False)
+        got = lax.ppermute(send, "tm", flip("tm", 2 << bit))
+        share = keep.astype(F32) + got.astype(F32)
+    return share[0]
 
 
 def edges(values, width):
@@ -567,12 +587,12 @@
     piece = 2 * width // owners
     arguments = (flags, grad_depth, grad_low, grad_high, lin, gate, kernel)
     if piece % LANES == 0:
-        give = gated(*arguments, piece, 2, 1 - core, sizes)
+        *give, own_lin, own_gate = gated(*arguments, piece, 2, core, sizes)
+        own = (own_lin, own_gate)
         others = [lax.ppermute(g, "tm", flip_bit("tm", 0)) for g in give]
-        own = gated(*arguments, piece, 2, core, sizes)
         gradients, run = (*own, *give), piece
     else:
-        gradients, run = tuple(gated(*arguments, lane_block, 1, 0, sizes)), width
+        gradients, run = tuple(gated(*arguments, lane_block, 1, core, sizes)), width
         pick_parity = lambda values, parity: lax.dynamic_index_in_dim(
             values.reshape(rows, owners // 4, 2, piece), parity, 2, keepdims=False
         ).reshape(rows, width // 2)

time: 349 us -> 285 us (0.82)
  waiting for transfers between devices: 178 us -> 106 us
  local copies, waits for them, and re-layouts: 13.9 us -> 17.8 us
    ppermute x3, waiting for transfers between devices: 66.3 us -> 0.64 us  [sum_everywhere(): terms.append(lax.ppermute(values, 'tm', flip('tm', mask)))]
    ppermute x4, waiting for transfers between devices: 28.9 us -> 25.3 us  [outer_halved(): got = lax.ppermute(send, 'dp', flip_bit('dp', bit))]
    concatenate x3 -> x4, local copies, waits for them, and re-layouts: 5.14 us -> 8.28 us  [local(): share = jnp.concatenate(shares, axis=1)]
    pallas_call x2 -> x1, Pallas kernels: 14.8 us -> 13.1 us  [gated(): pl.pallas_call(functools.partial(gated_body, steps=steps, **sizes), grid_...]
    ppermute x3 -> x2, waiting for transfers between devices: 23.5 us -> 22.6 us  [sum_across(): got = lax.ppermute(send, 'tm', flip('tm', 2 << bit))]
  transfers between devices with their start and end apart: 33 -> 32, of which waited for: 18 -> 14; matrix products, arithmetic and copies ran while one was open for 11% -> 15% of each run, Pallas kernels for 8% -> 26%
where the time goes in v6:
time: 285 us; the launch traced here: 281 us
  waiting for transfers between devices  106 us (37%)
  Pallas kernels  77.3 us (27%)
  starting transfers between devices  50.9 us (18%)
  local copies, waits for them, and re-layouts  17.8 us (6%)
  matrix products  15.3 us (5%)
  other arithmetic  12.4 us (4%)
    ppermute x4, waiting for transfers between devices, gather_order(): got = lax.ppermute(have, 'dp', flip_bit('dp', bit))  37.2 us
    ppermute x4, waiting for transfers between devices, outer_halved(): got = lax.ppermute(send, 'dp', flip_bit('dp', bit))  25.3 us
    ppermute x2, waiting for transfers between devices, sum_across(): got = lax.ppermute(send, 'tm', flip('tm', 2 << bit))  22.6 us
    dot_general x8, matrix products, outer_sum(): lax.dot_general(a, b, (((1,), (0,)), ((), ())), preferred_element_type=F32)  15.3 us
    pallas_call x1, Pallas kernels, back(): pl.pallas_call(functools.partial(back_body, grads=len(gradients), block=b...  14.5 us
    ppermute x3, waiting for transfers between devices, local(): lax.ppermute(tags, 'tm', flip('tm', i))  14.5 us
    pallas_call x2, Pallas kernels, put(): pl.pallas_call(body, grid_spec=pltpu.PrefetchScalarGridSpec(num_scalar_pr...  14.3 us
    pallas_call x1, Pallas kernels, gated(): pl.pallas_call(functools.partial(gated_body, steps=steps, **sizes), grid_...  13.1 us
  transfers between devices with their start and end apart: 32, of which 14 were waited for; matrix products, arithmetic and copies ran while one was open for 15% of the time, Pallas kernels for 26%

profile of v6, /device:TPU:8, one launch (start us, length us, event | category | flops | bytes accessed | tf_op | source)
XLA Modules:
  0.0 281.0 jit_solution(15425839215192239681)
XLA Ops:
  5.0 5.5 %all-to-all-start = ((bf16[8,128,1536]{2,1,0:T(8,128)(2,1)}), bf16[8,128,1536]{2,1,0:T(8,128)(2,1)}, u32[]{:S(2)}, u32[]{:S(2)}) async-start(bf16[8,128,1536]{2,1,0:T(8,128)(2,1)} %pick_panels.1), calls=%async_computation | async-start | bytes 6291456 | tf_op jit(solution)/shard_map/all_to_all | solution.py:533
  13.7 12.3 %collective-permute-done.7 = bf16[1,96,3072]{2,1,0:T(8,128)(2,1)S(1)} collective-permute-done((bf16[1,96,3072]{2,1,0:T(8,128)(2,1)S(1)}, bf16[1,96,3072]{2,1,0:T(8,128)(2,1)S(1)}, u32[]{:S(2)}, u32[]{:S(2)}) %collective-permute-start.7) | collective-permute-done | bytes 589856 | tf_op jit(solution)/shard_map/ppermute | solution.py:88
  29.5 23.8 %collective-permute-done.8 = bf16[2,96,3072]{2,1,0:T(8,128)(2,1)S(1)} collective-permute-done((bf16[2,96,3072]{2,1,0:T(8,128)(2,1)S(1)}, bf16[2,96,3072]{2,1,0:T(8,128)(2,1)S(1)}, u32[]{:S(2)}, u32[]{:S(2)}) %collective-permute-start.8) | collective-permute-done | bytes 1179680 | tf_op jit(solution)/shard_map/ppermute | solution.py:88
  59.7 3.1 %collective-permute-start.13 = (bf16[16,1536]{1,0:T(8,128)(2,1)S(1)}, bf16[16,1536]{1,0:T(8,128)(2,1)S(1)}, u32[]{:S(2)}, u32[]{:S(2)}) collective-permute-start(bf16[16,1536]{1,0:T(8,128)(2,1)S(1)} %get-tuple-element.42), channel_id=1, source_target_pairs={{1,0},{2,1},{3,2},{4,3},{5,4},{6,5},{7,6},{9,8},{10,9},{11,10},{12... | collective-permute-start | bytes 147464 | tf_op jit(solution)/shard_map/ppermute | solution.py:513
  63.3 3.6 %collective-permute-done.1 = s32[2,2,4]{2,1,0:T(2,128)S(1)} collective-permute-done((s32[2,2,4]{2,1,0:T(2,128)S(1)}, s32[2,2,4]{2,1,0:T(2,128)S(1)}, u32[]{:S(2)}, u32[]{:S(2)}) %collective-permute-start.1) | collective-permute-done | bytes 96 | tf_op jit(solution)/shard_map/ppermute | solution.py:537
  69.3 9.4 %collective-permute-done.2 = s32[2,2,4]{2,1,0:T(2,128)S(1)} collective-permute-done((s32[2,2,4]{2,1,0:T(2,128)S(1)}, s32[2,2,4]{2,1,0:T(2,128)S(1)}, u32[]{:S(2)}, u32[]{:S(2)}) %collective-permute-start.2) | collective-permute-done | bytes 96 | tf_op jit(solution)/shard_map/ppermute | solution.py:537
  83.2 6.3 %put_weights.2.rest_0_ = bf16[16,96,3072]{2,1,0:T(8,128)(2,1)} custom-call(s32[8]{0:T(128)S(1)} %stack.76._, bf16[4,96,3072]{2,1,0:T(8,128)(2,1)} %pad_maximum_fusion.a, bf16[4,96,3072]{2,1,0:T(8,128)(2,1)S(1)} %pad_maximum_fusion.1.b), custom_call_target="tpu_custom_call" | custom-call | tf_op jit(solution)/shard_map/put_weights/pallas_call | solution.py:130
  89.5 8.0 %put_weights.3 = bf16[16,96,3072]{2,1,0:T(8,128)(2,1)} custom-call(s32[8]{0:T(128)S(1)} %stack.67._, bf16[4,96,3072]{2,1,0:T(8,128)(2,1)} %collective-permute-done.6.a, bf16[4,96,3072]{2,1,0:T(8,128)(2,1)} %collective-permute-done.9.b, bf16[16,96,3072]{2,1,0:T(8,128)(2,1)} %put_weights.2.rest_0_), custom_call_target="tpu_custom_call", output_to_operand_aliasing={{}: (3, {})} | custom-call | tf_op jit(solution)/shard_map/put_weights/pallas_call | solution.py:130
  97.5 12.4 %forward.1 = (bf16[4,512,384]{2,1,0:T(8,128)(2,1)}, f32[512,1536]{1,0:T(8,128)}, f32[512,1536]{1,0:T(8,128)}, bf16[512,1536]{1,0:T(8,128)(2,1)S(1)}) custom-call(s32[5]{0:T(128)S(1)} %get-tuple-element.50.source, bf16[8,128,1536]{2,1,0:T(8,128)(2,1)} %all-to-all-done.x_hbm.refs_5_, f32[1,1536]{1,0:T(1,128)S(1)} %reshape.96.gain_ref.refs_7_, ...), custom_call_target="tpu_custom_call" | custom-call | tf_op jit(solution)/shard_map/forward/pallas_call | solution.py:188
  111.9 5.1 %collective-permute-start.11 = (bf16[32,1536]{1,0:T(8,128)(2,1)S(1)}, bf16[32,1536]{1,0:T(8,128)(2,1)S(1)}, u32[]{:S(2)}, u32[]{:S(2)}) collective-permute-start(bf16[32,1536]{1,0:T(8,128)(2,1)S(1)} %get-tuple-element.44), channel_id=1, source_target_pairs={{1,0},{2,1},{3,2},{4,3},{5,4},{6,5},{7,6},{9,8},{10,9},{11,10},{12... | collective-permute-start | bytes 294920 | tf_op jit(solution)/shard_map/ppermute | solution.py:513
  117.2 2.7 fusion.30
  119.9 9.7 %depth.1 = (bf16[512,1536]{1,0:T(8,128)(2,1)S(1)}, bf16[16,1536]{1,0:T(8,128)(2,1)S(1)}, bf16[16,1536]{1,0:T(8,128)(2,1)S(1)}) custom-call(s32[8]{0:T(128)S(1)} %add_convert_fusion.10.flags, bf16[512,1536]{1,0:T(8,128)(2,1)S(1)} %get-tuple-element.17.glu, bf16[32,1536]{1,0:T(8,128)(2,1)S(1)} %collective-permute-done.10.low, ...), custom_call_target="tpu_custom_call" | custom-call | tf_op jit(solution)/shard_map/depth/pallas_call | solution.py:557
  129.6 13.1 %gated.1 = (bf16[512,768]{1,0:T(8,128)(2,1)}, bf16[512,768]{1,0:T(8,128)(2,1)}, bf16[512,768]{1,0:T(8,128)(2,1)S(1)}, bf16[512,768]{1,0:T(8,128)(2,1)S(1)}) custom-call(s32[9]{0:T(128)S(1)} %pad_add_fusion.2.flags, bf16[512,1536]{1,0:T(8,128)(2,1)S(1)} %get-tuple-element.18.grad, bf16[16,1536]{1,0:T(8,128)(2,1)S(1)} %get-tuple-element.19.low, ...), custom_call_target="tpu_custom_call" | custom-call | tf_op jit(solution)/shard_map/gated/pallas_call | solution.py:337
  143.2 8.8 %taps.1 = f32[32,1536]{1,0:T(8,128)S(1)} custom-call(s32[8]{0:T(128)S(1)} %add_convert_fusion.10.flags, bf16[512,1536]{1,0:T(8,128)(2,1)S(1)} %get-tuple-element.17.glu, bf16[32,1536]{1,0:T(8,128)(2,1)S(1)} %collective-permute-done.10.low, bf16[32,1536]{1,0:T(8,128)(2,1)S(1)} %collective-permute-done.11.high, bf16[512,1536]{1,0:T(8,128)(2,1)S(1)} %get-tuple-element.18.grad), custom_call_target="tpu_custom_call" | custom-call | tf_op jit(solution)/shard_map/taps/pallas_call | solution.py:573
  152.1 14.5 %back.1 = (bf16[8,128,1536]{2,1,0:T(8,128)(2,1)}, f32[1,1536]{1,0:T(1,128)S(1)}) custom-call(s32[5]{0:T(128)S(1)} %get-tuple-element.51.source, bf16[512,768]{1,0:T(8,128)(2,1)S(1)} %get-tuple-element.23.refs_0_, bf16[512,768]{1,0:T(8,128)(2,1)S(1)} %get-tuple-element.24.refs_1_, bf16[512,768]{1,0:T(8,128)(2,1)} %get-tuple-element.25.refs_2_, ...), custom_call_target="tpu_custom_call" | custom-call | tf_op jit(solution)/shard_map/back/pallas_call | solution.py:422
  168.2 6.3 %all-to-all-start.1 = ((bf16[8,128,1536]{2,1,0:T(8,128)(2,1)}), bf16[8,128,1536]{2,1,0:T(8,128)(2,1)S(1)}, u32[]{:S(2)}, u32[]{:S(2)}) async-start(bf16[8,128,1536]{2,1,0:T(8,128)(2,1)} %get-tuple-element.27), calls=%async_computation.1 | async-start | bytes 6291456 | tf_op jit(solution)/shard_map/all_to_all | solution.py:605
  180.2 4.5 %collective-permute-done.24 = f32[32,1536]{1,0:T(8,128)S(1)} collective-permute-done((f32[32,1536]{1,0:T(8,128)S(1)}, f32[32,1536]{1,0:T(8,128)S(1)}, u32[]{:S(2)}, u32[]{:S(2)}) %collective-permute-start.24) | collective-permute-done | bytes 196640 | tf_op jit(solution)/shard_map/ppermute | solution.py:481
  200.8 16.0 %collective-permute-done.16 = bf16[2,384,768]{2,1,0:T(8,128)(2,1)S(1)} collective-permute-done((bf16[2,384,768]{2,1,0:T(8,128)(2,1)S(1)}, bf16[2,384,768]{2,1,0:T(8,128)(2,1)S(1)}, u32[]{:S(2)}, u32[]{:S(2)}) %collective-permute-start.16) | collective-permute-done | bytes 1179680 | tf_op jit(solution)/shard_map/ppermute | solution.py:469
  218.6 3.5 %collective-permute-done.19 = bf16[2,384,768]{2,1,0:T(8,128)(2,1)S(1)} collective-permute-done((bf16[2,384,768]{2,1,0:T(8,128)(2,1)S(1)}, bf16[2,384,768]{2,1,0:T(8,128)(2,1)S(1)}, u32[]{:S(2)}, u32[]{:S(2)}) %collective-permute-start.19) | collective-permute-done | bytes 1179680 | tf_op jit(solution)/shard_map/ppermute | solution.py:469
  225.1 2.5 collective-permute-start.27
  228.2 5.8 %collective-permute-done.17 = bf16[1,384,768]{2,1,0:T(8,128)(2,1)S(1)} collective-permute-done((bf16[1,384,768]{2,1,0:T(8,128)(2,1)S(1)}, bf16[1,384,768]{2,1,0:T(8,128)(2,1)S(1)}, u32[]{:S(2)}, u32[]{:S(2)}) %collective-permute-start.17) | collective-permute-done | bytes 589856 | tf_op jit(solution)/shard_map/ppermute | solution.py:469
  235.1 2.5 concatenate.87
  250.2 12.6 %collective-permute-done.21 = bf16[2,384,384]{2,1,0:T(8,128)(2,1)} collective-permute-done((bf16[2,384,384]{2,1,0:T(8,128)(2,1)}, bf16[2,384,384]{2,1,0:T(8,128)(2,1)}, u32[]{:S(2)}, u32[]{:S(2)}) %collective-permute-start.21) | collective-permute-done | bytes 589856 | tf_op jit(solution)/shard_map/ppermute | solution.py:505
  267.9 10.0 %collective-permute-done.22 = bf16[1,384,384]{2,1,0:T(8,128)(2,1)S(1)} collective-permute-done((bf16[1,384,384]{2,1,0:T(8,128)(2,1)S(1)}, bf16[1,384,384]{2,1,0:T(8,128)(2,1)S(1)}, u32[]{:S(2)}, u32[]{:S(2)}) %collective-permute-start.22) | collective-permute-done | bytes 294944 | tf_op jit(solution)/shard_map/ppermute | solution.py:505
  (148 shorter events, 77.7 us)
Async XLA Ops:
  5.0 92.5 %all-to-all-start = ((bf16[8,128,1536]{2,1,0:T(8,128)(2,1)}), bf16[8,128,1536]{2,1,0:T(8,128)(2,1)}, u32[]{:S(2)}, u32[]{:S(2)}) async-start(bf16[8,128,1536]{2,1,0:T(8,128)(2,1)} %pick_panels.1), calls=%async_computation | async-start | bytes 6291456 | tf_op jit(solution)/shard_map/all_to_all | solution.py:533
  10.6 15.4 %collective-permute-start.7 = (bf16[1,96,3072]{2,1,0:T(8,128)(2,1)S(1)}, bf16[1,96,3072]{2,1,0:T(8,128)(2,1)S(1)}, u32[]{:S(2)}, u32[]{:S(2)}) collective-permute-start(bf16[1,96,3072]{2,1,0:T(8,128)(2,1)S(1)} %get-tuple-element.32), channel_id=1, source_target_pairs={{0,16},{8,24},{16,0},{24,8},{1,17},{9,25},{17,1},{25,9},{2,18},{10... | collective-permute-start | bytes 1769480 | tf_op jit(solution)/shard_map/ppermute | solution.py:88
  12.2 15.5 %collective-permute-start.4 = (bf16[1,96,3072]{2,1,0:T(8,128)(2,1)S(1)}, bf16[1,96,3072]{2,1,0:T(8,128)(2,1)S(1)}, u32[]{:S(2)}, u32[]{:S(2)}) collective-permute-start(bf16[1,96,3072]{2,1,0:T(8,128)(2,1)S(1)} %get-tuple-element.33), channel_id=1, source_target_pairs={{0,8},{8,0},{16,24},{24,16},{1,9},{9,1},{17,25},{25,17},{2,10},{10... | collective-permute-start | bytes 1769480 | tf_op jit(solution)/shard_map/ppermute | solution.py:88
  26.1 27.2 %collective-permute-start.8 = (bf16[2,96,3072]{2,1,0:T(8,128)(2,1)S(1)}, bf16[2,96,3072]{2,1,0:T(8,128)(2,1)S(1)}, u32[]{:S(2)}, u32[]{:S(2)}) collective-permute-start(bf16[2,96,3072]{2,1,0:T(8,128)(2,1)S(1)} %pad_maximum_fusion.3), channel_id=1, source_target_pairs={{0,8},{8,0},{16,24},{24,16},{1,9},{9,1},{17,25},{25,17},{2,10},{10... | collective-permute-start | bytes 3538952 | tf_op jit(solution)/shard_map/ppermute | solution.py:88
  27.8 26.9 %collective-permute-start.5 = (bf16[2,96,3072]{2,1,0:T(8,128)(2,1)S(1)}, bf16[2,96,3072]{2,1,0:T(8,128)(2,1)S(1)}, u32[]{:S(2)}, u32[]{:S(2)}) collective-permute-start(bf16[2,96,3072]{2,1,0:T(8,128)(2,1)S(1)} %pad_maximum_fusion.2), channel_id=1, source_target_pairs={{0,16},{8,24},{16,0},{24,8},{1,17},{9,25},{17,1},{25,9},{2,18},{10... | collective-permute-start | bytes 3538952 | tf_op jit(solution)/shard_map/ppermute | solution.py:88
  29.4 33.7 %collective-permute-start = (s32[1,2,4]{2,1,0:T(2,128)S(1)}, s32[1,2,4]{2,1,0:T(2,128)S(1)}, u32[]{:S(2)}, u32[]{:S(2)}) collective-permute-start(s32[1,2,4]{2,1,0:T(2,128)S(1)} %add_bitcast_fusion.1), channel_id=1, source_target_pairs={{0,1},{1,0},{2,3},{3,2},{4,5},{5,4},{6,7},{7,6},{8,9},{9,8},{10,11... | collective-permute-start | bytes 104 | tf_op jit(solution)/shard_map/ppermute | solution.py:536
  53.6 35.9 %collective-permute-start.9 = (bf16[4,96,3072]{2,1,0:T(8,128)(2,1)S(1)}, bf16[4,96,3072]{2,1,0:T(8,128)(2,1)}, u32[]{:S(2)}, u32[]{:S(2)}) collective-permute-start(bf16[4,96,3072]{2,1,0:T(8,128)(2,1)S(1)} %pad_maximum_fusion.1.b), channel_id=1, source_target_pairs={{0,1},{1,0},{2,3},{3,2},{4,5},{5,4},{6,7},{7,6},{8,9},{9,8},{10,11... | collective-permute-start | bytes 7077896 | tf_op jit(solution)/shard_map/ppermute | solution.py:104
  56.4 33.1 %collective-permute-start.6 = (bf16[4,96,3072]{2,1,0:T(8,128)(2,1)}, bf16[4,96,3072]{2,1,0:T(8,128)(2,1)}, u32[]{:S(2)}, u32[]{:S(2)}) collective-permute-start(bf16[4,96,3072]{2,1,0:T(8,128)(2,1)} %pad_maximum_fusion.a), channel_id=1, source_target_pairs={{0,1},{1,0},{2,3},{3,2},{4,5},{5,4},{6,7},{7,6},{8,9},{9,8},{10,11... | collective-permute-start | bytes 7077896 | tf_op jit(solution)/shard_map/ppermute | solution.py:103
  57.3 62.6 %collective-permute-start.12 = (bf16[16,1536]{1,0:T(8,128)(2,1)S(1)}, bf16[16,1536]{1,0:T(8,128)(2,1)S(1)}, u32[]{:S(2)}, u32[]{:S(2)}) collective-permute-start(bf16[16,1536]{1,0:T(8,128)(2,1)S(1)} %get-tuple-element.43), channel_id=1, source_target_pairs={{0,1},{1,2},{2,3},{3,4},{4,5},{5,6},{6,7},{8,9},{9,10},{10,11},{11... | collective-permute-start | bytes 147464 | tf_op jit(solution)/shard_map/ppermute | solution.py:512
  59.7 60.2 %collective-permute-start.13 = (bf16[16,1536]{1,0:T(8,128)(2,1)S(1)}, bf16[16,1536]{1,0:T(8,128)(2,1)S(1)}, u32[]{:S(2)}, u32[]{:S(2)}) collective-permute-start(bf16[16,1536]{1,0:T(8,128)(2,1)S(1)} %get-tuple-element.42), channel_id=1, source_target_pairs={{1,0},{2,1},{3,2},{4,3},{5,4},{6,5},{7,6},{9,8},{10,9},{11,10},{12... | collective-permute-start | bytes 147464 | tf_op jit(solution)/shard_map/ppermute | solution.py:513
  117.1 67.8 %collective-permute-start.14 = (bf16[4,512,384]{2,1,0:T(8,128)(2,1)}, bf16[4,512,384]{2,1,0:T(8,128)(2,1)}, u32[]{:S(2)}, u32[]{:S(2)}) collective-permute-start(bf16[4,512,384]{2,1,0:T(8,128)(2,1)} %get-tuple-element.28), channel_id=1, source_target_pairs={{0,1},{1,0},{2,3},{3,2},{4,5},{5,4},{6,7},{7,6},{8,9},{9,8},{10,11... | collective-permute-start | bytes 4718600 | tf_op jit(solution)/shard_map/ppermute | solution.py:548
  142.7 43.8 %collective-permute-start.15 = (bf16[512,768]{1,0:T(8,128)(2,1)}, bf16[512,768]{1,0:T(8,128)(2,1)}, u32[]{:S(2)}, u32[]{:S(2)}) collective-permute-start(bf16[512,768]{1,0:T(8,128)(2,1)} %get-tuple-element.25.refs_2_), channel_id=1, source_target_pairs={{0,1},{1,0},{2,3},{3,2},{4,5},{5,4},{6,7},{7,6},{8,9},{9,8},{10,11... | collective-permute-start | bytes 2359304 | tf_op jit(solution)/shard_map/ppermute | solution.py:592
  143.1 46.0 %collective-permute-start.18 = (bf16[512,768]{1,0:T(8,128)(2,1)}, bf16[512,768]{1,0:T(8,128)(2,1)}, u32[]{:S(2)}, u32[]{:S(2)}) collective-permute-start(bf16[512,768]{1,0:T(8,128)(2,1)} %get-tuple-element.26.refs_3_), channel_id=1, source_target_pairs={{0,1},{1,0},{2,3},{3,2},{4,5},{5,4},{6,7},{7,6},{8,9},{9,8},{10,11... | collective-permute-start | bytes 2359304 | tf_op jit(solution)/shard_map/ppermute | solution.py:592
  168.2 110.6 %all-to-all-start.1 = ((bf16[8,128,1536]{2,1,0:T(8,128)(2,1)}), bf16[8,128,1536]{2,1,0:T(8,128)(2,1)S(1)}, u32[]{:S(2)}, u32[]{:S(2)}) async-start(bf16[8,128,1536]{2,1,0:T(8,128)(2,1)} %get-tuple-element.27), calls=%async_computation.1 | async-start | bytes 6291456 | tf_op jit(solution)/shard_map/all_to_all | solution.py:605
  184.8 39.9 %collective-permute-start.25 = (f32[16,1536]{1,0:T(8,128)S(1)}, f32[16,1536]{1,0:T(8,128)S(1)}, u32[]{:S(2)}, u32[]{:S(2)}) collective-permute-start(f32[16,1536]{1,0:T(8,128)S(1)} %dynamic-slice_bitcast_fusion.3), channel_id=1, source_target_pairs={{0,1},{1,0},{2,3},{3,2},{4,5},{5,4},{6,7},{7,6},{8,9},{9,8},{10,11... | collective-permute-start | bytes 294920 | tf_op jit(solution)/shard_map/ppermute | solution.py:486
  188.4 28.4 %collective-permute-start.16 = (bf16[2,384,768]{2,1,0:T(8,128)(2,1)S(1)}, bf16[2,384,768]{2,1,0:T(8,128)(2,1)S(1)}, u32[]{:S(2)}, u32[]{:S(2)}) collective-permute-start(bf16[2,384,768]{2,1,0:T(8,128)(2,1)S(1)} %add_convert_fusion.2), channel_id=1, source_target_pairs={{0,8},{8,0},{16,24},{24,16},{1,9},{9,1},{17,25},{25,17},{2,10},{10... | collective-permute-start | bytes 3538952 | tf_op jit(solution)/shard_map/ppermute | solution.py:469
  193.2 28.9 %collective-permute-start.19 = (bf16[2,384,768]{2,1,0:T(8,128)(2,1)S(1)}, bf16[2,384,768]{2,1,0:T(8,128)(2,1)S(1)}, u32[]{:S(2)}, u32[]{:S(2)}) collective-permute-start(bf16[2,384,768]{2,1,0:T(8,128)(2,1)S(1)} %add_convert_fusion), channel_id=1, source_target_pairs={{0,16},{8,24},{16,0},{24,8},{1,17},{9,25},{17,1},{25,9},{2,18},{10... | collective-permute-start | bytes 3538952 | tf_op jit(solution)/shard_map/ppermute | solution.py:469
  217.0 17.0 %collective-permute-start.17 = (bf16[1,384,768]{2,1,0:T(8,128)(2,1)S(1)}, bf16[1,384,768]{2,1,0:T(8,128)(2,1)S(1)}, u32[]{:S(2)}, u32[]{:S(2)}) collective-permute-start(bf16[1,384,768]{2,1,0:T(8,128)(2,1)S(1)} %add_convert_fusion.8), channel_id=1, source_target_pairs={{0,16},{8,24},{16,0},{24,8},{1,17},{9,25},{17,1},{25,9},{2,18},{10... | collective-permute-start | bytes 1769480 | tf_op jit(solution)/shard_map/ppermute | solution.py:469
  223.2 16.4 %collective-permute-start.20 = (bf16[1,384,768]{2,1,0:T(8,128)(2,1)}, bf16[1,384,768]{2,1,0:T(8,128)(2,1)}, u32[]{:S(2)}, u32[]{:S(2)}) collective-permute-start(bf16[1,384,768]{2,1,0:T(8,128)(2,1)} %add_convert_fusion.5), channel_id=1, source_target_pairs={{0,8},{8,0},{16,24},{24,16},{1,9},{9,1},{17,25},{25,17},{2,10},{10... | collective-permute-start | bytes 1769480 | tf_op jit(solution)/shard_map/ppermute | solution.py:469
  224.7 23.4 %collective-permute-start.26 = (bf16[16,1536]{1,0:T(8,128)(2,1)S(1)}, bf16[16,1536]{1,0:T(8,128)(2,1)S(1)}, u32[]{:S(2)}, u32[]{:S(2)}) collective-permute-start(bf16[16,1536]{1,0:T(8,128)(2,1)S(1)} %fusion.24), channel_id=1, source_target_pairs={{0,2},{1,3},{2,0},{3,1},{4,6},{5,7},{6,4},{7,5},{8,10},{9,11},{10,... | collective-permute-start | bytes 147464 | tf_op jit(solution)/shard_map/ppermute | solution.py:489
  225.1 23.0 %collective-permute-start.27 = (bf16[16,1536]{1,0:T(8,128)(2,1)S(1)}, bf16[16,1536]{1,0:T(8,128)(2,1)S(1)}, u32[]{:S(2)}, u32[]{:S(2)}) collective-permute-start(bf16[16,1536]{1,0:T(8,128)(2,1)S(1)} %fusion.24), channel_id=1, source_target_pairs={{0,4},{1,5},{2,6},{3,7},{4,0},{5,1},{6,2},{7,3},{8,12},{9,13},{10,... | collective-permute-start | bytes 147464 | tf_op jit(solution)/shard_map/ppermute | solution.py:489
  227.7 21.1 %collective-permute-start.28 = (bf16[16,1536]{1,0:T(8,128)(2,1)S(1)}, bf16[16,1536]{1,0:T(8,128)(2,1)S(1)}, u32[]{:S(2)}, u32[]{:S(2)}) collective-permute-start(bf16[16,1536]{1,0:T(8,128)(2,1)S(1)} %fusion.24), channel_id=1, source_target_pairs={{0,6},{1,7},{2,4},{3,5},{4,2},{5,3},{6,0},{7,1},{8,14},{9,15},{10,... | collective-permute-start | bytes 147464 | tf_op jit(solution)/shard_map/ppermute | solution.py:489
  247.7 15.0 %collective-permute-start.21 = (bf16[2,384,384]{2,1,0:T(8,128)(2,1)}, bf16[2,384,384]{2,1,0:T(8,128)(2,1)}, u32[]{:S(2)}, u32[]{:S(2)}) collective-permute-start(bf16[2,384,384]{2,1,0:T(8,128)(2,1)} %dynamic-slice_bitcast_fusion.2), channel_id=1, source_target_pairs={{0,2},{1,3},{2,0},{3,1},{4,6},{5,7},{6,4},{7,5},{8,10},{9,11},{10,... | collective-permute-start | bytes 1769480 | tf_op jit(solution)/shard_map/ppermute | solution.py:505
  264.1 13.8 %collective-permute-start.22 = (bf16[1,384,384]{2,1,0:T(8,128)(2,1)S(1)}, bf16[1,384,384]{2,1,0:T(8,128)(2,1)S(1)}, u32[]{:S(2)}, u32[]{:S(2)}) collective-permute-start(bf16[1,384,384]{2,1,0:T(8,128)(2,1)S(1)} %dynamic-slice_convert_fusion), channel_id=1, source_target_pairs={{0,4},{1,5},{2,6},{3,7},{4,0},{5,1},{6,2},{7,3},{8,12},{9,13},{10,... | collective-permute-start | bytes 884744 | tf_op jit(solution)/shard_map/ppermute | solution.py:505
  (26 other events, 149.4 us)

commit v7 on v6

--- a/solution.py
+++ b/solution.py
@@ -495,16 +495,22 @@
     return jnp.concatenate([jnp.where(core == 0, values, got), jnp.where(core == 0, got, values)])
 
 
-def sum_across(share):
+def sum_across(sides, piece):
     place = lax.axis_index("tm") // 2
-    for bit in bits_of(share.shape[0]):
-        pairs = share.reshape(share.shape[0] // 2, 2, *share.shape[1:])
-        mine = (place >> bit) & 1
-        send = lax.dynamic_index_in_dim(pairs, 1 - mine, 1, keepdims=False).astype(BF)
-        keep = lax.dynamic_index_in_dim(pairs, mine, 1, keepdims=False)
-        got = lax.ppermute(send, "tm", flip("tm", 2 << bit))
-        share = keep.astype(F32) + got.astype(F32)
-    return share[0]
+    each = sides[0].shape[1] // piece
+    lists = [[side[:, i * piece : (i + 1) * piece] for i in range(each)] for side in sides]
+
+    def exchange(blocks, bit):
+        upper = (place >> bit) & 1 == 1
+        send = [jnp.where(upper, a, b).astype(BF) for a, b in zip(blocks[::2], blocks[1::2])]
+        keep = [jnp.where(upper, b, a) for a, b in zip(blocks[::2], blocks[1::2])]
+        got = [lax.ppermute(block, "tm", flip("tm", 2 << bit)) for block in send]
+        return [k.astype(F32) + g.astype(F32) for k, g in zip(keep, got)]
+
+    *inner, last = bits_of(2 * each)
+    for bit in inner:
+        lists = [exchange(blocks, bit) for blocks in lists]
+    return exchange([lists[0][0], lists[1][0]], last)[0]
 
 
 def edges(values, width):
@@ -609,9 +615,7 @@
         outer_halved((normed, other_normed), (own[side], others[side]), order)
         for side, order in ((0, bits), (1, bits[::-1]))
     ]
-    share = jnp.concatenate(shares, axis=1)
-    share = share.reshape(width // count, owners // 2, piece).transpose(1, 0, 2)
-    shard_in = sum_across(share)
+    shard_in = sum_across(shares, piece)
     grad_loaded = pick_blocks(returned, owner_of.astype(jnp.int32), panels)
     sums = sum_everywhere(jnp.concatenate([kernel_term[:taps], gain_term], axis=0))
     return (grad_loaded[None, None], shard_in, sums[:taps], sums[taps])

time: 285 us -> 289 us (1.014)
  the two profiles are of different devices: /device:TPU:8 before, /device:TPU:0 now
where the time goes in v7:
time: 289 us; the launch traced here: 288 us
  waiting for transfers between devices  131 us (45%)
  Pallas kernels  77.4 us (27%)
  starting transfers between devices  48.5 us (17%)
  matrix products  15.3 us (5%)
  other arithmetic  7.5 us (3%)
  local copies, waits for them, and re-layouts  7.46 us (3%)
    ppermute x4, waiting for transfers between devices, gather_order(): got = lax.ppermute(have, 'dp', flip_bit('dp', bit))  38.1 us
    ppermute x3, waiting for transfers between devices, exchange(): got = [lax.ppermute(block, 'tm', flip('tm', 2 << bit)) for block in send]  26.9 us
    ppermute x3, waiting for transfers between devices, sum_everywhere(): terms.append(lax.ppermute(values, 'tm', flip('tm', mask)))  22.1 us
    ppermute x4, waiting for transfers between devices, outer_halved(): got = lax.ppermute(send, 'dp', flip_bit('dp', bit))  19.6 us
    ppermute x3, waiting for transfers between devices, local(): lax.ppermute(tags, 'tm', flip('tm', i))  19.6 us
    dot_general x8, matrix products, outer_sum(): lax.dot_general(a, b, (((1,), (0,)), ((), ())), preferred_element_type=F32)  15.3 us
    pallas_call x1, Pallas kernels, back(): pl.pallas_call(functools.partial(back_body, grads=len(gradients), block=b...  14.5 us
    pallas_call x2, Pallas kernels, put(): pl.pallas_call(body, grid_spec=pltpu.PrefetchScalarGridSpec(num_scalar_pr...  14.3 us
  transfers between devices with their start and end apart: 33, of which 15 were waited for; matrix products, arithmetic and copies ran while one was open for 10% of the time, Pallas kernels for 25%

profile of v7, /device:TPU:0, one launch (start us, length us, event | category | flops | bytes accessed | tf_op | source)
XLA Modules:
  0.0 288.2 jit_solution(8217158137441544163)
XLA Ops:
  5.1 6.5 %all-to-all-start = ((bf16[8,128,1536]{2,1,0:T(8,128)(2,1)}), bf16[8,128,1536]{2,1,0:T(8,128)(2,1)}, u32[]{:S(2)}, u32[]{:S(2)}) async-start(bf16[8,128,1536]{2,1,0:T(8,128)(2,1)} %pick_panels.1), calls=%async_computation | async-start | bytes 6291456 | tf_op jit(solution)/shard_map/all_to_all | solution.py:539
  14.7 12.7 %collective-permute-done.7 = bf16[1,96,3072]{2,1,0:T(8,128)(2,1)S(1)} collective-permute-done((bf16[1,96,3072]{2,1,0:T(8,128)(2,1)S(1)}, bf16[1,96,3072]{2,1,0:T(8,128)(2,1)S(1)}, u32[]{:S(2)}, u32[]{:S(2)}) %collective-permute-start.7) | collective-permute-done | bytes 589856 | tf_op jit(solution)/shard_map/ppermute | solution.py:88
  30.9 24.3 %collective-permute-done.8 = bf16[2,96,3072]{2,1,0:T(8,128)(2,1)S(1)} collective-permute-done((bf16[2,96,3072]{2,1,0:T(8,128)(2,1)S(1)}, bf16[2,96,3072]{2,1,0:T(8,128)(2,1)S(1)}, u32[]{:S(2)}, u32[]{:S(2)}) %collective-permute-start.8) | collective-permute-done | bytes 1179680 | tf_op jit(solution)/shard_map/ppermute | solution.py:88
  59.2 2.4 collective-permute-start.12
  63.2 3.1 %collective-permute-start.1 = (s32[2,2,4]{2,1,0:T(2,128)S(1)}, s32[2,2,4]{2,1,0:T(2,128)S(1)}, u32[]{:S(2)}, u32[]{:S(2)}) collective-permute-start(s32[2,2,4]{2,1,0:T(2,128)S(1)} %pad_add_fusion), channel_id=1, source_target_pairs={{0,2},{1,3},{2,0},{3,1},{4,6},{5,7},{6,4},{7,5},{8,10},{9,11},{10,... | collective-permute-start | bytes 200 | tf_op jit(solution)/shard_map/ppermute | solution.py:543
  70.8 12.9 %collective-permute-done.2 = s32[2,2,4]{2,1,0:T(2,128)S(1)} collective-permute-done((s32[2,2,4]{2,1,0:T(2,128)S(1)}, s32[2,2,4]{2,1,0:T(2,128)S(1)}, u32[]{:S(2)}, u32[]{:S(2)}) %collective-permute-start.2) | collective-permute-done | bytes 96 | tf_op jit(solution)/shard_map/ppermute | solution.py:543
  84.6 4.5 %collective-permute-done.3 = s32[2,2,4]{2,1,0:T(2,128)S(1)} collective-permute-done((s32[2,2,4]{2,1,0:T(2,128)S(1)}, s32[2,2,4]{2,1,0:T(2,128)S(1)}, u32[]{:S(2)}, u32[]{:S(2)}) %collective-permute-start.3) | collective-permute-done | bytes 96 | tf_op jit(solution)/shard_map/ppermute | solution.py:543
  89.9 6.3 %put_weights.2.rest_0_ = bf16[16,96,3072]{2,1,0:T(8,128)(2,1)} custom-call(s32[8]{0:T(128)S(1)} %stack.76._, bf16[4,96,3072]{2,1,0:T(8,128)(2,1)} %pad_maximum_fusion.a, bf16[4,96,3072]{2,1,0:T(8,128)(2,1)S(1)} %pad_maximum_fusion.1.b), custom_call_target="tpu_custom_call" | custom-call | tf_op jit(solution)/shard_map/put_weights/pallas_call | solution.py:130
  96.2 8.0 %put_weights.3 = bf16[16,96,3072]{2,1,0:T(8,128)(2,1)} custom-call(s32[8]{0:T(128)S(1)} %stack.67._, bf16[4,96,3072]{2,1,0:T(8,128)(2,1)} %collective-permute-done.6.a, bf16[4,96,3072]{2,1,0:T(8,128)(2,1)} %collective-permute-done.9.b, bf16[16,96,3072]{2,1,0:T(8,128)(2,1)} %put_weights.2.rest_0_), custom_call_target="tpu_custom_call", output_to_operand_aliasing={{}: (3, {})} | custom-call | tf_op jit(solution)/shard_map/put_weights/pallas_call | solution.py:130
  104.3 12.4 %forward.1 = (bf16[4,512,384]{2,1,0:T(8,128)(2,1)}, f32[512,1536]{1,0:T(8,128)}, f32[512,1536]{1,0:T(8,128)}, bf16[512,1536]{1,0:T(8,128)(2,1)S(1)}) custom-call(s32[5]{0:T(128)S(1)} %get-tuple-element.50.source, bf16[8,128,1536]{2,1,0:T(8,128)(2,1)} %all-to-all-done.x_hbm.refs_5_, f32[1,1536]{1,0:T(1,128)S(1)} %reshape.79.gain_ref.refs_7_, ...), custom_call_target="tpu_custom_call" | custom-call | tf_op jit(solution)/shard_map/forward/pallas_call | solution.py:188
  121.2 9.7 %depth.1 = (bf16[512,1536]{1,0:T(8,128)(2,1)S(1)}, bf16[16,1536]{1,0:T(8,128)(2,1)S(1)}, bf16[16,1536]{1,0:T(8,128)(2,1)S(1)}) custom-call(s32[8]{0:T(128)S(1)} %add_convert_fusion.10.flags, bf16[512,1536]{1,0:T(8,128)(2,1)S(1)} %get-tuple-element.17.glu, bf16[32,1536]{1,0:T(8,128)(2,1)S(1)} %collective-permute-done.10.low, ...), custom_call_target="tpu_custom_call" | custom-call | tf_op jit(solution)/shard_map/depth/pallas_call | solution.py:563
  130.9 13.1 %gated.1 = (bf16[512,768]{1,0:T(8,128)(2,1)}, bf16[512,768]{1,0:T(8,128)(2,1)}, bf16[512,768]{1,0:T(8,128)(2,1)S(1)}, bf16[512,768]{1,0:T(8,128)(2,1)S(1)}) custom-call(s32[9]{0:T(128)S(1)} %pad_add_fusion.2.flags, bf16[512,1536]{1,0:T(8,128)(2,1)S(1)} %get-tuple-element.18.grad, bf16[16,1536]{1,0:T(8,128)(2,1)S(1)} %get-tuple-element.19.low, ...), custom_call_target="tpu_custom_call" | custom-call | tf_op jit(solution)/shard_map/gated/pallas_call | solution.py:337
  144.1 8.8 %taps.1 = f32[32,1536]{1,0:T(8,128)S(1)} custom-call(s32[8]{0:T(128)S(1)} %add_convert_fusion.10.flags, bf16[512,1536]{1,0:T(8,128)(2,1)S(1)} %get-tuple-element.17.glu, bf16[32,1536]{1,0:T(8,128)(2,1)S(1)} %collective-permute-done.10.low, bf16[32,1536]{1,0:T(8,128)(2,1)S(1)} %collective-permute-done.11.high, bf16[512,1536]{1,0:T(8,128)(2,1)S(1)} %get-tuple-element.18.grad), custom_call_target="tpu_custom_call" | custom-call | tf_op jit(solution)/shard_map/taps/pallas_call | solution.py:579
  152.9 14.5 %back.1 = (bf16[8,128,1536]{2,1,0:T(8,128)(2,1)}, f32[1,1536]{1,0:T(1,128)S(1)}) custom-call(s32[5]{0:T(128)S(1)} %get-tuple-element.51.source, bf16[512,768]{1,0:T(8,128)(2,1)S(1)} %get-tuple-element.23.refs_0_, bf16[512,768]{1,0:T(8,128)(2,1)S(1)} %get-tuple-element.24.refs_1_, bf16[512,768]{1,0:T(8,128)(2,1)} %get-tuple-element.25.refs_2_, ...), custom_call_target="tpu_custom_call" | custom-call | tf_op jit(solution)/shard_map/back/pallas_call | solution.py:422
  169.0 2.5 fusion.32
  172.5 5.0 %all-to-all-start.1 = ((bf16[8,128,1536]{2,1,0:T(8,128)(2,1)}), bf16[8,128,1536]{2,1,0:T(8,128)(2,1)S(1)}, u32[]{:S(2)}, u32[]{:S(2)}) async-start(bf16[8,128,1536]{2,1,0:T(8,128)(2,1)} %get-tuple-element.27), calls=%async_computation.1 | async-start | bytes 6291456 | tf_op jit(solution)/shard_map/all_to_all | solution.py:611
  182.3 3.5 %collective-permute-done.25 = f32[32,1536]{1,0:T(8,128)S(1)} collective-permute-done((f32[32,1536]{1,0:T(8,128)S(1)}, f32[32,1536]{1,0:T(8,128)S(1)}, u32[]{:S(2)}, u32[]{:S(2)}) %collective-permute-start.25) | collective-permute-done | bytes 196640 | tf_op jit(solution)/shard_map/ppermute | solution.py:481
  189.0 2.4 collective-permute-start.28
  207.6 14.9 %collective-permute-done.20 = bf16[2,384,768]{2,1,0:T(8,128)(2,1)S(1)} collective-permute-done((bf16[2,384,768]{2,1,0:T(8,128)(2,1)S(1)}, bf16[2,384,768]{2,1,0:T(8,128)(2,1)S(1)}, u32[]{:S(2)}, u32[]{:S(2)}) %collective-permute-start.20) | collective-permute-done | bytes 1179680 | tf_op jit(solution)/shard_map/ppermute | solution.py:469
  224.2 4.7 %collective-permute-done.16 = bf16[2,384,768]{2,1,0:T(8,128)(2,1)S(1)} collective-permute-done((bf16[2,384,768]{2,1,0:T(8,128)(2,1)S(1)}, bf16[2,384,768]{2,1,0:T(8,128)(2,1)S(1)}, u32[]{:S(2)}, u32[]{:S(2)}) %collective-permute-start.16) | collective-permute-done | bytes 1179680 | tf_op jit(solution)/shard_map/ppermute | solution.py:469
  230.6 22.1 %collective-permute-done.28 = bf16[16,1536]{1,0:T(8,128)(2,1)S(1)} collective-permute-done((bf16[16,1536]{1,0:T(8,128)(2,1)S(1)}, bf16[16,1536]{1,0:T(8,128)(2,1)S(1)}, u32[]{:S(2)}, u32[]{:S(2)}) %collective-permute-start.28) | collective-permute-done | bytes 49184 | tf_op jit(solution)/shard_map/ppermute | solution.py:489
  255.5 7.5 %collective-permute-done.22 = bf16[384,384]{1,0:T(8,128)(2,1)S(1)} collective-permute-done((bf16[384,384]{1,0:T(8,128)(2,1)S(1)}, bf16[384,384]{1,0:T(8,128)(2,1)S(1)}, u32[]{:S(2)}, u32[]{:S(2)}) %collective-permute-start.22) | collective-permute-done | bytes 294944 | tf_op jit(solution)/shard_map/ppermute | solution.py:507
  263.0 5.8 %collective-permute-done.18 = bf16[384,384]{1,0:T(8,128)(2,1)S(1)} collective-permute-done((bf16[384,384]{1,0:T(8,128)(2,1)S(1)}, bf16[384,384]{1,0:T(8,128)(2,1)S(1)}, u32[]{:S(2)}, u32[]{:S(2)}) %collective-permute-start.18) | collective-permute-done | bytes 294944 | tf_op jit(solution)/shard_map/ppermute | solution.py:507
  271.4 13.5 %collective-permute-done.23 = bf16[384,384]{1,0:T(8,128)(2,1)S(1)} collective-permute-done((bf16[384,384]{1,0:T(8,128)(2,1)S(1)}, bf16[384,384]{1,0:T(8,128)(2,1)S(1)}, u32[]{:S(2)}, u32[]{:S(2)}) %collective-permute-start.23) | collective-permute-done | bytes 294944 | tf_op jit(solution)/shard_map/ppermute | solution.py:507
  (135 shorter events, 65.7 us)
Async XLA Ops:
  5.1 99.2 %all-to-all-start = ((bf16[8,128,1536]{2,1,0:T(8,128)(2,1)}), bf16[8,128,1536]{2,1,0:T(8,128)(2,1)}, u32[]{:S(2)}, u32[]{:S(2)}) async-start(bf16[8,128,1536]{2,1,0:T(8,128)(2,1)} %pick_panels.1), calls=%async_computation | async-start | bytes 6291456 | tf_op jit(solution)/shard_map/all_to_all | solution.py:539
  11.7 15.8 %collective-permute-start.7 = (bf16[1,96,3072]{2,1,0:T(8,128)(2,1)S(1)}, bf16[1,96,3072]{2,1,0:T(8,128)(2,1)S(1)}, u32[]{:S(2)}, u32[]{:S(2)}) collective-permute-start(bf16[1,96,3072]{2,1,0:T(8,128)(2,1)S(1)} %get-tuple-element.32), channel_id=1, source_target_pairs={{0,16},{8,24},{16,0},{24,8},{1,17},{9,25},{17,1},{25,9},{2,18},{10... | collective-permute-start | bytes 1769480 | tf_op jit(solution)/shard_map/ppermute | solution.py:88
  13.2 15.9 %collective-permute-start.4 = (bf16[1,96,3072]{2,1,0:T(8,128)(2,1)S(1)}, bf16[1,96,3072]{2,1,0:T(8,128)(2,1)S(1)}, u32[]{:S(2)}, u32[]{:S(2)}) collective-permute-start(bf16[1,96,3072]{2,1,0:T(8,128)(2,1)S(1)} %get-tuple-element.33), channel_id=1, source_target_pairs={{0,8},{8,0},{16,24},{24,16},{1,9},{9,1},{17,25},{25,17},{2,10},{10... | collective-permute-start | bytes 1769480 | tf_op jit(solution)/shard_map/ppermute | solution.py:88
  27.6 27.7 %collective-permute-start.8 = (bf16[2,96,3072]{2,1,0:T(8,128)(2,1)S(1)}, bf16[2,96,3072]{2,1,0:T(8,128)(2,1)S(1)}, u32[]{:S(2)}, u32[]{:S(2)}) collective-permute-start(bf16[2,96,3072]{2,1,0:T(8,128)(2,1)S(1)} %pad_maximum_fusion.3), channel_id=1, source_target_pairs={{0,8},{8,0},{16,24},{24,16},{1,9},{9,1},{17,25},{25,17},{2,10},{10... | collective-permute-start | bytes 3538952 | tf_op jit(solution)/shard_map/ppermute | solution.py:88
  29.3 27.4 %collective-permute-start.5 = (bf16[2,96,3072]{2,1,0:T(8,128)(2,1)S(1)}, bf16[2,96,3072]{2,1,0:T(8,128)(2,1)S(1)}, u32[]{:S(2)}, u32[]{:S(2)}) collective-permute-start(bf16[2,96,3072]{2,1,0:T(8,128)(2,1)S(1)} %pad_maximum_fusion.2), channel_id=1, source_target_pairs={{0,16},{8,24},{16,0},{24,8},{1,17},{9,25},{17,1},{25,9},{2,18},{10... | collective-permute-start | bytes 3538952 | tf_op jit(solution)/shard_map/ppermute | solution.py:88
  30.9 32.3 %collective-permute-start = (s32[1,2,4]{2,1,0:T(2,128)S(1)}, s32[1,2,4]{2,1,0:T(2,128)S(1)}, u32[]{:S(2)}, u32[]{:S(2)}) collective-permute-start(s32[1,2,4]{2,1,0:T(2,128)S(1)} %add_bitcast_fusion), channel_id=1, source_target_pairs={{0,1},{1,0},{2,3},{3,2},{4,5},{5,4},{6,7},{7,6},{8,9},{9,8},{10,11... | collective-permute-start | bytes 104 | tf_op jit(solution)/shard_map/ppermute | solution.py:542
  55.5 40.7 %collective-permute-start.9 = (bf16[4,96,3072]{2,1,0:T(8,128)(2,1)S(1)}, bf16[4,96,3072]{2,1,0:T(8,128)(2,1)}, u32[]{:S(2)}, u32[]{:S(2)}) collective-permute-start(bf16[4,96,3072]{2,1,0:T(8,128)(2,1)S(1)} %pad_maximum_fusion.1.b), channel_id=1, source_target_pairs={{0,1},{1,0},{2,3},{3,2},{4,5},{5,4},{6,7},{7,6},{8,9},{9,8},{10,11... | collective-permute-start | bytes 7077896 | tf_op jit(solution)/shard_map/ppermute | solution.py:104
  58.3 37.9 %collective-permute-start.6 = (bf16[4,96,3072]{2,1,0:T(8,128)(2,1)}, bf16[4,96,3072]{2,1,0:T(8,128)(2,1)}, u32[]{:S(2)}, u32[]{:S(2)}) collective-permute-start(bf16[4,96,3072]{2,1,0:T(8,128)(2,1)} %pad_maximum_fusion.a), channel_id=1, source_target_pairs={{0,1},{1,0},{2,3},{3,2},{4,5},{5,4},{6,7},{7,6},{8,9},{9,8},{10,11... | collective-permute-start | bytes 7077896 | tf_op jit(solution)/shard_map/ppermute | solution.py:103
  59.2 61.4 %collective-permute-start.12 = (bf16[16,1536]{1,0:T(8,128)(2,1)S(1)}, bf16[16,1536]{1,0:T(8,128)(2,1)S(1)}, u32[]{:S(2)}, u32[]{:S(2)}) collective-permute-start(bf16[16,1536]{1,0:T(8,128)(2,1)S(1)} %get-tuple-element.43), channel_id=1, source_target_pairs={{0,1},{1,2},{2,3},{3,4},{4,5},{5,6},{6,7},{8,9},{9,10},{10,11},{11... | collective-permute-start | bytes 147464 | tf_op jit(solution)/shard_map/ppermute | solution.py:518
  61.6 58.9 %collective-permute-start.13 = (bf16[16,1536]{1,0:T(8,128)(2,1)S(1)}, bf16[16,1536]{1,0:T(8,128)(2,1)S(1)}, u32[]{:S(2)}, u32[]{:S(2)}) collective-permute-start(bf16[16,1536]{1,0:T(8,128)(2,1)S(1)} %get-tuple-element.42), channel_id=1, source_target_pairs={{1,0},{2,1},{3,2},{4,3},{5,4},{6,5},{7,6},{9,8},{10,9},{11,10},{12... | collective-permute-start | bytes 147464 | tf_op jit(solution)/shard_map/ppermute | solution.py:519
  68.5 15.2 %collective-permute-start.2 = (s32[2,2,4]{2,1,0:T(2,128)S(1)}, s32[2,2,4]{2,1,0:T(2,128)S(1)}, u32[]{:S(2)}, u32[]{:S(2)}) collective-permute-start(s32[2,2,4]{2,1,0:T(2,128)S(1)} %pad_add_fusion), channel_id=1, source_target_pairs={{0,4},{1,5},{2,6},{3,7},{4,0},{5,1},{6,2},{7,3},{8,12},{9,13},{10,... | collective-permute-start | bytes 200 | tf_op jit(solution)/shard_map/ppermute | solution.py:543
  119.4 72.0 %collective-permute-start.14 = (bf16[4,512,384]{2,1,0:T(8,128)(2,1)}, bf16[4,512,384]{2,1,0:T(8,128)(2,1)}, u32[]{:S(2)}, u32[]{:S(2)}) collective-permute-start(bf16[4,512,384]{2,1,0:T(8,128)(2,1)} %get-tuple-element.28), channel_id=1, source_target_pairs={{0,1},{1,0},{2,3},{3,2},{4,5},{5,4},{6,7},{7,6},{8,9},{9,8},{10,11... | collective-permute-start | bytes 4718600 | tf_op jit(solution)/shard_map/ppermute | solution.py:554
  171.5 21.8 %collective-permute-start.19 = (bf16[512,768]{1,0:T(8,128)(2,1)}, bf16[512,768]{1,0:T(8,128)(2,1)}, u32[]{:S(2)}, u32[]{:S(2)}) collective-permute-start(bf16[512,768]{1,0:T(8,128)(2,1)} %get-tuple-element.25.refs_2_), channel_id=1, source_target_pairs={{0,1},{1,0},{2,3},{3,2},{4,5},{5,4},{6,7},{7,6},{8,9},{9,8},{10,11... | collective-permute-start | bytes 2359304 | tf_op jit(solution)/shard_map/ppermute | solution.py:598
  172.5 23.4 %collective-permute-start.15 = (bf16[512,768]{1,0:T(8,128)(2,1)}, bf16[512,768]{1,0:T(8,128)(2,1)}, u32[]{:S(2)}, u32[]{:S(2)}) collective-permute-start(bf16[512,768]{1,0:T(8,128)(2,1)} %get-tuple-element.26.refs_3_), channel_id=1, source_target_pairs={{0,1},{1,0},{2,3},{3,2},{4,5},{5,4},{6,7},{7,6},{8,9},{9,8},{10,11... | collective-permute-start | bytes 2359304 | tf_op jit(solution)/shard_map/ppermute | solution.py:598
  172.5 113.5 %all-to-all-start.1 = ((bf16[8,128,1536]{2,1,0:T(8,128)(2,1)}), bf16[8,128,1536]{2,1,0:T(8,128)(2,1)S(1)}, u32[]{:S(2)}, u32[]{:S(2)}) async-start(bf16[8,128,1536]{2,1,0:T(8,128)(2,1)} %get-tuple-element.27), calls=%async_computation.1 | async-start | bytes 6291456 | tf_op jit(solution)/shard_map/all_to_all | solution.py:611
  187.3 43.3 %collective-permute-start.27 = (bf16[16,1536]{1,0:T(8,128)(2,1)S(1)}, bf16[16,1536]{1,0:T(8,128)(2,1)S(1)}, u32[]{:S(2)}, u32[]{:S(2)}) collective-permute-start(bf16[16,1536]{1,0:T(8,128)(2,1)S(1)} %fusion.26), channel_id=1, source_target_pairs={{0,2},{1,3},{2,0},{3,1},{4,6},{5,7},{6,4},{7,5},{8,10},{9,11},{10,... | collective-permute-start | bytes 147464 | tf_op jit(solution)/shard_map/ppermute | solution.py:489
  189.0 63.7 %collective-permute-start.28 = (bf16[16,1536]{1,0:T(8,128)(2,1)S(1)}, bf16[16,1536]{1,0:T(8,128)(2,1)S(1)}, u32[]{:S(2)}, u32[]{:S(2)}) collective-permute-start(bf16[16,1536]{1,0:T(8,128)(2,1)S(1)} %fusion.26), channel_id=1, source_target_pairs={{0,4},{1,5},{2,6},{3,7},{4,0},{5,1},{6,2},{7,3},{8,12},{9,13},{10,... | collective-permute-start | bytes 147464 | tf_op jit(solution)/shard_map/ppermute | solution.py:489
  191.4 61.3 %collective-permute-start.29 = (bf16[16,1536]{1,0:T(8,128)(2,1)S(1)}, bf16[16,1536]{1,0:T(8,128)(2,1)S(1)}, u32[]{:S(2)}, u32[]{:S(2)}) collective-permute-start(bf16[16,1536]{1,0:T(8,128)(2,1)S(1)} %fusion.26), channel_id=1, source_target_pairs={{0,6},{1,7},{2,4},{3,5},{4,2},{5,3},{6,0},{7,1},{8,14},{9,15},{10,... | collective-permute-start | bytes 147464 | tf_op jit(solution)/shard_map/ppermute | solution.py:489
  195.2 27.3 %collective-permute-start.20 = (bf16[2,384,768]{2,1,0:T(8,128)(2,1)S(1)}, bf16[2,384,768]{2,1,0:T(8,128)(2,1)S(1)}, u32[]{:S(2)}, u32[]{:S(2)}) collective-permute-start(bf16[2,384,768]{2,1,0:T(8,128)(2,1)S(1)} %add_convert_fusion), channel_id=1, source_target_pairs={{0,8},{8,0},{16,24},{24,16},{1,9},{9,1},{17,25},{25,17},{2,10},{10... | collective-permute-start | bytes 3538952 | tf_op jit(solution)/shard_map/ppermute | solution.py:469
  200.0 28.9 %collective-permute-start.16 = (bf16[2,384,768]{2,1,0:T(8,128)(2,1)S(1)}, bf16[2,384,768]{2,1,0:T(8,128)(2,1)S(1)}, u32[]{:S(2)}, u32[]{:S(2)}) collective-permute-start(bf16[2,384,768]{2,1,0:T(8,128)(2,1)S(1)} %add_convert_fusion.2), channel_id=1, source_target_pairs={{0,16},{8,24},{16,0},{24,8},{1,17},{9,25},{17,1},{25,9},{2,18},{10... | collective-permute-start | bytes 3538952 | tf_op jit(solution)/shard_map/ppermute | solution.py:469
  222.6 30.2 %collective-permute-start.21 = (bf16[1,384,768]{2,1,0:T(8,128)(2,1)S(1)}, bf16[1,384,768]{2,1,0:T(8,128)(2,1)S(1)}, u32[]{:S(2)}, u32[]{:S(2)}) collective-permute-start(bf16[1,384,768]{2,1,0:T(8,128)(2,1)S(1)} %add_convert_fusion.5), channel_id=1, source_target_pairs={{0,16},{8,24},{16,0},{24,8},{1,17},{9,25},{17,1},{25,9},{2,18},{10... | collective-permute-start | bytes 1769480 | tf_op jit(solution)/shard_map/ppermute | solution.py:469
  229.0 25.2 %collective-permute-start.17 = (bf16[1,384,768]{2,1,0:T(8,128)(2,1)S(1)}, bf16[1,384,768]{2,1,0:T(8,128)(2,1)S(1)}, u32[]{:S(2)}, u32[]{:S(2)}) collective-permute-start(bf16[1,384,768]{2,1,0:T(8,128)(2,1)S(1)} %add_convert_fusion.8), channel_id=1, source_target_pairs={{0,8},{8,0},{16,24},{24,16},{1,9},{9,1},{17,25},{25,17},{2,10},{10... | collective-permute-start | bytes 1769480 | tf_op jit(solution)/shard_map/ppermute | solution.py:469
  254.5 14.4 %collective-permute-start.18 = (bf16[384,384]{1,0:T(8,128)(2,1)S(1)}, bf16[384,384]{1,0:T(8,128)(2,1)S(1)}, u32[]{:S(2)}, u32[]{:S(2)}) collective-permute-start(bf16[384,384]{1,0:T(8,128)(2,1)S(1)} %broadcast_select_fusion.2), channel_id=1, source_target_pairs={{0,2},{1,3},{2,0},{3,1},{4,6},{5,7},{6,4},{7,5},{8,10},{9,11},{10,... | collective-permute-start | bytes 884744 | tf_op jit(solution)/shard_map/ppermute | solution.py:507
  269.1 15.8 %collective-permute-start.23 = (bf16[384,384]{1,0:T(8,128)(2,1)S(1)}, bf16[384,384]{1,0:T(8,128)(2,1)S(1)}, u32[]{:S(2)}, u32[]{:S(2)}) collective-permute-start(bf16[384,384]{1,0:T(8,128)(2,1)S(1)} %select_convert_fusion), channel_id=1, source_target_pairs={{0,4},{1,5},{2,6},{3,7},{4,0},{5,1},{6,2},{7,3},{8,12},{9,13},{10,... | collective-permute-start | bytes 884744 | tf_op jit(solution)/shard_map/ppermute | solution.py:507
  (22 other events, 143.4 us)

commit v8 on v6

--- a/solution.py
+++ b/solution.py
@@ -57,7 +57,6 @@
         ),
         out_shape=jax.ShapeDtypeStruct((count, rows, width), source.dtype),
         compiler_params=params(1, 48),
-        name="pick_panels",
     )(index, source)
 
 
@@ -77,7 +76,6 @@
         ),
         out_shape=jax.ShapeDtypeStruct((count, rows, width), source.dtype),
         compiler_params=params(1, 48),
-        name="pick_blocks",
     )(index, source)
 
 
@@ -141,7 +139,6 @@
             out_shape=jax.ShapeDtypeStruct((4 * count, quarter, width), w_in.dtype),
             input_output_aliases={3: 0} if base else {},
             compiler_params=params(2, 48),
-            name="put_weights",
         )(out_index(side), *pair, *base)
 
     full = put(core, (first, second))
@@ -210,7 +207,6 @@
         ),
         out_shape=[parts, wide(F32), wide(F32), wide(BF)],
         compiler_params=params(1, 48),
-        name="forward",
     )(jnp.append(source, lax.axis_index("dp")), arrived, gain.reshape(1, width), full_in, full_in)
 
 
@@ -347,7 +343,6 @@
         ),
         out_shape=[jax.ShapeDtypeStruct((rows, width // parts), BF)] * (2 * parts),
         compiler_params=params(1, 48),
-        name="gated",
     )(jnp.append(flags, core), grad_depth, low, high, lin, gate, kernel)
 
 
@@ -445,7 +440,6 @@
             jax.ShapeDtypeStruct((1, width), F32),
         ],
         compiler_params=params(1, 48),
-        name="back",
     )(jnp.append(source, core), *gradients, full_in, arrived, upstream, gain.reshape(1, width))
 
 
@@ -496,15 +490,13 @@
 
 
 def sum_across(share):
+    count = share.shape[0]
     place = lax.axis_index("tm") // 2
-    for bit in bits_of(share.shape[0]):
-        pairs = share.reshape(share.shape[0] // 2, 2, *share.shape[1:])
-        mine = (place >> bit) & 1
-        send = lax.dynamic_index_in_dim(pairs, 1 - mine, 1, keepdims=False).astype(BF)
-        keep = lax.dynamic_index_in_dim(pairs, mine, 1, keepdims=False)
-        got = lax.ppermute(send, "tm", flip("tm", 2 << bit))
-        share = keep.astype(F32) + got.astype(F32)
-    return share[0]
+    total = lax.dynamic_index_in_dim(share, place, 0, keepdims=False).astype(F32)
+    for turn in range(1, count):
+        piece = lax.dynamic_index_in_dim(share, place ^ turn, 0, keepdims=False)
+        total = total + lax.ppermute(piece, "tm", flip("tm", 2 * turn)).astype(F32)
+    return total
 
 
 def edges(values, width):
@@ -568,7 +560,6 @@
         ),
         out_shape=[jax.ShapeDtypeStruct((h, width), BF) for h in (rows, RIM, RIM)],
         compiler_params=params(1, 48),
-        name="depth",
     )(flags, glu, glu_low, glu_high, up_rows, up_low, up_high, kernel)
     kernel_term = pl.pallas_call(
         functools.partial(taps_body, **sizes),

time: 285 us -> 347 us (1.22)
  waiting for transfers between devices: 106 us -> 178 us
  local copies, waits for them, and re-layouts: 17.8 us -> 13.9 us
    ppermute x3, waiting for transfers between devices: 0.64 us -> 66.3 us  [sum_everywhere(): terms.append(lax.ppermute(values, 'tm', flip('tm', mask)))]
    ppermute x4, waiting for transfers between devices: 25.3 us -> 29 us  [outer_halved(): got = lax.ppermute(send, 'dp', flip_bit('dp', bit))]
    concatenate x4 -> x3, local copies, waits for them, and re-layouts: 8.28 us -> 5.16 us  [local(): share = jnp.concatenate(shares, axis=1)]
    ppermute x2 -> x3, waiting for transfers between devices: 22.6 us -> 23.5 us  [sum_across(): total = total + lax.ppermute(piece, 'tm', flip('tm', 2 * turn)).astype(F32)]
  transfers between devices with their start and end apart: 32 -> 33, of which waited for: 14 -> 18; matrix products, arithmetic and copies ran while one was open for 15% -> 11% of each run, Pallas kernels for 26% -> 8%
where the time goes in v8:
time: 347 us; the launch traced here: 346 us
  waiting for transfers between devices  178 us (51%)
  Pallas kernels  77.1 us (22%)
  starting transfers between devices  50.2 us (14%)
  local copies, waits for them, and re-layouts  13.9 us (4%)
  matrix products  13.5 us (4%)
  other arithmetic  11.9 us (3%)
    ppermute x3, waiting for transfers between devices, sum_everywhere(): terms.append(lax.ppermute(values, 'tm', flip('tm', mask)))  66.3 us
    ppermute x4, waiting for transfers between devices, gather_order(): got = lax.ppermute(have, 'dp', flip_bit('dp', bit))  37.2 us
    ppermute x4, waiting for transfers between devices, outer_halved(): got = lax.ppermute(send, 'dp', flip_bit('dp', bit))  29 us
    ppermute x3, waiting for transfers between devices, sum_across(): total = total + lax.ppermute(piece, 'tm', flip('tm', 2 * turn)).astype(F32)  23.5 us
    ppermute x3, waiting for transfers between devices, local(): lax.ppermute(tags, 'tm', flip('tm', i))  14.5 us
    pallas_call x2, Pallas kernels, put(): pl.pallas_call(body, grid_spec=pltpu.PrefetchScalarGridSpec(num_scalar_pr...  14.3 us
    pallas_call x1, Pallas kernels, back(): pl.pallas_call(functools.partial(back_body, grads=len(gradients), block=b...  14.3 us
    dot_general x8, matrix products, outer_sum(): lax.dot_general(a, b, (((1,), (0,)), ((), ())), preferred_element_type=F32)  13.5 us
  transfers between devices with their start and end apart: 33, of which 18 were waited for; matrix products, arithmetic and copies ran while one was open for 11% of the time, Pallas kernels for 8%

profile of v8, /device:TPU:8, one launch (start us, length us, event | category | flops | bytes accessed | tf_op | source)
XLA Modules:
  0.0 345.9 jit_solution(2673893111570415687)
XLA Ops:
  5.1 5.5 %all-to-all-start = ((bf16[8,128,1536]{2,1,0:T(8,128)(2,1)}), bf16[8,128,1536]{2,1,0:T(8,128)(2,1)}, u32[]{:S(2)}, u32[]{:S(2)}) async-start(bf16[8,128,1536]{2,1,0:T(8,128)(2,1)} %shard_map.102), calls=%async_computation | async-start | bytes 6291456 | tf_op jit(solution)/shard_map/all_to_all | solution.py:525
  13.7 12.3 %collective-permute-done.7 = bf16[1,96,3072]{2,1,0:T(8,128)(2,1)S(1)} collective-permute-done((bf16[1,96,3072]{2,1,0:T(8,128)(2,1)S(1)}, bf16[1,96,3072]{2,1,0:T(8,128)(2,1)S(1)}, u32[]{:S(2)}, u32[]{:S(2)}) %collective-permute-start.7) | collective-permute-done | bytes 589856 | tf_op jit(solution)/shard_map/ppermute | solution.py:86
  29.5 23.8 %collective-permute-done.8 = bf16[2,96,3072]{2,1,0:T(8,128)(2,1)S(1)} collective-permute-done((bf16[2,96,3072]{2,1,0:T(8,128)(2,1)S(1)}, bf16[2,96,3072]{2,1,0:T(8,128)(2,1)S(1)}, u32[]{:S(2)}, u32[]{:S(2)}) %collective-permute-start.8) | collective-permute-done | bytes 1179680 | tf_op jit(solution)/shard_map/ppermute | solution.py:86
  59.7 3.1 collective-permute-start.13
  63.2 3.6 %collective-permute-done.1 = s32[2,2,4]{2,1,0:T(2,128)S(1)} collective-permute-done((s32[2,2,4]{2,1,0:T(2,128)S(1)}, s32[2,2,4]{2,1,0:T(2,128)S(1)}, u32[]{:S(2)}, u32[]{:S(2)}) %collective-permute-start.1) | collective-permute-done | bytes 96 | tf_op jit(solution)/shard_map/ppermute | solution.py:529
  69.3 9.4 %collective-permute-done.2 = s32[2,2,4]{2,1,0:T(2,128)S(1)} collective-permute-done((s32[2,2,4]{2,1,0:T(2,128)S(1)}, s32[2,2,4]{2,1,0:T(2,128)S(1)}, u32[]{:S(2)}, u32[]{:S(2)}) %collective-permute-start.2) | collective-permute-done | bytes 96 | tf_op jit(solution)/shard_map/ppermute | solution.py:529
  83.2 6.3 %shard_map.103.rest_0_ = bf16[16,96,3072]{2,1,0:T(8,128)(2,1)} custom-call(s32[8]{0:T(128)S(1)} %stack.76._, bf16[4,96,3072]{2,1,0:T(8,128)(2,1)} %pad_maximum_fusion.a, bf16[4,96,3072]{2,1,0:T(8,128)(2,1)S(1)} %pad_maximum_fusion.1.b), custom_call_target="tpu_custom_call" | custom-call | tf_op jit(solution)/shard_map/pallas_call | solution.py:128
  89.5 8.0 %shard_map.104 = bf16[16,96,3072]{2,1,0:T(8,128)(2,1)} custom-call(s32[8]{0:T(128)S(1)} %stack.67._, bf16[4,96,3072]{2,1,0:T(8,128)(2,1)} %collective-permute-done.6.a, bf16[4,96,3072]{2,1,0:T(8,128)(2,1)} %collective-permute-done.9.b, bf16[16,96,3072]{2,1,0:T(8,128)(2,1)} %shard_map.103.rest_0_), custom_call_target="tpu_custom_call", output_to_operand_aliasing={{}: (3, {})} | custom-call | tf_op jit(solution)/shard_map/pallas_call | solution.py:128
  97.5 12.5 %shard_map.105 = (bf16[4,512,384]{2,1,0:T(8,128)(2,1)}, f32[512,1536]{1,0:T(8,128)}, f32[512,1536]{1,0:T(8,128)}, bf16[512,1536]{1,0:T(8,128)(2,1)S(1)}) custom-call(s32[5]{0:T(128)S(1)} %get-tuple-element.53.source, bf16[8,128,1536]{2,1,0:T(8,128)(2,1)} %all-to-all-done.x_hbm.refs_5_, f32[1,1536]{1,0:T(1,128)S(1)} %reshape.94.gain_ref.refs_7_, ...), custom_call_target="tpu_custom_call" | custom-call | tf_op jit(solution)/shard_map/pallas_call | solution.py:185
  111.9 5.3 %collective-permute-start.11 = (bf16[32,1536]{1,0:T(8,128)(2,1)S(1)}, bf16[32,1536]{1,0:T(8,128)(2,1)S(1)}, u32[]{:S(2)}, u32[]{:S(2)}) collective-permute-start(bf16[32,1536]{1,0:T(8,128)(2,1)S(1)} %get-tuple-element.44), channel_id=1, source_target_pairs={{1,0},{2,1},{3,2},{4,3},{5,4},{6,5},{7,6},{9,8},{10,9},{11,10},{12... | collective-permute-start | bytes 294920 | tf_op jit(solution)/shard_map/ppermute | solution.py:505
  119.2 9.7 %shard_map.106 = (bf16[512,1536]{1,0:T(8,128)(2,1)S(1)}, bf16[16,1536]{1,0:T(8,128)(2,1)S(1)}, bf16[16,1536]{1,0:T(8,128)(2,1)S(1)}) custom-call(s32[8]{0:T(128)S(1)} %add_convert_fusion.10.flags, bf16[512,1536]{1,0:T(8,128)(2,1)S(1)} %get-tuple-element.17.glu, bf16[32,1536]{1,0:T(8,128)(2,1)S(1)} %collective-permute-done.10.low, ...), custom_call_target="tpu_custom_call" | custom-call | tf_op jit(solution)/shard_map/pallas_call | solution.py:549
  129.0 13.0 %shard_map.107 = (bf16[512,768]{1,0:T(8,128)(2,1)S(1)}, bf16[512,768]{1,0:T(8,128)(2,1)}, bf16[512,768]{1,0:T(8,128)(2,1)S(1)}, bf16[512,768]{1,0:T(8,128)(2,1)S(1)}) custom-call(s32[9]{0:T(128)S(1)} %pad_add_fusion.2.flags, bf16[512,1536]{1,0:T(8,128)(2,1)S(1)} %get-tuple-element.18.grad, bf16[16,1536]{1,0:T(8,128)(2,1)S(1)} %get-tuple-element.19.low, ...), custom_call_target="tpu_custom_call" | custom-call | tf_op jit(solution)/shard_map/pallas_call | solution.py:333
  142.0 8.8 %taps.1 = f32[32,1536]{1,0:T(8,128)S(1)} custom-call(s32[8]{0:T(128)S(1)} %add_convert_fusion.10.flags, bf16[512,1536]{1,0:T(8,128)(2,1)S(1)} %get-tuple-element.17.glu, bf16[32,1536]{1,0:T(8,128)(2,1)S(1)} %collective-permute-done.10.low, bf16[32,1536]{1,0:T(8,128)(2,1)S(1)} %collective-permute-done.11.high, bf16[512,1536]{1,0:T(8,128)(2,1)S(1)} %get-tuple-element.18.grad), custom_call_target="tpu_custom_call" | custom-call | tf_op jit(solution)/shard_map/taps/pallas_call | solution.py:564
  150.8 14.3 %shard_map.108 = (bf16[8,128,1536]{2,1,0:T(8,128)(2,1)}, f32[1,1536]{1,0:T(1,128)S(1)}) custom-call(s32[5]{0:T(128)S(1)} %get-tuple-element.54.source, bf16[512,768]{1,0:T(8,128)(2,1)S(1)} %get-tuple-element.23.refs_0_, bf16[512,768]{1,0:T(8,128)(2,1)S(1)} %get-tuple-element.24.refs_1_, bf16[512,768]{1,0:T(8,128)(2,1)S(1)} %get-tuple-element.25.refs_2_, ...), custom_call_target="tpu_custom_call" | custom-call | tf_op jit(solution)/shard_map/pallas_call | solution.py:417
  167.1 5.6 %collective-permute-done.24 = f32[32,1536]{1,0:T(8,128)S(1)} collective-permute-done((f32[32,1536]{1,0:T(8,128)S(1)}, f32[32,1536]{1,0:T(8,128)S(1)}, u32[]{:S(2)}, u32[]{:S(2)}) %collective-permute-start.24) | collective-permute-done | bytes 196640 | tf_op jit(solution)/shard_map/ppermute | solution.py:475
  177.3 4.7 %all-to-all-start.1 = ((bf16[8,128,1536]{2,1,0:T(8,128)(2,1)}), bf16[8,128,1536]{2,1,0:T(8,128)(2,1)S(1)}, u32[]{:S(2)}, u32[]{:S(2)}) async-start(bf16[8,128,1536]{2,1,0:T(8,128)(2,1)} %get-tuple-element.27), calls=%async_computation.1 | async-start | bytes 6291456 | tf_op jit(solution)/shard_map/all_to_all | solution.py:596
  189.9 45.5 %collective-permute-done.27 = bf16[16,1536]{1,0:T(8,128)(2,1)S(1)} collective-permute-done((bf16[16,1536]{1,0:T(8,128)(2,1)S(1)}, bf16[16,1536]{1,0:T(8,128)(2,1)S(1)}, u32[]{:S(2)}, u32[]{:S(2)}) %collective-permute-start.27) | collective-permute-done | bytes 49184 | tf_op jit(solution)/shard_map/ppermute | solution.py:483
  235.5 17.7 %collective-permute-done.28 = bf16[16,1536]{1,0:T(8,128)(2,1)S(1)} collective-permute-done((bf16[16,1536]{1,0:T(8,128)(2,1)S(1)}, bf16[16,1536]{1,0:T(8,128)(2,1)S(1)}, u32[]{:S(2)}, u32[]{:S(2)}) %collective-permute-start.28) | collective-permute-done | bytes 49184 | tf_op jit(solution)/shard_map/ppermute | solution.py:483
  253.1 3.1 collective-permute-done.29
  270.5 18.4 %collective-permute-done.19 = bf16[2,384,768]{2,1,0:T(8,128)(2,1)S(1)} collective-permute-done((bf16[2,384,768]{2,1,0:T(8,128)(2,1)S(1)}, bf16[2,384,768]{2,1,0:T(8,128)(2,1)S(1)}, u32[]{:S(2)}, u32[]{:S(2)}) %collective-permute-start.19) | collective-permute-done | bytes 1179680 | tf_op jit(solution)/shard_map/ppermute | solution.py:463
  295.1 9.2 %collective-permute-done.20 = bf16[1,384,768]{2,1,0:T(8,128)(2,1)S(1)} collective-permute-done((bf16[1,384,768]{2,1,0:T(8,128)(2,1)S(1)}, bf16[1,384,768]{2,1,0:T(8,128)(2,1)S(1)}, u32[]{:S(2)}, u32[]{:S(2)}) %collective-permute-start.20) | collective-permute-done | bytes 589856 | tf_op jit(solution)/shard_map/ppermute | solution.py:463
  319.2 6.5 %collective-permute-done.21 = bf16[384,384]{1,0:T(8,128)(2,1)S(1)} collective-permute-done((bf16[384,384]{1,0:T(8,128)(2,1)S(1)}, bf16[384,384]{1,0:T(8,128)(2,1)S(1)}, u32[]{:S(2)}, u32[]{:S(2)}) %collective-permute-start.21) | collective-permute-done | bytes 294944 | tf_op jit(solution)/shard_map/ppermute | solution.py:498
  325.7 10.7 %collective-permute-done.22 = bf16[384,384]{1,0:T(8,128)(2,1)S(1)} collective-permute-done((bf16[384,384]{1,0:T(8,128)(2,1)S(1)}, bf16[384,384]{1,0:T(8,128)(2,1)S(1)}, u32[]{:S(2)}, u32[]{:S(2)}) %collective-permute-start.22) | collective-permute-done | bytes 294944 | tf_op jit(solution)/shard_map/ppermute | solution.py:498
  336.4 6.3 %collective-permute-done.23 = bf16[384,384]{1,0:T(8,128)(2,1)S(1)} collective-permute-done((bf16[384,384]{1,0:T(8,128)(2,1)S(1)}, bf16[384,384]{1,0:T(8,128)(2,1)S(1)}, u32[]{:S(2)}, u32[]{:S(2)}) %collective-permute-start.23) | collective-permute-done | bytes 294944 | tf_op jit(solution)/shard_map/ppermute | solution.py:498
  (145 shorter events, 81.4 us)
Async XLA Ops:
  5.1 92.4 %all-to-all-start = ((bf16[8,128,1536]{2,1,0:T(8,128)(2,1)}), bf16[8,128,1536]{2,1,0:T(8,128)(2,1)}, u32[]{:S(2)}, u32[]{:S(2)}) async-start(bf16[8,128,1536]{2,1,0:T(8,128)(2,1)} %shard_map.102), calls=%async_computation | async-start | bytes 6291456 | tf_op jit(solution)/shard_map/all_to_all | solution.py:525
  10.6 15.4 %collective-permute-start.7 = (bf16[1,96,3072]{2,1,0:T(8,128)(2,1)S(1)}, bf16[1,96,3072]{2,1,0:T(8,128)(2,1)S(1)}, u32[]{:S(2)}, u32[]{:S(2)}) collective-permute-start(bf16[1,96,3072]{2,1,0:T(8,128)(2,1)S(1)} %get-tuple-element.32), channel_id=1, source_target_pairs={{0,16},{8,24},{16,0},{24,8},{1,17},{9,25},{17,1},{25,9},{2,18},{10... | collective-permute-start | bytes 1769480 | tf_op jit(solution)/shard_map/ppermute | solution.py:86
  12.2 15.5 %collective-permute-start.4 = (bf16[1,96,3072]{2,1,0:T(8,128)(2,1)S(1)}, bf16[1,96,3072]{2,1,0:T(8,128)(2,1)S(1)}, u32[]{:S(2)}, u32[]{:S(2)}) collective-permute-start(bf16[1,96,3072]{2,1,0:T(8,128)(2,1)S(1)} %get-tuple-element.33), channel_id=1, source_target_pairs={{0,8},{8,0},{16,24},{24,16},{1,9},{9,1},{17,25},{25,17},{2,10},{10... | collective-permute-start | bytes 1769480 | tf_op jit(solution)/shard_map/ppermute | solution.py:86
  26.2 27.2 %collective-permute-start.8 = (bf16[2,96,3072]{2,1,0:T(8,128)(2,1)S(1)}, bf16[2,96,3072]{2,1,0:T(8,128)(2,1)S(1)}, u32[]{:S(2)}, u32[]{:S(2)}) collective-permute-start(bf16[2,96,3072]{2,1,0:T(8,128)(2,1)S(1)} %pad_maximum_fusion.3), channel_id=1, source_target_pairs={{0,8},{8,0},{16,24},{24,16},{1,9},{9,1},{17,25},{25,17},{2,10},{10... | collective-permute-start | bytes 3538952 | tf_op jit(solution)/shard_map/ppermute | solution.py:86
  27.8 26.9 %collective-permute-start.5 = (bf16[2,96,3072]{2,1,0:T(8,128)(2,1)S(1)}, bf16[2,96,3072]{2,1,0:T(8,128)(2,1)S(1)}, u32[]{:S(2)}, u32[]{:S(2)}) collective-permute-start(bf16[2,96,3072]{2,1,0:T(8,128)(2,1)S(1)} %pad_maximum_fusion.2), channel_id=1, source_target_pairs={{0,16},{8,24},{16,0},{24,8},{1,17},{9,25},{17,1},{25,9},{2,18},{10... | collective-permute-start | bytes 3538952 | tf_op jit(solution)/shard_map/ppermute | solution.py:86
  29.4 33.7 %collective-permute-start = (s32[1,2,4]{2,1,0:T(2,128)S(1)}, s32[1,2,4]{2,1,0:T(2,128)S(1)}, u32[]{:S(2)}, u32[]{:S(2)}) collective-permute-start(s32[1,2,4]{2,1,0:T(2,128)S(1)} %add_bitcast_fusion), channel_id=1, source_target_pairs={{0,1},{1,0},{2,3},{3,2},{4,5},{5,4},{6,7},{7,6},{8,9},{9,8},{10,11... | collective-permute-start | bytes 104 | tf_op jit(solution)/shard_map/ppermute | solution.py:528
  53.6 35.8 %collective-permute-start.9 = (bf16[4,96,3072]{2,1,0:T(8,128)(2,1)S(1)}, bf16[4,96,3072]{2,1,0:T(8,128)(2,1)}, u32[]{:S(2)}, u32[]{:S(2)}) collective-permute-start(bf16[4,96,3072]{2,1,0:T(8,128)(2,1)S(1)} %pad_maximum_fusion.1.b), channel_id=1, source_target_pairs={{0,1},{1,0},{2,3},{3,2},{4,5},{5,4},{6,7},{7,6},{8,9},{9,8},{10,11... | collective-permute-start | bytes 7077896 | tf_op jit(solution)/shard_map/ppermute | solution.py:102
  56.4 33.0 %collective-permute-start.6 = (bf16[4,96,3072]{2,1,0:T(8,128)(2,1)}, bf16[4,96,3072]{2,1,0:T(8,128)(2,1)}, u32[]{:S(2)}, u32[]{:S(2)}) collective-permute-start(bf16[4,96,3072]{2,1,0:T(8,128)(2,1)} %pad_maximum_fusion.a), channel_id=1, source_target_pairs={{0,1},{1,0},{2,3},{3,2},{4,5},{5,4},{6,7},{7,6},{8,9},{9,8},{10,11... | collective-permute-start | bytes 7077896 | tf_op jit(solution)/shard_map/ppermute | solution.py:101
  57.3 60.0 %collective-permute-start.12 = (bf16[16,1536]{1,0:T(8,128)(2,1)S(1)}, bf16[16,1536]{1,0:T(8,128)(2,1)S(1)}, u32[]{:S(2)}, u32[]{:S(2)}) collective-permute-start(bf16[16,1536]{1,0:T(8,128)(2,1)S(1)} %get-tuple-element.43), channel_id=1, source_target_pairs={{0,1},{1,2},{2,3},{3,4},{4,5},{5,6},{6,7},{8,9},{9,10},{10,11},{11... | collective-permute-start | bytes 147464 | tf_op jit(solution)/shard_map/ppermute | solution.py:504
  59.7 57.6 %collective-permute-start.13 = (bf16[16,1536]{1,0:T(8,128)(2,1)S(1)}, bf16[16,1536]{1,0:T(8,128)(2,1)S(1)}, u32[]{:S(2)}, u32[]{:S(2)}) collective-permute-start(bf16[16,1536]{1,0:T(8,128)(2,1)S(1)} %get-tuple-element.42), channel_id=1, source_target_pairs={{1,0},{2,1},{3,2},{4,3},{5,4},{6,5},{7,6},{9,8},{10,9},{11,10},{12... | collective-permute-start | bytes 147464 | tf_op jit(solution)/shard_map/ppermute | solution.py:505
  166.7 89.6 %collective-permute-start.14 = (bf16[4,512,384]{2,1,0:T(8,128)(2,1)}, bf16[4,512,384]{2,1,0:T(8,128)(2,1)}, u32[]{:S(2)}, u32[]{:S(2)}) collective-permute-start(bf16[4,512,384]{2,1,0:T(8,128)(2,1)} %get-tuple-element.28), channel_id=1, source_target_pairs={{0,1},{1,0},{2,3},{3,2},{4,5},{5,4},{6,7},{7,6},{8,9},{9,8},{10,11... | collective-permute-start | bytes 4718600 | tf_op jit(solution)/shard_map/ppermute | solution.py:540
  177.3 79.0 %collective-permute-start.18 = (bf16[512,768]{1,0:T(8,128)(2,1)}, bf16[512,768]{1,0:T(8,128)(2,1)}, u32[]{:S(2)}, u32[]{:S(2)}) collective-permute-start(bf16[512,768]{1,0:T(8,128)(2,1)} %get-tuple-element.26.refs_3_), channel_id=1, source_target_pairs={{0,1},{1,0},{2,3},{3,2},{4,5},{5,4},{6,7},{7,6},{8,9},{9,8},{10,11... | collective-permute-start | bytes 2359304 | tf_op jit(solution)/shard_map/ppermute | solution.py:583
  177.3 166.4 %all-to-all-start.1 = ((bf16[8,128,1536]{2,1,0:T(8,128)(2,1)}), bf16[8,128,1536]{2,1,0:T(8,128)(2,1)S(1)}, u32[]{:S(2)}, u32[]{:S(2)}) async-start(bf16[8,128,1536]{2,1,0:T(8,128)(2,1)} %get-tuple-element.27), calls=%async_computation.1 | async-start | bytes 6291456 | tf_op jit(solution)/shard_map/all_to_all | solution.py:596
  185.5 49.9 %collective-permute-start.27 = (bf16[16,1536]{1,0:T(8,128)(2,1)S(1)}, bf16[16,1536]{1,0:T(8,128)(2,1)S(1)}, u32[]{:S(2)}, u32[]{:S(2)}) collective-permute-start(bf16[16,1536]{1,0:T(8,128)(2,1)S(1)} %fusion.26), channel_id=1, source_target_pairs={{0,2},{1,3},{2,0},{3,1},{4,6},{5,7},{6,4},{7,5},{8,10},{9,11},{10,... | collective-permute-start | bytes 147464 | tf_op jit(solution)/shard_map/ppermute | solution.py:483
  186.1 67.1 %collective-permute-start.28 = (bf16[16,1536]{1,0:T(8,128)(2,1)S(1)}, bf16[16,1536]{1,0:T(8,128)(2,1)S(1)}, u32[]{:S(2)}, u32[]{:S(2)}) collective-permute-start(bf16[16,1536]{1,0:T(8,128)(2,1)S(1)} %fusion.26), channel_id=1, source_target_pairs={{0,4},{1,5},{2,6},{3,7},{4,0},{5,1},{6,2},{7,3},{8,12},{9,13},{10,... | collective-permute-start | bytes 147464 | tf_op jit(solution)/shard_map/ppermute | solution.py:483
  188.5 67.7 %collective-permute-start.29 = (bf16[16,1536]{1,0:T(8,128)(2,1)S(1)}, bf16[16,1536]{1,0:T(8,128)(2,1)S(1)}, u32[]{:S(2)}, u32[]{:S(2)}) collective-permute-start(bf16[16,1536]{1,0:T(8,128)(2,1)S(1)} %fusion.26), channel_id=1, source_target_pairs={{0,6},{1,7},{2,4},{3,5},{4,2},{5,3},{6,0},{7,1},{8,14},{9,15},{10,... | collective-permute-start | bytes 147464 | tf_op jit(solution)/shard_map/ppermute | solution.py:483
  235.4 27.3 %collective-permute-start.15 = (bf16[512,768]{1,0:T(8,128)(2,1)S(1)}, bf16[512,768]{1,0:T(8,128)(2,1)S(1)}, u32[]{:S(2)}, u32[]{:S(2)}) collective-permute-start(bf16[512,768]{1,0:T(8,128)(2,1)S(1)} %copy-done.7), channel_id=1, source_target_pairs={{0,1},{1,0},{2,3},{3,2},{4,5},{5,4},{6,7},{7,6},{8,9},{9,8},{10,11... | collective-permute-start | bytes 2359304 | tf_op jit(solution)/shard_map/ppermute | solution.py:583
  256.2 38.9 %collective-permute-start.30 = (f32[16,1536]{1,0:T(8,128)S(1)}, f32[16,1536]{1,0:T(8,128)S(1)}, u32[]{:S(2)}, u32[]{:S(2)}) collective-permute-start(f32[16,1536]{1,0:T(8,128)S(1)} %add_add_fusion), channel_id=1, source_target_pairs={{0,1},{1,0},{2,3},{3,2},{4,5},{5,4},{6,7},{7,6},{8,9},{9,8},{10,11... | collective-permute-start | bytes 294920 | tf_op jit(solution)/shard_map/ppermute | solution.py:488
  260.5 28.4 %collective-permute-start.19 = (bf16[2,384,768]{2,1,0:T(8,128)(2,1)S(1)}, bf16[2,384,768]{2,1,0:T(8,128)(2,1)S(1)}, u32[]{:S(2)}, u32[]{:S(2)}) collective-permute-start(bf16[2,384,768]{2,1,0:T(8,128)(2,1)S(1)} %add_convert_fusion), channel_id=1, source_target_pairs={{0,16},{8,24},{16,0},{24,8},{1,17},{9,25},{17,1},{25,9},{2,18},{10... | collective-permute-start | bytes 3538952 | tf_op jit(solution)/shard_map/ppermute | solution.py:463
  263.6 28.5 %collective-permute-start.16 = (bf16[2,384,768]{2,1,0:T(8,128)(2,1)S(1)}, bf16[2,384,768]{2,1,0:T(8,128)(2,1)S(1)}, u32[]{:S(2)}, u32[]{:S(2)}) collective-permute-start(bf16[2,384,768]{2,1,0:T(8,128)(2,1)S(1)} %add_convert_fusion.2), channel_id=1, source_target_pairs={{0,8},{8,0},{16,24},{24,16},{1,9},{9,1},{17,25},{25,17},{2,10},{10... | collective-permute-start | bytes 3538952 | tf_op jit(solution)/shard_map/ppermute | solution.py:463
  289.0 15.3 %collective-permute-start.20 = (bf16[1,384,768]{2,1,0:T(8,128)(2,1)S(1)}, bf16[1,384,768]{2,1,0:T(8,128)(2,1)S(1)}, u32[]{:S(2)}, u32[]{:S(2)}) collective-permute-start(bf16[1,384,768]{2,1,0:T(8,128)(2,1)S(1)} %add_convert_fusion.5), channel_id=1, source_target_pairs={{0,8},{8,0},{16,24},{24,16},{1,9},{9,1},{17,25},{25,17},{2,10},{10... | collective-permute-start | bytes 1769480 | tf_op jit(solution)/shard_map/ppermute | solution.py:463
  293.2 14.6 %collective-permute-start.17 = (bf16[1,384,768]{2,1,0:T(8,128)(2,1)}, bf16[1,384,768]{2,1,0:T(8,128)(2,1)}, u32[]{:S(2)}, u32[]{:S(2)}) collective-permute-start(bf16[1,384,768]{2,1,0:T(8,128)(2,1)} %add_convert_fusion.8), channel_id=1, source_target_pairs={{0,16},{8,24},{16,0},{24,8},{1,17},{9,25},{17,1},{25,9},{2,18},{10... | collective-permute-start | bytes 1769480 | tf_op jit(solution)/shard_map/ppermute | solution.py:463
  315.3 21.0 %collective-permute-start.22 = (bf16[384,384]{1,0:T(8,128)(2,1)S(1)}, bf16[384,384]{1,0:T(8,128)(2,1)S(1)}, u32[]{:S(2)}, u32[]{:S(2)}) collective-permute-start(bf16[384,384]{1,0:T(8,128)(2,1)S(1)} %get-tuple-element.48), channel_id=1, source_target_pairs={{0,4},{1,5},{2,6},{3,7},{4,0},{5,1},{6,2},{7,3},{8,12},{9,13},{10,... | collective-permute-start | bytes 884744 | tf_op jit(solution)/shard_map/ppermute | solution.py:498
  316.3 26.4 %collective-permute-start.23 = (bf16[384,384]{1,0:T(8,128)(2,1)S(1)}, bf16[384,384]{1,0:T(8,128)(2,1)S(1)}, u32[]{:S(2)}, u32[]{:S(2)}) collective-permute-start(bf16[384,384]{1,0:T(8,128)(2,1)S(1)} %get-tuple-element.47), channel_id=1, source_target_pairs={{0,6},{1,7},{2,4},{3,5},{4,2},{5,3},{6,0},{7,1},{8,14},{9,15},{10,... | collective-permute-start | bytes 884744 | tf_op jit(solution)/shard_map/ppermute | solution.py:498
  (26 other events, 245.7 us)
